TPU v7x, 32 devices: a whole 2x2x4 slice. The times are simulated.
32 devices in a mesh: tm: 32 (over z, y, x, core).
Axes of the slice: x: 2, y: 2, z: 4, core: 2. Of those that a mesh axis runs over, the one named last changes fastest.
Arguments:
- samples: float32 [32, 2, 256, 256], P('tm'), may hold values from -0.5 to 0.5
Outputs:
- propagators: float32 [32, 2, 256, 256], P('tm')
All inputs are finite; a program needn't handle non-finite values.
Results may differ from a plain program's by a relative error of at most 0.0003.
Values sent between devices are 32-bit elements; how exact they have to be, the bound alone decides.
No kernel may reach another device: no remote copies, remote signals or barrier semaphores. Data moves between devices by JAX's collectives and lax.ppermute only.
A program may use at most 64 MiB of HBM per device.

v0:
```python
import jax
import jax.numpy as jnp
from jax import lax
from jax.sharding import PartitionSpec as P

time_step = 0.25


def shifted(x, axis, by):
    size = lax.axis_size(axis)
    return lax.ppermute(x, axis, [(i, (i + by) % size) for i in range(size)])


def from_behind(x, axis, by):
    size = lax.axis_size(axis)
    pairs = [(i, i + by) for i in range(size) if 0 <= i + by < size]
    return lax.ppermute(x, axis, pairs)


def complex_product(left, right):
    size = left.shape[-1]
    joined = jnp.concatenate([right[0], right[1]], axis=1)
    real_rows = jnp.dot(
        left[0], joined, preferred_element_type=jnp.float32, precision=lax.Precision.HIGHEST
    )
    imag_rows = jnp.dot(
        left[1], joined, preferred_element_type=jnp.float32, precision=lax.Precision.HIGHEST
    )
    real_part = real_rows[:, :size] - imag_rows[:, size:]
    imag_part = real_rows[:, size:] + imag_rows[:, :size]
    return jnp.stack([real_part, imag_part])


def hermitian(drawn):
    return jnp.stack([(drawn[0] + drawn[0].T) * 0.5, (drawn[1] - drawn[1].T) * 0.5])


def unit_matrix(size):
    return jnp.stack([jnp.eye(size, dtype=jnp.float32), jnp.zeros((size, size), jnp.float32)])


def magnus_factor(first, second):
    size = first.shape[-1]
    summed = first + second
    product = complex_product(second, first)
    comm_real = product[0] - product[0].T
    comm_imag = product[1] + product[1].T
    shrink = time_step * time_step / 12.0
    omega = jnp.stack(
        [
            0.5 * time_step * summed[1] - shrink * comm_real,
            -0.5 * time_step * summed[0] - shrink * comm_imag,
        ]
    )
    identity = unit_matrix(size)
    nested = identity + omega / 4.0
    nested = identity + complex_product(omega, nested) / 3.0
    nested = identity + complex_product(omega, nested) / 2.0
    return identity + complex_product(omega, nested)


def on_device(samples):
    current = hermitian(samples[0])
    following = shifted(current, "tm", -1)
    factor = magnus_factor(current, following)
    cumulative = factor
    position = lax.axis_index("tm")
    devices = lax.axis_size("tm")
    stride = 1
    while stride < devices:
        received = from_behind(cumulative, "tm", stride)
        cumulative = jnp.where(
            position >= stride, complex_product(cumulative, received), cumulative
        )
        stride = stride * 2
    return cumulative[None]


def solution(mesh):
    in_specs = (P("tm", None, None, None),)
    out_specs = P("tm", None, None, None)
    return jax.shard_map(
        on_device, mesh=mesh, in_specs=in_specs, out_specs=out_specs, check_vma=False
    )
```

profile of v0, /device:TPU:27, one launch (start us, length us, event | category | flops | bytes accessed | tf_op | source)
XLA Modules:
  0.0 107.2 jit_solution(3271876734787624260)
XLA Ops:
  0.0 1.1 fusion.63
  1.4 0.8 copy-done
  2.2 0.7 collective-permute-start
  3.0 8.8 %collective-permute-done = f32[2,256,256]{2,1,0:T(8,128)S(1)} collective-permute-done((f32[2,256,256]{2,1,0:T(8,128)S(1)}, f32[2,256,256]{2,1,0:T(8,128)S(1)}, u32[]{:S(2)}, u32[]{:S(2)}) %collective-permute-start) | collective-permute-done | bytes 524320 | tf_op jit(solution)/shard_map/ppermute | solution.py:11
  12.4 0.6 fusion.18
  14.0 0.6 fusion.15
  14.6 0.6 fusion.16
  15.4 0.6 fusion.13
  16.0 0.6 fusion.14
  16.8 0.6 fusion.11
  17.4 0.6 fusion.12
  18.2 1.9 %collective-permute-start.1 = (f32[2,256,256]{2,1,0:T(8,128)S(1)}, f32[2,256,256]{2,1,0:T(8,128)S(1)}, u32[]{:S(2)}, u32[]{:S(2)}) collective-permute-start(f32[2,256,256]{2,1,0:T(8,128)S(1)} %convert_add_fusion), channel_id=1, source_target_pairs={{0,1},{1,2},{2,3},{3,4},{4,5},{5,6},{6,7},{7,8},{8,9},{9,10},{10,1... | collective-permute-start | bytes 1572872 | tf_op jit(solution)/shard_map/ppermute | solution.py:17
  20.1 6.1 %collective-permute-done.1 = f32[2,256,256]{2,1,0:T(8,128)S(1)} collective-permute-done((f32[2,256,256]{2,1,0:T(8,128)S(1)}, f32[2,256,256]{2,1,0:T(8,128)S(1)}, u32[]{:S(2)}, u32[]{:S(2)}) %collective-permute-start.1) | collective-permute-done | bytes 524320 | tf_op jit(solution)/shard_map/ppermute | solution.py:17
  26.3 0.6 fusion.9
  26.9 0.6 fusion.10
  27.7 2.3 %collective-permute-start.2 = (f32[2,256,256]{2,1,0:T(8,128)S(1)}, f32[2,256,256]{2,1,0:T(8,128)S(1)}, u32[]{:S(2)}, u32[]{:S(2)}) collective-permute-start(f32[2,256,256]{2,1,0:T(8,128)S(1)} %maximum_select_fusion), channel_id=1, source_target_pairs={{0,2},{1,3},{2,4},{3,5},{4,6},{5,7},{6,8},{7,9},{8,10},{9,11},{10,... | collective-permute-start | bytes 1572872 | tf_op jit(solution)/shard_map/ppermute | solution.py:17
  29.9 10.5 %collective-permute-done.2 = f32[2,256,256]{2,1,0:T(8,128)S(1)} collective-permute-done((f32[2,256,256]{2,1,0:T(8,128)S(1)}, f32[2,256,256]{2,1,0:T(8,128)S(1)}, u32[]{:S(2)}, u32[]{:S(2)}) %collective-permute-start.2) | collective-permute-done | bytes 524320 | tf_op jit(solution)/shard_map/ppermute | solution.py:17
  40.5 0.6 fusion.7
  41.1 0.6 fusion.8
  41.9 1.9 %collective-permute-start.3 = (f32[2,256,256]{2,1,0:T(8,128)S(1)}, f32[2,256,256]{2,1,0:T(8,128)S(1)}, u32[]{:S(2)}, u32[]{:S(2)}) collective-permute-start(f32[2,256,256]{2,1,0:T(8,128)S(1)} %maximum_select_fusion.1), channel_id=1, source_target_pairs={{0,4},{1,5},{2,6},{3,7},{4,8},{5,9},{6,10},{7,11},{8,12},{9,13},{1... | collective-permute-start | bytes 1572872 | tf_op jit(solution)/shard_map/ppermute | solution.py:17
  43.8 15.6 %collective-permute-done.3 = f32[2,256,256]{2,1,0:T(8,128)S(1)} collective-permute-done((f32[2,256,256]{2,1,0:T(8,128)S(1)}, f32[2,256,256]{2,1,0:T(8,128)S(1)}, u32[]{:S(2)}, u32[]{:S(2)}) %collective-permute-start.3) | collective-permute-done | bytes 524320 | tf_op jit(solution)/shard_map/ppermute | solution.py:17
  60.1 0.6 fusion.6
  61.0 1.3 %collective-permute-start.4 = (f32[2,256,256]{2,1,0:T(8,128)S(1)}, f32[2,256,256]{2,1,0:T(8,128)S(1)}, u32[]{:S(2)}, u32[]{:S(2)}) collective-permute-start(f32[2,256,256]{2,1,0:T(8,128)S(1)} %maximum_select_fusion.2), channel_id=1, source_target_pairs={{0,8},{1,9},{2,10},{3,11},{4,12},{5,13},{6,14},{7,15},{8,16},{9,17... | collective-permute-start | bytes 1572872 | tf_op jit(solution)/shard_map/ppermute | solution.py:17
  62.3 12.1 %collective-permute-done.4 = f32[2,256,256]{2,1,0:T(8,128)S(1)} collective-permute-done((f32[2,256,256]{2,1,0:T(8,128)S(1)}, f32[2,256,256]{2,1,0:T(8,128)S(1)}, u32[]{:S(2)}, u32[]{:S(2)}) %collective-permute-start.4) | collective-permute-done | bytes 524320 | tf_op jit(solution)/shard_map/ppermute | solution.py:17
  74.4 0.6 fusion.3
  75.0 0.6 fusion.4
  75.9 1.3 %collective-permute-start.5 = (f32[2,256,256]{2,1,0:T(8,128)S(1)}, f32[2,256,256]{2,1,0:T(8,128)}, u32[]{:S(2)}, u32[]{:S(2)}) collective-permute-start(f32[2,256,256]{2,1,0:T(8,128)S(1)} %maximum_select_fusion.3), channel_id=1, source_target_pairs={{0,16},{1,17},{2,18},{3,19},{4,20},{5,21},{6,22},{7,23},{8,24},{9,... | collective-permute-start | bytes 1572872 | tf_op jit(solution)/shard_map/ppermute | solution.py:17
  77.2 26.6 %collective-permute-done.5 = f32[2,256,256]{2,1,0:T(8,128)} collective-permute-done((f32[2,256,256]{2,1,0:T(8,128)S(1)}, f32[2,256,256]{2,1,0:T(8,128)}, u32[]{:S(2)}, u32[]{:S(2)}) %collective-permute-start.5) | collective-permute-done | bytes 524320 | tf_op jit(solution)/shard_map/ppermute | solution.py:17
  103.8 1.1 slice_bitcast_fusion.3
  104.8 0.6 fusion.1
  105.5 0.6 fusion.2
  106.2 1.0 fusion
  (39 shorter events, 3.9 us)
Async XLA Ops:
  1.1 1.0 copy-start
  2.2 9.6 %collective-permute-start = (f32[2,256,256]{2,1,0:T(8,128)S(1)}, f32[2,256,256]{2,1,0:T(8,128)S(1)}, u32[]{:S(2)}, u32[]{:S(2)}) collective-permute-start(f32[2,256,256]{2,1,0:T(8,128)S(1)} %pad_maximum_fusion), channel_id=1, source_target_pairs={{0,31},{1,0},{2,1},{3,2},{4,3},{5,4},{6,5},{7,6},{8,7},{9,8},{10,9... | collective-permute-start | bytes 1572872 | tf_op jit(solution)/shard_map/ppermute | solution.py:11
  18.2 8.0 %collective-permute-start.1 = (f32[2,256,256]{2,1,0:T(8,128)S(1)}, f32[2,256,256]{2,1,0:T(8,128)S(1)}, u32[]{:S(2)}, u32[]{:S(2)}) collective-permute-start(f32[2,256,256]{2,1,0:T(8,128)S(1)} %convert_add_fusion), channel_id=1, source_target_pairs={{0,1},{1,2},{2,3},{3,4},{4,5},{5,6},{6,7},{7,8},{8,9},{9,10},{10,1... | collective-permute-start | bytes 1572872 | tf_op jit(solution)/shard_map/ppermute | solution.py:17
  27.7 12.8 %collective-permute-start.2 = (f32[2,256,256]{2,1,0:T(8,128)S(1)}, f32[2,256,256]{2,1,0:T(8,128)S(1)}, u32[]{:S(2)}, u32[]{:S(2)}) collective-permute-start(f32[2,256,256]{2,1,0:T(8,128)S(1)} %maximum_select_fusion), channel_id=1, source_target_pairs={{0,2},{1,3},{2,4},{3,5},{4,6},{5,7},{6,8},{7,9},{8,10},{9,11},{10,... | collective-permute-start | bytes 1572872 | tf_op jit(solution)/shard_map/ppermute | solution.py:17
  41.9 17.5 %collective-permute-start.3 = (f32[2,256,256]{2,1,0:T(8,128)S(1)}, f32[2,256,256]{2,1,0:T(8,128)S(1)}, u32[]{:S(2)}, u32[]{:S(2)}) collective-permute-start(f32[2,256,256]{2,1,0:T(8,128)S(1)} %maximum_select_fusion.1), channel_id=1, source_target_pairs={{0,4},{1,5},{2,6},{3,7},{4,8},{5,9},{6,10},{7,11},{8,12},{9,13},{1... | collective-permute-start | bytes 1572872 | tf_op jit(solution)/shard_map/ppermute | solution.py:17
  61.0 13.4 %collective-permute-start.4 = (f32[2,256,256]{2,1,0:T(8,128)S(1)}, f32[2,256,256]{2,1,0:T(8,128)S(1)}, u32[]{:S(2)}, u32[]{:S(2)}) collective-permute-start(f32[2,256,256]{2,1,0:T(8,128)S(1)} %maximum_select_fusion.2), channel_id=1, source_target_pairs={{0,8},{1,9},{2,10},{3,11},{4,12},{5,13},{6,14},{7,15},{8,16},{9,17... | collective-permute-start | bytes 1572872 | tf_op jit(solution)/shard_map/ppermute | solution.py:17
  75.9 27.9 %collective-permute-start.5 = (f32[2,256,256]{2,1,0:T(8,128)S(1)}, f32[2,256,256]{2,1,0:T(8,128)}, u32[]{:S(2)}, u32[]{:S(2)}) collective-permute-start(f32[2,256,256]{2,1,0:T(8,128)S(1)} %maximum_select_fusion.3), channel_id=1, source_target_pairs={{0,16},{1,17},{2,18},{3,19},{4,20},{5,21},{6,22},{7,23},{8,24},{9,... | collective-permute-start | bytes 1572872 | tf_op jit(solution)/shard_map/ppermute | solution.py:17
where the time goes:
time: 107 us
  waiting for transfers between devices  79.7 us (74%)
  matrix products  11 us (10%)
  starting transfers between devices  9.41 us (9%)
  local copies, waits for them, and re-layouts  3.91 us (4%)
  other arithmetic  2.66 us (2%)
    ppermute x5, waiting for transfers between devices, from_behind(): return lax.ppermute(x, axis, pairs)  70.9 us
    ppermute x1, waiting for transfers between devices, shifted(): return lax.ppermute(x, axis, [(i, (i + by) % size) for i in range(size)])  8.8 us
    ppermute x5, starting transfers between devices, from_behind(): return lax.ppermute(x, axis, pairs)  8.68 us
    dot_general x9, matrix products, complex_product(): jnp.dot(left[0], joined, preferred_element_type=jnp.float32, precision=la...  5.53 us
    dot_general x9, matrix products, complex_product(): jnp.dot(left[1], joined, preferred_element_type=jnp.float32, precision=la...  5.5 us
  transfers between devices with their start and end apart: 6, of which 6 were waited for; matrix products, arithmetic and copies ran while one was open for 0% of the time, Pallas kernels for 0%

commit v1 on v0

v1 whole, which is shorter than its diff:
```python
import functools

import jax
import jax.numpy as jnp
from jax import lax
from jax.experimental import pallas as pl
from jax.experimental.pallas import tpu as pltpu
from jax.sharding import PartitionSpec as P


time_step = 0.25
plane = 8
parts = 8


def exchanged(x, axis, mask):
    size = lax.axis_size(axis)
    return lax.ppermute(x, axis, [(i, i ^ mask) for i in range(size)])


def from_next(x, axis):
    size = lax.axis_size(axis)
    return lax.ppermute(x, axis, [(i, (i - 1) % size) for i in range(size)])


def split(x):
    high = x.astype(jnp.bfloat16)
    low = (x - high.astype(jnp.float32)).astype(jnp.bfloat16)
    return high, low


def halves(pair):
    real, imag = split(pair[0]), split(pair[1])
    return (real[0], imag[0]), (real[1], imag[1])


def dot(left, right, turned):
    dims = (((1,), (1 if turned else 0,)), ((), ()))
    return lax.dot_general(left, right, dims, preferred_element_type=jnp.float32)


def product(left, right, turned=False):
    (lrh, lih), (lrl, lil) = left
    (rrh, rih), (rrl, ril) = right
    rows = lrh.shape[0]
    high = jnp.concatenate([lrh, lih], axis=0)
    low = jnp.concatenate([lrl, lil], axis=0)
    by_real = dot(high, rrh, turned) + (dot(high, rrl, turned) + dot(low, rrh, turned))
    by_imag = dot(high, rih, turned) + (dot(high, ril, turned) + dot(low, rih, turned))
    return by_real[:rows] - by_imag[rows:], by_imag[:rows] + by_real[rows:]


def call(kernel, outs, scratch, flops, *args):
    as_list = isinstance(outs, list)
    shapes = outs if as_list else [outs]
    moved = sum(a.size * a.dtype.itemsize for a in args)
    moved += sum(s.size * s.dtype.itemsize for s in shapes)
    vmem = pl.BlockSpec(memory_space=pltpu.VMEM)
    return pl.pallas_call(
        kernel,
        out_shape=outs,
        in_specs=[vmem] * len(args),
        out_specs=[vmem] * len(shapes) if as_list else vmem,
        scratch_shapes=scratch,
        compiler_params=pltpu.CompilerParams(vmem_limit_bytes=24 * 1024 * 1024),
        cost_estimate=pl.CostEstimate(flops=flops, bytes_accessed=moved, transcendentals=0),
    )(*args)


def f32(*shape):
    return jax.ShapeDtypeStruct(shape, jnp.float32)


def index_grid(size):
    row = lax.broadcasted_iota(jnp.int32, (size, size), 0)
    col = lax.broadcasted_iota(jnp.int32, (size, size), 1)
    return row, col


def pack_kernel(drawn_ref, packed_ref):
    first, second = drawn_ref[0, 0], drawn_ref[0, 1]
    row, col = index_grid(first.shape[0])
    mirrored = jnp.where(row >= col, first, -second).T
    packed_ref[...] = (jnp.where(row <= col, first, second) + mirrored) * 0.5


def unpacked(packed):
    row, col = index_grid(packed.shape[0])
    mirrored = packed.T
    real = jnp.where(row <= col, packed, mirrored)
    imag = jnp.where(row > col, packed, jnp.where(row < col, -mirrored, 0.0))
    return real, imag


def factor_kernel(first_ref, second_ref, factor_ref):
    first = unpacked(first_ref[...])
    second = unpacked(second_ref[...])
    row, col = index_grid(first[0].shape[0])
    identity = jnp.where(row == col, 1.0, 0.0).astype(jnp.float32)
    both = product(halves(second), halves(first))
    comm_real = both[0] - both[0].T
    comm_imag = both[1] + both[1].T
    shrink = time_step * time_step / 12.0
    real = 0.5 * time_step * (first[1] + second[1]) - shrink * comm_real
    imag = -0.5 * time_step * (first[0] + second[0]) - shrink * comm_imag
    real = -real
    exponent = halves((real, imag))
    nested = (identity + real * 0.25, imag * 0.25)
    for order in (3.0, 2.0, 1.0):
        grown = product(exponent, halves(nested))
        nested = (identity + grown[0] * (1.0 / order), grown[1] * (1.0 / order))
    factor_ref[0] = nested[0]
    factor_ref[1] = nested[1]


def load(ref, rows=slice(None)):
    return ref[0, rows, :], ref[1, rows, :]


def store(ref, pair, rows=slice(None)):
    ref[0, rows, :] = pair[0]
    ref[1, rows, :] = pair[1]


def chip_kernel(axis, own_ref, other_ref, half_ref):
    odd = lax.axis_index(axis) & 1
    rows = half_ref.shape[1]
    half = pl.ds(pl.multiple_of(odd * rows, rows), rows)

    @pl.when(odd == 0)
    def _():
        store(half_ref, product(halves(load(own_ref, half)), halves(load(other_ref))))

    @pl.when(odd == 1)
    def _():
        store(half_ref, product(halves(load(other_ref, half)), halves(load(own_ref))))


def get(high_ref, low_ref, q, rows=slice(None)):
    return (
        (high_ref[q, 0, rows, :], high_ref[q, 1, rows, :]),
        (low_ref[q, 0, rows, :], low_ref[q, 1, rows, :]),
    )


def picked(pair, chosen):
    high, low = pair
    return tuple(
        dot(chosen, high[k], True) + dot(chosen, low[k], True) for k in range(2)
    )


def one_hot_rows(count, size, begin):
    row = lax.broadcasted_iota(jnp.int32, (count, size), 0)
    col = lax.broadcasted_iota(jnp.int32, (count, size), 1)
    return jnp.where(row + begin == col, 1.0, 0.0).astype(jnp.bfloat16)


def gather_kernel(axis, level, *refs):
    in_refs, (slice_ref, high_ref, low_ref) = refs[:8], refs[8:]
    me = lax.axis_index(axis)
    odd, chip = me & 1, (me >> 1) & 3
    size = high_ref.shape[-1]
    half = size // 2
    for rel in range(4):
        for other in range(2):
            begin = pl.multiple_of((odd ^ other) * half, half)
            for k in range(2):
                high, low = split(in_refs[2 * rel + other][k])
                high_ref[chip ^ rel, k, pl.ds(begin, half), :] = high
                low_ref[chip ^ rel, k, pl.ds(begin, half), :] = low
    count = size // parts
    begin = pl.multiple_of((me & (parts - 1)) * count, count)
    upper = (me // level) & 1

    @pl.when(upper == 0)
    def _():
        value = get(high_ref, low_ref, 0, pl.ds(begin, count))
        for q in (1, 2, 3):
            grown = product(value, get(high_ref, low_ref, q))
            value = halves(grown)
        store(slice_ref, grown)

    @pl.when(upper == 1)
    def _():
        chosen = one_hot_rows(count, size, begin)
        grown = picked(get(high_ref, low_ref, 3), chosen)
        for q in (2, 1, 0):
            grown = product(halves(grown), get(high_ref, low_ref, q), True)
        store(slice_ref, grown)


def prefix_kernel(axis, high_ref, low_ref, own_ref, total_ref, local_ref):
    me = lax.axis_index(axis)
    odd, chip = me & 1, (me >> 1) & 3
    first = get(high_ref, low_ref, 0)

    @pl.when((chip == 0) & (odd == 1))
    def _():
        for k in range(2):
            local_ref[k] = first[0][k].astype(jnp.float32) + first[1][k].astype(jnp.float32)

    @pl.when((chip == 0) & (odd == 0))
    def _():
        store(local_ref, load(own_ref))

    value = first
    for q in (1, 2, 3):

        @pl.when((chip == q) & (odd == 0))
        def _(value=value):
            store(local_ref, product(value, halves(load(own_ref))))

        grown = product(value, get(high_ref, low_ref, q))
        store(total_ref, grown)
        value = halves(load(total_ref))

        @pl.when((chip == q) & (odd == 1))
        def _():
            store(local_ref, load(total_ref))


def cut_kernel(axis, level, total_ref, slice_ref):
    me = lax.axis_index(axis)
    count, size = slice_ref.shape[1], slice_ref.shape[2]
    begin = pl.multiple_of((me & (parts - 1)) * count, count)
    upper = (me // level) & 1

    @pl.when(upper == 0)
    def _():
        store(slice_ref, load(total_ref, pl.ds(begin, count)))

    @pl.when(upper == 1)
    def _():
        store(slice_ref, picked(halves(load(total_ref)), one_hot_rows(count, size, begin)))


def double_kernel(axis, level, total_ref, local_ref, mine_ref, other_ref, next_total_ref, next_local_ref):
    me = lax.axis_index(axis)
    odd, upper = me & 1, (me // level) & 1
    half = mine_ref.shape[1]
    top = [jnp.where(odd == 0, mine_ref[k], other_ref[k]) for k in range(2)]
    low = [jnp.where(odd == 0, other_ref[k], mine_ref[k]) for k in range(2)]
    came = halves([jnp.concatenate([top[k], low[k]], axis=0) for k in range(2)])
    total = halves(load(total_ref))

    @pl.when(upper == 0)
    def _():
        store(next_total_ref, product(total, came))
        store(next_local_ref, load(local_ref))

    @pl.when(upper == 1)
    def _():
        store(next_total_ref, product(came, total))
        store(next_local_ref, product(came, halves(load(local_ref))))


def step_kernel(axis, level, came_ref, total_ref, slice_ref):
    upper = (lax.axis_index(axis) // level) & 1
    came = halves(load(came_ref))
    total = halves(load(total_ref))

    @pl.when(upper == 0)
    def _():
        store(slice_ref, product(came, total, True))

    @pl.when(upper == 1)
    def _():
        store(slice_ref, product(came, total))


def assemble(axis, in_refs, whole_ref):
    me = lax.axis_index(axis) & (parts - 1)
    count = in_refs[0].shape[1]
    for k, ref in enumerate(in_refs):
        begin = pl.multiple_of((me ^ k) * count, count)
        store(whole_ref, load(ref), pl.ds(begin, count))


def local_kernel(axis, level, *refs):
    in_refs, local_ref, out_ref, whole_ref = refs[:8], refs[8], refs[9], refs[10]
    upper = (lax.axis_index(axis) // level) & 1

    @pl.when(upper == 0)
    def _():
        for k in range(2):
            out_ref[k] = local_ref[k].T

    @pl.when(upper == 1)
    def _():
        assemble(axis, in_refs, whole_ref)
        grown = product(halves(load(whole_ref)), halves(load(local_ref)))
        for k in range(2):
            out_ref[k] = grown[k].T


def final_kernel(axis, level, *refs):
    in_refs, local_ref, out_ref, whole_ref = refs[:8], refs[8], refs[9], refs[10]
    block = (lax.axis_index(axis) // level) & 3

    def put(pair):
        out_ref[0, 0] = pair[0]
        out_ref[0, 1] = pair[1]

    @pl.when(block < 2)
    def _():
        put(load(local_ref))

    @pl.when(block >= 2)
    def _():
        assemble(axis, in_refs, whole_ref)

    @pl.when(block == 2)
    def _():
        put(product(halves(load(local_ref)), halves(load(whole_ref))))

    @pl.when(block == 3)
    def _():
        put(product(halves(load(local_ref)), halves(load(whole_ref)), True))


def plane_slices(mine, axis):
    even = [mine] + [exchanged(mine, axis, mask) for mask in (2, 4, 6)]
    odd = [exchanged(piece, axis, 1) for piece in even]
    return [piece for both in zip(even, odd) for piece in both]


def on_device(samples):
    axis = "tm"
    devices = lax.axis_size(axis)
    size = samples.shape[-1]
    cube = 8 * size**3
    part = size // parts
    whole = f32(2, size, size)
    strip = f32(2, part, size)

    packed = call(pack_kernel, f32(size, size), [], size * size, samples)
    factor = call(factor_kernel, whole, [], 12 * cube, packed, from_next(packed, axis))
    other = exchanged(factor, axis, 1)
    half = call(
        functools.partial(chip_kernel, axis), f32(2, size // 2, size), [], 3 * cube // 2, factor, other
    )
    received = [half] + [exchanged(half, axis, mask) for mask in (2, 4, 6)]
    pieces = [p for piece in received for p in (piece, exchanged(piece, axis, 1))]

    level = plane
    split_shape = jax.ShapeDtypeStruct((4, 2, size, size), jnp.bfloat16)
    mine, high, low = call(
        functools.partial(gather_kernel, axis, level), [strip, split_shape, split_shape], [], cube, *pieces
    )
    total, local = call(
        functools.partial(prefix_kernel, axis), [whole, whole], [], 12 * cube, high, low, factor
    )
    if devices > 4 * plane:
        while 4 * level < devices:
            came = exchanged(lax.dynamic_slice_in_dim(total, (lax.axis_index(axis) & 1) * (size // 2), size // 2, 1), axis, level)
            paired = exchanged(came, axis, 1)
            total, local = call(
                functools.partial(double_kernel, axis, level), [whole, whole], [], 6 * cube, total, local, came, paired
            )
            level = 2 * level
        mine = call(functools.partial(cut_kernel, axis, level), strip, [], cube, total)
    came = exchanged(mine, axis, level)
    step = call(functools.partial(step_kernel, axis, level), strip, [], 3 * cube // parts, came, total)
    below = exchanged(step, axis, 2 * level)
    room = [pltpu.VMEM((2, size, size), jnp.float32)]
    local = call(
        functools.partial(local_kernel, axis, level), whole, room, 3 * cube, *plane_slices(came, axis), local
    )
    return call(
        functools.partial(final_kernel, axis, level),
        f32(1, 2, size, size),
        room,
        3 * cube,
        *plane_slices(below, axis),
        local,
    )


def solution(mesh):
    in_specs = (P("tm", None, None, None),)
    out_specs = P("tm", None, None, None)
    return jax.shard_map(
        on_device, mesh=mesh, in_specs=in_specs, out_specs=out_specs, check_vma=False
    )
```

time: 107 us -> 60.6 us (0.57)
  waiting for transfers between devices: 79.7 us -> 21 us
  starting transfers between devices: 9.41 us -> 27.3 us
  matrix products: 11 us -> 0 us
  Pallas kernels: 0 us -> 10.8 us
  local copies, waits for them, and re-layouts: 3.91 us -> 1.04 us
  other arithmetic: 2.66 us -> 0 us
    ppermute x6 -> x25, waiting for transfers between devices: 79.7 us -> 21 us  [the longest x24 14.9 us: exchanged(): return lax.ppermute(x, axis, [(i, i ^ mask) for i in range(size)])]
    ppermute x6 -> x25, starting transfers between devices: 9.41 us -> 27.3 us  [the longest x24 26.6 us: exchanged(): return lax.ppermute(x, axis, [(i, i ^ mask) for i in range(size)])]
    dot_general x18 -> x0, matrix products: 11 us -> none  [the longest x9 5.53 us: complex_product(): jnp.dot(left[0], joined, preferred_element_type=jnp.float32, precision=la...]
    pallas_call x0 -> x8, Pallas kernels: none -> 10.8 us  [call(): pl.pallas_call(kernel, out_shape=outs, in_specs=[vmem] * len(args), out_s...]
    squeeze x8 -> x0, local copies, waits for them, and re-layouts: 1.31 us -> none  [complex_product(): joined = jnp.concatenate([right[0], right[1]], axis=1)]
  transfers between devices with their start and end apart: 6 -> 25, of which waited for: 6 -> 8; matrix products, arithmetic and copies ran while one was open for 0% -> 0% of each run, Pallas kernels for 0% -> 5%
where the time goes in v1:
time: 60.6 us; the launch traced here: 60.2 us
  starting transfers between devices  27.3 us (45%)
  waiting for transfers between devices  21 us (35%)
  Pallas kernels  10.8 us (18%)
  local copies, waits for them, and re-layouts  1.04 us (2%)
    ppermute x24, starting transfers between devices, exchanged(): return lax.ppermute(x, axis, [(i, i ^ mask) for i in range(size)])  26.6 us
    ppermute x24, waiting for transfers between devices, exchanged(): return lax.ppermute(x, axis, [(i, i ^ mask) for i in range(size)])  14.9 us
    pallas_call x8, Pallas kernels, call(): pl.pallas_call(kernel, out_shape=outs, in_specs=[vmem] * len(args), out_s...  10.8 us
    ppermute x1, waiting for transfers between devices, from_next(): return lax.ppermute(x, axis, [(i, (i - 1) % size) for i in range(size)])  6.02 us
  transfers between devices with their start and end apart: 25, of which 8 were waited for; matrix products, arithmetic and copies ran while one was open for 0% of the time, Pallas kernels for 5%

profile of v1, /device:TPU:27, one launch (start us, length us, event | category | flops | bytes accessed | tf_op | source)
XLA Modules:
  0.0 60.2 jit_solution(15979518468380981414)
XLA Ops:
  0.0 1.0 %copy-done = f32[1,2,256,256]{3,2,1,0:T(8,128)S(1)} copy-done((f32[1,2,256,256]{3,2,1,0:T(8,128)S(1)}, f32[1,2,256,256]{3,2,1,0:T(8,128)}, u32[]{:S(2)}) %copy-start) | copy-done | bytes 524312
  1.2 0.7 %collective-permute-start = (f32[256,256]{1,0:T(8,128)S(1)}, f32[256,256]{1,0:T(8,128)S(1)}, u32[]{:S(2)}, u32[]{:S(2)}) collective-permute-start(f32[256,256]{1,0:T(8,128)S(1)} %shard_map.17.first_ref), channel_id=1, source_target_pairs={{0,31},{1,0},{2,1},{3,2},{4,3},{5,4},{6,5},{7,6},{8,7},{9,8},{10,9... | collective-permute-start | bytes 786440 | tf_op jit(solution)/shard_map/ppermute | solution.py:23
  1.9 6.0 %collective-permute-done.second_ref = f32[256,256]{1,0:T(8,128)S(1)} collective-permute-done((f32[256,256]{1,0:T(8,128)S(1)}, f32[256,256]{1,0:T(8,128)S(1)}, u32[]{:S(2)}, u32[]{:S(2)}) %collective-permute-start) | collective-permute-done | bytes 262176 | tf_op jit(solution)/shard_map/ppermute | solution.py:23
  7.9 4.0 %shard_map.18.own_ref = f32[2,256,256]{2,1,0:T(8,128)S(1)} custom-call(f32[256,256]{1,0:T(8,128)S(1)} %shard_map.17.first_ref, f32[256,256]{1,0:T(8,128)S(1)} %collective-permute-done.second_ref), custom_call_target="tpu_custom_call" | custom-call | flops 1610612736 | bytes 1048576 | tf_op jit(solution)/shard_map/pallas_call | solution.py:59
  12.1 1.9 %collective-permute-done.1.other_ref = f32[2,256,256]{2,1,0:T(8,128)S(1)} collective-permute-done((f32[2,256,256]{2,1,0:T(8,128)S(1)}, f32[2,256,256]{2,1,0:T(8,128)S(1)}, u32[]{:S(2)}, u32[]{:S(2)}) %collective-permute-start.1) | collective-permute-done | bytes 524320 | tf_op jit(solution)/shard_map/ppermute | solution.py:18
  14.0 0.4 shard_map.19.refs_0_
  14.3 0.4 collective-permute-start.7
  14.8 3.7 %collective-permute-start.5 = (f32[2,128,256]{2,1,0:T(8,128)S(1)}, f32[2,128,256]{2,1,0:T(8,128)S(1)}, u32[]{:S(2)}, u32[]{:S(2)}) collective-permute-start(f32[2,128,256]{2,1,0:T(8,128)S(1)} %shard_map.19.refs_0_), channel_id=1, source_target_pairs={{0,4},{1,5},{2,6},{3,7},{4,0},{5,1},{6,2},{7,3},{8,12},{9,13},{10,... | collective-permute-start | bytes 786440 | tf_op jit(solution)/shard_map/ppermute | solution.py:18
  18.4 1.1 %collective-permute-start.3 = (f32[2,128,256]{2,1,0:T(8,128)S(1)}, f32[2,128,256]{2,1,0:T(8,128)S(1)}, u32[]{:S(2)}, u32[]{:S(2)}) collective-permute-start(f32[2,128,256]{2,1,0:T(8,128)S(1)} %shard_map.19.refs_0_), channel_id=1, source_target_pairs={{0,2},{1,3},{2,0},{3,1},{4,6},{5,7},{6,4},{7,5},{8,10},{9,11},{10,... | collective-permute-start | bytes 786440 | tf_op jit(solution)/shard_map/ppermute | solution.py:18
  19.5 0.7 %collective-permute-start.2 = (f32[2,128,256]{2,1,0:T(8,128)S(1)}, f32[2,128,256]{2,1,0:T(8,128)S(1)}, u32[]{:S(2)}, u32[]{:S(2)}) collective-permute-start(f32[2,128,256]{2,1,0:T(8,128)S(1)} %shard_map.19.refs_0_), channel_id=1, source_target_pairs={{0,1},{1,0},{2,3},{3,2},{4,5},{5,4},{6,7},{7,6},{8,9},{9,8},{10,11... | collective-permute-start | bytes 786440 | tf_op jit(solution)/shard_map/ppermute | solution.py:18
  20.2 2.8 %collective-permute-done.7.refs_6_ = f32[2,128,256]{2,1,0:T(8,128)S(1)} collective-permute-done((f32[2,128,256]{2,1,0:T(8,128)S(1)}, f32[2,128,256]{2,1,0:T(8,128)S(1)}, u32[]{:S(2)}, u32[]{:S(2)}) %collective-permute-start.7) | collective-permute-done | bytes 262176 | tf_op jit(solution)/shard_map/ppermute | solution.py:18
  23.1 1.6 %collective-permute-start.8 = (f32[2,128,256]{2,1,0:T(8,128)S(1)}, f32[2,128,256]{2,1,0:T(8,128)S(1)}, u32[]{:S(2)}, u32[]{:S(2)}) collective-permute-start(f32[2,128,256]{2,1,0:T(8,128)S(1)} %collective-permute-done.7.refs_6_), channel_id=1, source_target_pairs={{0,1},{1,0},{2,3},{3,2},{4,5},{5,4},{6,7},{7,6},{8,9},{9,8},{10,11... | collective-permute-start | bytes 786440 | tf_op jit(solution)/shard_map/ppermute | solution.py:18
  24.7 4.9 %collective-permute-done.5.refs_4_ = f32[2,128,256]{2,1,0:T(8,128)S(1)} collective-permute-done((f32[2,128,256]{2,1,0:T(8,128)S(1)}, f32[2,128,256]{2,1,0:T(8,128)S(1)}, u32[]{:S(2)}, u32[]{:S(2)}) %collective-permute-start.5) | collective-permute-done | bytes 262176 | tf_op jit(solution)/shard_map/ppermute | solution.py:18
  29.6 1.0 %collective-permute-start.6 = (f32[2,128,256]{2,1,0:T(8,128)S(1)}, f32[2,128,256]{2,1,0:T(8,128)S(1)}, u32[]{:S(2)}, u32[]{:S(2)}) collective-permute-start(f32[2,128,256]{2,1,0:T(8,128)S(1)} %collective-permute-done.5.refs_4_), channel_id=1, source_target_pairs={{0,1},{1,0},{2,3},{3,2},{4,5},{5,4},{6,7},{7,6},{8,9},{9,8},{10,11... | collective-permute-start | bytes 786440 | tf_op jit(solution)/shard_map/ppermute | solution.py:18
  30.6 0.9 %collective-permute-done.3.refs_2_ = f32[2,128,256]{2,1,0:T(8,128)S(1)} collective-permute-done((f32[2,128,256]{2,1,0:T(8,128)S(1)}, f32[2,128,256]{2,1,0:T(8,128)S(1)}, u32[]{:S(2)}, u32[]{:S(2)}) %collective-permute-start.3) | collective-permute-done | bytes 262176 | tf_op jit(solution)/shard_map/ppermute | solution.py:18
  31.5 1.0 %collective-permute-start.4 = (f32[2,128,256]{2,1,0:T(8,128)S(1)}, f32[2,128,256]{2,1,0:T(8,128)S(1)}, u32[]{:S(2)}, u32[]{:S(2)}) collective-permute-start(f32[2,128,256]{2,1,0:T(8,128)S(1)} %collective-permute-done.3.refs_2_), channel_id=1, source_target_pairs={{0,1},{1,0},{2,3},{3,2},{4,5},{5,4},{6,7},{7,6},{8,9},{9,8},{10,11... | collective-permute-start | bytes 786440 | tf_op jit(solution)/shard_map/ppermute | solution.py:18
  32.5 1.1 %collective-permute-done.4.refs_3_ = f32[2,128,256]{2,1,0:T(8,128)S(1)} collective-permute-done((f32[2,128,256]{2,1,0:T(8,128)S(1)}, f32[2,128,256]{2,1,0:T(8,128)S(1)}, u32[]{:S(2)}, u32[]{:S(2)}) %collective-permute-start.4) | collective-permute-done | bytes 262176 | tf_op jit(solution)/shard_map/ppermute | solution.py:18
  33.6 1.9 %shard_map.20 = (f32[2,32,256]{2,1,0:T(8,128)S(1)}, bf16[4,2,256,256]{3,2,1,0:T(8,128)(2,1)S(1)}, bf16[4,2,256,256]{3,2,1,0:T(8,128)(2,1)S(1)}) custom-call(f32[2,128,256]{2,1,0:T(8,128)S(1)} %shard_map.19.refs_0_, f32[2,128,256]{2,1,0:T(8,128)S(1)} %collective-permute-done.2.refs_1_, f32[2,128,256]{2,1,0:T(8,128)S(1)} %collective-permute-done.3.refs_2_, ...), custom_call_target="tpu_custom_call" | custom-call | flops 134217728 | bytes 4259840 | tf_op jit(solution)/shard_map/pallas_call | solution.py:59
  35.6 3.1 %collective-permute-done.9.came_ref.refs_0_ = f32[2,32,256]{2,1,0:T(8,128)S(1)} collective-permute-done((f32[2,32,256]{2,1,0:T(8,128)S(1)}, f32[2,32,256]{2,1,0:T(8,128)S(1)}, u32[]{:S(2)}, u32[]{:S(2)}) %collective-permute-start.9) | collective-permute-done | bytes 65568 | tf_op jit(solution)/shard_map/ppermute | solution.py:18
  38.7 1.8 %shard_map.21 = (f32[2,256,256]{2,1,0:T(8,128)S(1)}, f32[2,256,256]{2,1,0:T(8,128)S(1)}) custom-call(bf16[4,2,256,256]{3,2,1,0:T(8,128)(2,1)S(1)} %get-tuple-element.11.high_ref, bf16[4,2,256,256]{3,2,1,0:T(8,128)(2,1)S(1)} %get-tuple-element.12.low_ref, f32[2,256,256]{2,1,0:T(8,128)S(1)} %shard_map.18.own_ref), custom_call_target="tpu_custom_call" | custom-call | flops 1610612736 | bytes 3670016 | tf_op jit(solution)/shard_map/pallas_call | solution.py:59
  40.6 1.6 %collective-permute-start.21 = (f32[2,32,256]{2,1,0:T(8,128)S(1)}, f32[2,32,256]{2,1,0:T(8,128)S(1)}, u32[]{:S(2)}, u32[]{:S(2)}) collective-permute-start(f32[2,32,256]{2,1,0:T(8,128)S(1)} %collective-permute-done.9.came_ref.refs_0_), channel_id=1, source_target_pairs={{0,4},{1,5},{2,6},{3,7},{4,0},{5,1},{6,2},{7,3},{8,12},{9,13},{10,... | collective-permute-start | bytes 196616 | tf_op jit(solution)/shard_map/ppermute | solution.py:18
  42.1 0.3 shard_map.22
  42.6 1.2 %collective-permute-start.19 = (f32[2,32,256]{2,1,0:T(8,128)S(1)}, f32[2,32,256]{2,1,0:T(8,128)S(1)}, u32[]{:S(2)}, u32[]{:S(2)}) collective-permute-start(f32[2,32,256]{2,1,0:T(8,128)S(1)} %collective-permute-done.9.came_ref.refs_0_), channel_id=1, source_target_pairs={{0,2},{1,3},{2,0},{3,1},{4,6},{5,7},{6,4},{7,5},{8,10},{9,11},{10,... | collective-permute-start | bytes 196616 | tf_op jit(solution)/shard_map/ppermute | solution.py:18
  43.8 2.9 %collective-permute-start.18 = (f32[2,32,256]{2,1,0:T(8,128)S(1)}, f32[2,32,256]{2,1,0:T(8,128)S(1)}, u32[]{:S(2)}, u32[]{:S(2)}) collective-permute-start(f32[2,32,256]{2,1,0:T(8,128)S(1)} %collective-permute-done.9.came_ref.refs_0_), channel_id=1, source_target_pairs={{0,1},{1,0},{2,3},{3,2},{4,5},{5,4},{6,7},{7,6},{8,9},{9,8},{10,11... | collective-permute-start | bytes 196616 | tf_op jit(solution)/shard_map/ppermute | solution.py:18
  46.7 0.6 collective-permute-start.22
  47.3 2.3 %collective-permute-start.16 = (f32[2,32,256]{2,1,0:T(8,128)S(1)}, f32[2,32,256]{2,1,0:T(8,128)S(1)}, u32[]{:S(2)}, u32[]{:S(2)}) collective-permute-start(f32[2,32,256]{2,1,0:T(8,128)S(1)} %collective-permute-done.10.refs_0_), channel_id=1, source_target_pairs={{0,6},{1,7},{2,4},{3,5},{4,2},{5,3},{6,0},{7,1},{8,14},{9,15},{10,... | collective-permute-start | bytes 196616 | tf_op jit(solution)/shard_map/ppermute | solution.py:18
  50.0 4.2 %collective-permute-start.20 = (f32[2,32,256]{2,1,0:T(8,128)S(1)}, f32[2,32,256]{2,1,0:T(8,128)S(1)}, u32[]{:S(2)}, u32[]{:S(2)}) collective-permute-start(f32[2,32,256]{2,1,0:T(8,128)S(1)} %collective-permute-done.19.refs_2_), channel_id=1, source_target_pairs={{0,1},{1,0},{2,3},{3,2},{4,5},{5,4},{6,7},{7,6},{8,9},{9,8},{10,11... | collective-permute-start | bytes 196616 | tf_op jit(solution)/shard_map/ppermute | solution.py:18
  54.3 1.6 %collective-permute-start.17 = (f32[2,32,256]{2,1,0:T(8,128)S(1)}, f32[2,32,256]{2,1,0:T(8,128)S(1)}, u32[]{:S(2)}, u32[]{:S(2)}) collective-permute-start(f32[2,32,256]{2,1,0:T(8,128)S(1)} %collective-permute-done.16.refs_6_), channel_id=1, source_target_pairs={{0,1},{1,0},{2,3},{3,2},{4,5},{5,4},{6,7},{7,6},{8,9},{9,8},{10,11... | collective-permute-start | bytes 196616 | tf_op jit(solution)/shard_map/ppermute | solution.py:18
  56.0 0.7 %collective-permute-start.15 = (f32[2,32,256]{2,1,0:T(8,128)S(1)}, f32[2,32,256]{2,1,0:T(8,128)S(1)}, u32[]{:S(2)}, u32[]{:S(2)}) collective-permute-start(f32[2,32,256]{2,1,0:T(8,128)S(1)} %collective-permute-done.14.refs_4_), channel_id=1, source_target_pairs={{0,1},{1,0},{2,3},{3,2},{4,5},{5,4},{6,7},{7,6},{8,9},{9,8},{10,11... | collective-permute-start | bytes 196616 | tf_op jit(solution)/shard_map/ppermute | solution.py:18
  56.6 1.3 %collective-permute-start.13 = (f32[2,32,256]{2,1,0:T(8,128)S(1)}, f32[2,32,256]{2,1,0:T(8,128)S(1)}, u32[]{:S(2)}, u32[]{:S(2)}) collective-permute-start(f32[2,32,256]{2,1,0:T(8,128)S(1)} %collective-permute-done.12.refs_2_), channel_id=1, source_target_pairs={{0,1},{1,0},{2,3},{3,2},{4,5},{5,4},{6,7},{7,6},{8,9},{9,8},{10,11... | collective-permute-start | bytes 196616 | tf_op jit(solution)/shard_map/ppermute | solution.py:18
  57.9 0.8 %shard_map.23.refs_8_ = f32[2,256,256]{2,1,0:T(8,128)S(1)} custom-call(f32[2,32,256]{2,1,0:T(8,128)S(1)} %collective-permute-done.9.came_ref.refs_0_, f32[2,32,256]{2,1,0:T(8,128)S(1)} %collective-permute-done.18.refs_1_, f32[2,32,256]{2,1,0:T(8,128)S(1)} %collective-permute-done.19.refs_2_, f32[2,32,256]{2,1,0:T(8,128)S(1)} %collective-permute-done.20.refs_3_, ...), custom_call_target="tpu_custom_call" | custom-call | flops 402653184 | bytes 1572864 | tf_op jit(solution)/shard_map/pallas_call | solution.py:59
  58.8 1.4 %shard_map.24 = f32[1,2,256,256]{3,2,1,0:T(8,128)} custom-call(f32[2,32,256]{2,1,0:T(8,128)S(1)} %collective-permute-done.10.refs_0_, f32[2,32,256]{2,1,0:T(8,128)S(1)} %collective-permute-done.11.refs_1_, f32[2,32,256]{2,1,0:T(8,128)S(1)} %collective-permute-done.12.refs_2_, f32[2,32,256]{2,1,0:T(8,128)S(1)} %collective-permute-done.13.refs_3_, ...), custom_call_target="tpu_custom_call" | custom-call | flops 402653184 | bytes 1572864 | tf_op jit(solution)/shard_map/pallas_call | solution.py:59
  (28 shorter events, 1.0 us)
Async XLA Ops:
  0.0 1.0 %copy-start = (f32[1,2,256,256]{3,2,1,0:T(8,128)S(1)}, f32[1,2,256,256]{3,2,1,0:T(8,128)}, u32[]{:S(2)}) copy-start(f32[1,2,256,256]{3,2,1,0:T(8,128)} %drawn_ref.1) | copy-start | bytes 1572868
  1.2 6.7 %collective-permute-start = (f32[256,256]{1,0:T(8,128)S(1)}, f32[256,256]{1,0:T(8,128)S(1)}, u32[]{:S(2)}, u32[]{:S(2)}) collective-permute-start(f32[256,256]{1,0:T(8,128)S(1)} %shard_map.17.first_ref), channel_id=1, source_target_pairs={{0,31},{1,0},{2,1},{3,2},{4,3},{5,4},{6,5},{7,6},{8,7},{9,8},{10,9... | collective-permute-start | bytes 786440 | tf_op jit(solution)/shard_map/ppermute | solution.py:23
  12.0 2.0 %collective-permute-start.1 = (f32[2,256,256]{2,1,0:T(8,128)S(1)}, f32[2,256,256]{2,1,0:T(8,128)S(1)}, u32[]{:S(2)}, u32[]{:S(2)}) collective-permute-start(f32[2,256,256]{2,1,0:T(8,128)S(1)} %shard_map.18.own_ref), channel_id=1, source_target_pairs={{0,1},{1,0},{2,3},{3,2},{4,5},{5,4},{6,7},{7,6},{8,9},{9,8},{10,11... | collective-permute-start | bytes 1572872 | tf_op jit(solution)/shard_map/ppermute | solution.py:18
  14.3 8.7 %collective-permute-start.7 = (f32[2,128,256]{2,1,0:T(8,128)S(1)}, f32[2,128,256]{2,1,0:T(8,128)S(1)}, u32[]{:S(2)}, u32[]{:S(2)}) collective-permute-start(f32[2,128,256]{2,1,0:T(8,128)S(1)} %shard_map.19.refs_0_), channel_id=1, source_target_pairs={{0,6},{1,7},{2,4},{3,5},{4,2},{5,3},{6,0},{7,1},{8,14},{9,15},{10,... | collective-permute-start | bytes 786440 | tf_op jit(solution)/shard_map/ppermute | solution.py:18
  14.8 14.8 %collective-permute-start.5 = (f32[2,128,256]{2,1,0:T(8,128)S(1)}, f32[2,128,256]{2,1,0:T(8,128)S(1)}, u32[]{:S(2)}, u32[]{:S(2)}) collective-permute-start(f32[2,128,256]{2,1,0:T(8,128)S(1)} %shard_map.19.refs_0_), channel_id=1, source_target_pairs={{0,4},{1,5},{2,6},{3,7},{4,0},{5,1},{6,2},{7,3},{8,12},{9,13},{10,... | collective-permute-start | bytes 786440 | tf_op jit(solution)/shard_map/ppermute | solution.py:18
  18.4 13.0 %collective-permute-start.3 = (f32[2,128,256]{2,1,0:T(8,128)S(1)}, f32[2,128,256]{2,1,0:T(8,128)S(1)}, u32[]{:S(2)}, u32[]{:S(2)}) collective-permute-start(f32[2,128,256]{2,1,0:T(8,128)S(1)} %shard_map.19.refs_0_), channel_id=1, source_target_pairs={{0,2},{1,3},{2,0},{3,1},{4,6},{5,7},{6,4},{7,5},{8,10},{9,11},{10,... | collective-permute-start | bytes 786440 | tf_op jit(solution)/shard_map/ppermute | solution.py:18
  19.5 12.9 %collective-permute-start.2 = (f32[2,128,256]{2,1,0:T(8,128)S(1)}, f32[2,128,256]{2,1,0:T(8,128)S(1)}, u32[]{:S(2)}, u32[]{:S(2)}) collective-permute-start(f32[2,128,256]{2,1,0:T(8,128)S(1)} %shard_map.19.refs_0_), channel_id=1, source_target_pairs={{0,1},{1,0},{2,3},{3,2},{4,5},{5,4},{6,7},{7,6},{8,9},{9,8},{10,11... | collective-permute-start | bytes 786440 | tf_op jit(solution)/shard_map/ppermute | solution.py:18
  23.1 9.4 %collective-permute-start.8 = (f32[2,128,256]{2,1,0:T(8,128)S(1)}, f32[2,128,256]{2,1,0:T(8,128)S(1)}, u32[]{:S(2)}, u32[]{:S(2)}) collective-permute-start(f32[2,128,256]{2,1,0:T(8,128)S(1)} %collective-permute-done.7.refs_6_), channel_id=1, source_target_pairs={{0,1},{1,0},{2,3},{3,2},{4,5},{5,4},{6,7},{7,6},{8,9},{9,8},{10,11... | collective-permute-start | bytes 786440 | tf_op jit(solution)/shard_map/ppermute | solution.py:18
  29.6 2.9 %collective-permute-start.6 = (f32[2,128,256]{2,1,0:T(8,128)S(1)}, f32[2,128,256]{2,1,0:T(8,128)S(1)}, u32[]{:S(2)}, u32[]{:S(2)}) collective-permute-start(f32[2,128,256]{2,1,0:T(8,128)S(1)} %collective-permute-done.5.refs_4_), channel_id=1, source_target_pairs={{0,1},{1,0},{2,3},{3,2},{4,5},{5,4},{6,7},{7,6},{8,9},{9,8},{10,11... | collective-permute-start | bytes 786440 | tf_op jit(solution)/shard_map/ppermute | solution.py:18
  31.5 2.2 %collective-permute-start.4 = (f32[2,128,256]{2,1,0:T(8,128)S(1)}, f32[2,128,256]{2,1,0:T(8,128)S(1)}, u32[]{:S(2)}, u32[]{:S(2)}) collective-permute-start(f32[2,128,256]{2,1,0:T(8,128)S(1)} %collective-permute-done.3.refs_2_), channel_id=1, source_target_pairs={{0,1},{1,0},{2,3},{3,2},{4,5},{5,4},{6,7},{7,6},{8,9},{9,8},{10,11... | collective-permute-start | bytes 786440 | tf_op jit(solution)/shard_map/ppermute | solution.py:18
  35.5 3.2 %collective-permute-start.9 = (f32[2,32,256]{2,1,0:T(8,128)S(1)}, f32[2,32,256]{2,1,0:T(8,128)S(1)}, u32[]{:S(2)}, u32[]{:S(2)}) collective-permute-start(f32[2,32,256]{2,1,0:T(8,128)S(1)} %get-tuple-element.10), channel_id=1, source_target_pairs={{0,8},{1,9},{2,10},{3,11},{4,12},{5,13},{6,14},{7,15},{8,0},{9,1},... | collective-permute-start | bytes 196616 | tf_op jit(solution)/shard_map/ppermute | solution.py:18
  38.7 8.0 %collective-permute-start.23 = (f32[2,32,256]{2,1,0:T(8,128)S(1)}, f32[2,32,256]{2,1,0:T(8,128)S(1)}, u32[]{:S(2)}, u32[]{:S(2)}) collective-permute-start(f32[2,32,256]{2,1,0:T(8,128)S(1)} %collective-permute-done.9.came_ref.refs_0_), channel_id=1, source_target_pairs={{0,6},{1,7},{2,4},{3,5},{4,2},{5,3},{6,0},{7,1},{8,14},{9,15},{10,... | collective-permute-start | bytes 196616 | tf_op jit(solution)/shard_map/ppermute | solution.py:18
  40.6 6.1 %collective-permute-start.21 = (f32[2,32,256]{2,1,0:T(8,128)S(1)}, f32[2,32,256]{2,1,0:T(8,128)S(1)}, u32[]{:S(2)}, u32[]{:S(2)}) collective-permute-start(f32[2,32,256]{2,1,0:T(8,128)S(1)} %collective-permute-done.9.came_ref.refs_0_), channel_id=1, source_target_pairs={{0,4},{1,5},{2,6},{3,7},{4,0},{5,1},{6,2},{7,3},{8,12},{9,13},{10,... | collective-permute-start | bytes 196616 | tf_op jit(solution)/shard_map/ppermute | solution.py:18
  42.5 4.8 %collective-permute-start.10 = (f32[2,32,256]{2,1,0:T(8,128)S(1)}, f32[2,32,256]{2,1,0:T(8,128)S(1)}, u32[]{:S(2)}, u32[]{:S(2)}) collective-permute-start(f32[2,32,256]{2,1,0:T(8,128)S(1)} %shard_map.22), channel_id=1, source_target_pairs={{0,16},{1,17},{2,18},{3,19},{4,20},{5,21},{6,22},{7,23},{8,24},{9,... | collective-permute-start | bytes 196616 | tf_op jit(solution)/shard_map/ppermute | solution.py:18
  42.6 7.0 %collective-permute-start.19 = (f32[2,32,256]{2,1,0:T(8,128)S(1)}, f32[2,32,256]{2,1,0:T(8,128)S(1)}, u32[]{:S(2)}, u32[]{:S(2)}) collective-permute-start(f32[2,32,256]{2,1,0:T(8,128)S(1)} %collective-permute-done.9.came_ref.refs_0_), channel_id=1, source_target_pairs={{0,2},{1,3},{2,0},{3,1},{4,6},{5,7},{6,4},{7,5},{8,10},{9,11},{10,... | collective-permute-start | bytes 196616 | tf_op jit(solution)/shard_map/ppermute | solution.py:18
  43.8 6.0 %collective-permute-start.18 = (f32[2,32,256]{2,1,0:T(8,128)S(1)}, f32[2,32,256]{2,1,0:T(8,128)S(1)}, u32[]{:S(2)}, u32[]{:S(2)}) collective-permute-start(f32[2,32,256]{2,1,0:T(8,128)S(1)} %collective-permute-done.9.came_ref.refs_0_), channel_id=1, source_target_pairs={{0,1},{1,0},{2,3},{3,2},{4,5},{5,4},{6,7},{7,6},{8,9},{9,8},{10,11... | collective-permute-start | bytes 196616 | tf_op jit(solution)/shard_map/ppermute | solution.py:18
  46.7 3.3 %collective-permute-start.24 = (f32[2,32,256]{2,1,0:T(8,128)S(1)}, f32[2,32,256]{2,1,0:T(8,128)S(1)}, u32[]{:S(2)}, u32[]{:S(2)}) collective-permute-start(f32[2,32,256]{2,1,0:T(8,128)S(1)} %collective-permute-done.23.refs_6_), channel_id=1, source_target_pairs={{0,1},{1,0},{2,3},{3,2},{4,5},{5,4},{6,7},{7,6},{8,9},{9,8},{10,11... | collective-permute-start | bytes 196616 | tf_op jit(solution)/shard_map/ppermute | solution.py:18
  46.7 7.6 %collective-permute-start.22 = (f32[2,32,256]{2,1,0:T(8,128)S(1)}, f32[2,32,256]{2,1,0:T(8,128)S(1)}, u32[]{:S(2)}, u32[]{:S(2)}) collective-permute-start(f32[2,32,256]{2,1,0:T(8,128)S(1)} %collective-permute-done.21.refs_4_), channel_id=1, source_target_pairs={{0,1},{1,0},{2,3},{3,2},{4,5},{5,4},{6,7},{7,6},{8,9},{9,8},{10,11... | collective-permute-start | bytes 196616 | tf_op jit(solution)/shard_map/ppermute | solution.py:18
  47.3 7.1 %collective-permute-start.16 = (f32[2,32,256]{2,1,0:T(8,128)S(1)}, f32[2,32,256]{2,1,0:T(8,128)S(1)}, u32[]{:S(2)}, u32[]{:S(2)}) collective-permute-start(f32[2,32,256]{2,1,0:T(8,128)S(1)} %collective-permute-done.10.refs_0_), channel_id=1, source_target_pairs={{0,6},{1,7},{2,4},{3,5},{4,2},{5,3},{6,0},{7,1},{8,14},{9,15},{10,... | collective-permute-start | bytes 196616 | tf_op jit(solution)/shard_map/ppermute | solution.py:18
  49.6 6.3 %collective-permute-start.14 = (f32[2,32,256]{2,1,0:T(8,128)S(1)}, f32[2,32,256]{2,1,0:T(8,128)S(1)}, u32[]{:S(2)}, u32[]{:S(2)}) collective-permute-start(f32[2,32,256]{2,1,0:T(8,128)S(1)} %collective-permute-done.10.refs_0_), channel_id=1, source_target_pairs={{0,4},{1,5},{2,6},{3,7},{4,0},{5,1},{6,2},{7,3},{8,12},{9,13},{10,... | collective-permute-start | bytes 196616 | tf_op jit(solution)/shard_map/ppermute | solution.py:18
  49.7 6.9 %collective-permute-start.12 = (f32[2,32,256]{2,1,0:T(8,128)S(1)}, f32[2,32,256]{2,1,0:T(8,128)S(1)}, u32[]{:S(2)}, u32[]{:S(2)}) collective-permute-start(f32[2,32,256]{2,1,0:T(8,128)S(1)} %collective-permute-done.10.refs_0_), channel_id=1, source_target_pairs={{0,2},{1,3},{2,0},{3,1},{4,6},{5,7},{6,4},{7,5},{8,10},{9,11},{10,... | collective-permute-start | bytes 196616 | tf_op jit(solution)/shard_map/ppermute | solution.py:18
  50.0 7.9 %collective-permute-start.20 = (f32[2,32,256]{2,1,0:T(8,128)S(1)}, f32[2,32,256]{2,1,0:T(8,128)S(1)}, u32[]{:S(2)}, u32[]{:S(2)}) collective-permute-start(f32[2,32,256]{2,1,0:T(8,128)S(1)} %collective-permute-done.19.refs_2_), channel_id=1, source_target_pairs={{0,1},{1,0},{2,3},{3,2},{4,5},{5,4},{6,7},{7,6},{8,9},{9,8},{10,11... | collective-permute-start | bytes 196616 | tf_op jit(solution)/shard_map/ppermute | solution.py:18
  54.3 4.4 %collective-permute-start.11 = (f32[2,32,256]{2,1,0:T(8,128)S(1)}, f32[2,32,256]{2,1,0:T(8,128)S(1)}, u32[]{:S(2)}, u32[]{:S(2)}) collective-permute-start(f32[2,32,256]{2,1,0:T(8,128)S(1)} %collective-permute-done.10.refs_0_), channel_id=1, source_target_pairs={{0,1},{1,0},{2,3},{3,2},{4,5},{5,4},{6,7},{7,6},{8,9},{9,8},{10,11... | collective-permute-start | bytes 196616 | tf_op jit(solution)/shard_map/ppermute | solution.py:18
  54.3 4.3 %collective-permute-start.17 = (f32[2,32,256]{2,1,0:T(8,128)S(1)}, f32[2,32,256]{2,1,0:T(8,128)S(1)}, u32[]{:S(2)}, u32[]{:S(2)}) collective-permute-start(f32[2,32,256]{2,1,0:T(8,128)S(1)} %collective-permute-done.16.refs_6_), channel_id=1, source_target_pairs={{0,1},{1,0},{2,3},{3,2},{4,5},{5,4},{6,7},{7,6},{8,9},{9,8},{10,11... | collective-permute-start | bytes 196616 | tf_op jit(solution)/shard_map/ppermute | solution.py:18
  56.0 2.7 %collective-permute-start.15 = (f32[2,32,256]{2,1,0:T(8,128)S(1)}, f32[2,32,256]{2,1,0:T(8,128)S(1)}, u32[]{:S(2)}, u32[]{:S(2)}) collective-permute-start(f32[2,32,256]{2,1,0:T(8,128)S(1)} %collective-permute-done.14.refs_4_), channel_id=1, source_target_pairs={{0,1},{1,0},{2,3},{3,2},{4,5},{5,4},{6,7},{7,6},{8,9},{9,8},{10,11... | collective-permute-start | bytes 196616 | tf_op jit(solution)/shard_map/ppermute | solution.py:18
  56.6 2.2 %collective-permute-start.13 = (f32[2,32,256]{2,1,0:T(8,128)S(1)}, f32[2,32,256]{2,1,0:T(8,128)S(1)}, u32[]{:S(2)}, u32[]{:S(2)}) collective-permute-start(f32[2,32,256]{2,1,0:T(8,128)S(1)} %collective-permute-done.12.refs_2_), channel_id=1, source_target_pairs={{0,1},{1,0},{2,3},{3,2},{4,5},{5,4},{6,7},{7,6},{8,9},{9,8},{10,11... | collective-permute-start | bytes 196616 | tf_op jit(solution)/shard_map/ppermute | solution.py:18

commit v2 on v1

--- a/solution.py
+++ b/solution.py
@@ -238,7 +238,6 @@
 def double_kernel(axis, level, total_ref, local_ref, mine_ref, other_ref, next_total_ref, next_local_ref):
     me = lax.axis_index(axis)
     odd, upper = me & 1, (me // level) & 1
-    half = mine_ref.shape[1]
     top = [jnp.where(odd == 0, mine_ref[k], other_ref[k]) for k in range(2)]
     low = [jnp.where(odd == 0, other_ref[k], mine_ref[k]) for k in range(2)]
     came = halves([jnp.concatenate([top[k], low[k]], axis=0) for k in range(2)])
@@ -325,7 +324,7 @@
     return [piece for both in zip(even, odd) for piece in both]
 
 
-def on_device(samples):
+def cumulative(samples):
     axis = "tm"
     devices = lax.axis_size(axis)
     size = samples.shape[-1]
@@ -337,9 +336,7 @@
     packed = call(pack_kernel, f32(size, size), [], size * size, samples)
     factor = call(factor_kernel, whole, [], 12 * cube, packed, from_next(packed, axis))
     other = exchanged(factor, axis, 1)
-    half = call(
-        functools.partial(chip_kernel, axis), f32(2, size // 2, size), [], 3 * cube // 2, factor, other
-    )
+    half = call(functools.partial(chip_kernel, axis), f32(2, size // 2, size), [], 3 * cube // 2, factor, other)
     received = [half] + [exchanged(half, axis, mask) for mask in (2, 4, 6)]
     pieces = [p for piece in received for p in (piece, exchanged(piece, axis, 1))]
 
@@ -348,12 +345,11 @@
     mine, high, low = call(
         functools.partial(gather_kernel, axis, level), [strip, split_shape, split_shape], [], cube, *pieces
     )
-    total, local = call(
-        functools.partial(prefix_kernel, axis), [whole, whole], [], 12 * cube, high, low, factor
-    )
+    total, local = call(functools.partial(prefix_kernel, axis), [whole, whole], [], 12 * cube, high, low, factor)
     if devices > 4 * plane:
         while 4 * level < devices:
-            came = exchanged(lax.dynamic_slice_in_dim(total, (lax.axis_index(axis) & 1) * (size // 2), size // 2, 1), axis, level)
+            half_of = lax.dynamic_slice_in_dim(total, (lax.axis_index(axis) & 1) * (size // 2), size // 2, 1)
+            came = exchanged(half_of, axis, level)
             paired = exchanged(came, axis, 1)
             total, local = call(
                 functools.partial(double_kernel, axis, level), [whole, whole], [], 6 * cube, total, local, came, paired
@@ -364,9 +360,7 @@
     step = call(functools.partial(step_kernel, axis, level), strip, [], 3 * cube // parts, came, total)
     below = exchanged(step, axis, 2 * level)
     room = [pltpu.VMEM((2, size, size), jnp.float32)]
-    local = call(
-        functools.partial(local_kernel, axis, level), whole, room, 3 * cube, *plane_slices(came, axis), local
-    )
+    local = call(functools.partial(local_kernel, axis, level), whole, room, 3 * cube, *plane_slices(came, axis), local)
     return call(
         functools.partial(final_kernel, axis, level),
         f32(1, 2, size, size),
@@ -380,6 +374,4 @@
 def solution(mesh):
     in_specs = (P("tm", None, None, None),)
     out_specs = P("tm", None, None, None)
-    return jax.shard_map(
-        on_device, mesh=mesh, in_specs=in_specs, out_specs=out_specs, check_vma=False
-    )
+    return jax.shard_map(cumulative, mesh=mesh, in_specs=in_specs, out_specs=out_specs, check_vma=False)

time: 60.6 us -> 60.6 us (level)
  no operation moved by 1% of the time
where the time goes in v2:
time: 60.6 us; the launch traced here: 60.2 us
  starting transfers between devices  27.3 us (45%)
  waiting for transfers between devices  21 us (35%)
  Pallas kernels  10.8 us (18%)
  local copies, waits for them, and re-layouts  1.04 us (2%)
    ppermute x24, starting transfers between devices, exchanged(): return lax.ppermute(x, axis, [(i, i ^ mask) for i in range(size)])  26.6 us
    ppermute x24, waiting for transfers between devices, exchanged(): return lax.ppermute(x, axis, [(i, i ^ mask) for i in range(size)])  14.9 us
    pallas_call x8, Pallas kernels, call(): pl.pallas_call(kernel, out_shape=outs, in_specs=[vmem] * len(args), out_s...  10.8 us
    ppermute x1, waiting for transfers between devices, from_next(): return lax.ppermute(x, axis, [(i, (i - 1) % size) for i in range(size)])  6.02 us
  transfers between devices with their start and end apart: 25, of which 8 were waited for; matrix products, arithmetic and copies ran while one was open for 0% of the time, Pallas kernels for 5%

profile of v2, /device:TPU:27, one launch (start us, length us, event | category | flops | bytes accessed | tf_op | source)
XLA Modules:
  0.0 60.2 jit_solution(15979518468380981414)
XLA Ops:
  0.0 1.0 %copy-done = f32[1,2,256,256]{3,2,1,0:T(8,128)S(1)} copy-done((f32[1,2,256,256]{3,2,1,0:T(8,128)S(1)}, f32[1,2,256,256]{3,2,1,0:T(8,128)}, u32[]{:S(2)}) %copy-start) | copy-done | bytes 524312
  1.2 0.7 %collective-permute-start = (f32[256,256]{1,0:T(8,128)S(1)}, f32[256,256]{1,0:T(8,128)S(1)}, u32[]{:S(2)}, u32[]{:S(2)}) collective-permute-start(f32[256,256]{1,0:T(8,128)S(1)} %shard_map.17.first_ref), channel_id=1, source_target_pairs={{0,31},{1,0},{2,1},{3,2},{4,3},{5,4},{6,5},{7,6},{8,7},{9,8},{10,9... | collective-permute-start | bytes 786440 | tf_op jit(solution)/shard_map/ppermute | solution.py:23
  1.9 6.0 %collective-permute-done.second_ref = f32[256,256]{1,0:T(8,128)S(1)} collective-permute-done((f32[256,256]{1,0:T(8,128)S(1)}, f32[256,256]{1,0:T(8,128)S(1)}, u32[]{:S(2)}, u32[]{:S(2)}) %collective-permute-start) | collective-permute-done | bytes 262176 | tf_op jit(solution)/shard_map/ppermute | solution.py:23
  7.9 4.0 %shard_map.18.own_ref = f32[2,256,256]{2,1,0:T(8,128)S(1)} custom-call(f32[256,256]{1,0:T(8,128)S(1)} %shard_map.17.first_ref, f32[256,256]{1,0:T(8,128)S(1)} %collective-permute-done.second_ref), custom_call_target="tpu_custom_call" | custom-call | flops 1610612736 | bytes 1048576 | tf_op jit(solution)/shard_map/pallas_call | solution.py:59
  12.1 1.9 %collective-permute-done.1.other_ref = f32[2,256,256]{2,1,0:T(8,128)S(1)} collective-permute-done((f32[2,256,256]{2,1,0:T(8,128)S(1)}, f32[2,256,256]{2,1,0:T(8,128)S(1)}, u32[]{:S(2)}, u32[]{:S(2)}) %collective-permute-start.1) | collective-permute-done | bytes 524320 | tf_op jit(solution)/shard_map/ppermute | solution.py:18
  14.0 0.4 shard_map.19.refs_0_
  14.3 0.4 collective-permute-start.7
  14.8 3.7 %collective-permute-start.5 = (f32[2,128,256]{2,1,0:T(8,128)S(1)}, f32[2,128,256]{2,1,0:T(8,128)S(1)}, u32[]{:S(2)}, u32[]{:S(2)}) collective-permute-start(f32[2,128,256]{2,1,0:T(8,128)S(1)} %shard_map.19.refs_0_), channel_id=1, source_target_pairs={{0,4},{1,5},{2,6},{3,7},{4,0},{5,1},{6,2},{7,3},{8,12},{9,13},{10,... | collective-permute-start | bytes 786440 | tf_op jit(solution)/shard_map/ppermute | solution.py:18
  18.4 1.1 %collective-permute-start.3 = (f32[2,128,256]{2,1,0:T(8,128)S(1)}, f32[2,128,256]{2,1,0:T(8,128)S(1)}, u32[]{:S(2)}, u32[]{:S(2)}) collective-permute-start(f32[2,128,256]{2,1,0:T(8,128)S(1)} %shard_map.19.refs_0_), channel_id=1, source_target_pairs={{0,2},{1,3},{2,0},{3,1},{4,6},{5,7},{6,4},{7,5},{8,10},{9,11},{10,... | collective-permute-start | bytes 786440 | tf_op jit(solution)/shard_map/ppermute | solution.py:18
  19.5 0.7 %collective-permute-start.2 = (f32[2,128,256]{2,1,0:T(8,128)S(1)}, f32[2,128,256]{2,1,0:T(8,128)S(1)}, u32[]{:S(2)}, u32[]{:S(2)}) collective-permute-start(f32[2,128,256]{2,1,0:T(8,128)S(1)} %shard_map.19.refs_0_), channel_id=1, source_target_pairs={{0,1},{1,0},{2,3},{3,2},{4,5},{5,4},{6,7},{7,6},{8,9},{9,8},{10,11... | collective-permute-start | bytes 786440 | tf_op jit(solution)/shard_map/ppermute | solution.py:18
  20.2 2.8 %collective-permute-done.7.refs_6_ = f32[2,128,256]{2,1,0:T(8,128)S(1)} collective-permute-done((f32[2,128,256]{2,1,0:T(8,128)S(1)}, f32[2,128,256]{2,1,0:T(8,128)S(1)}, u32[]{:S(2)}, u32[]{:S(2)}) %collective-permute-start.7) | collective-permute-done | bytes 262176 | tf_op jit(solution)/shard_map/ppermute | solution.py:18
  23.1 1.6 %collective-permute-start.8 = (f32[2,128,256]{2,1,0:T(8,128)S(1)}, f32[2,128,256]{2,1,0:T(8,128)S(1)}, u32[]{:S(2)}, u32[]{:S(2)}) collective-permute-start(f32[2,128,256]{2,1,0:T(8,128)S(1)} %collective-permute-done.7.refs_6_), channel_id=1, source_target_pairs={{0,1},{1,0},{2,3},{3,2},{4,5},{5,4},{6,7},{7,6},{8,9},{9,8},{10,11... | collective-permute-start | bytes 786440 | tf_op jit(solution)/shard_map/ppermute | solution.py:18
  24.7 4.9 %collective-permute-done.5.refs_4_ = f32[2,128,256]{2,1,0:T(8,128)S(1)} collective-permute-done((f32[2,128,256]{2,1,0:T(8,128)S(1)}, f32[2,128,256]{2,1,0:T(8,128)S(1)}, u32[]{:S(2)}, u32[]{:S(2)}) %collective-permute-start.5) | collective-permute-done | bytes 262176 | tf_op jit(solution)/shard_map/ppermute | solution.py:18
  29.6 1.0 %collective-permute-start.6 = (f32[2,128,256]{2,1,0:T(8,128)S(1)}, f32[2,128,256]{2,1,0:T(8,128)S(1)}, u32[]{:S(2)}, u32[]{:S(2)}) collective-permute-start(f32[2,128,256]{2,1,0:T(8,128)S(1)} %collective-permute-done.5.refs_4_), channel_id=1, source_target_pairs={{0,1},{1,0},{2,3},{3,2},{4,5},{5,4},{6,7},{7,6},{8,9},{9,8},{10,11... | collective-permute-start | bytes 786440 | tf_op jit(solution)/shard_map/ppermute | solution.py:18
  30.6 0.9 %collective-permute-done.3.refs_2_ = f32[2,128,256]{2,1,0:T(8,128)S(1)} collective-permute-done((f32[2,128,256]{2,1,0:T(8,128)S(1)}, f32[2,128,256]{2,1,0:T(8,128)S(1)}, u32[]{:S(2)}, u32[]{:S(2)}) %collective-permute-start.3) | collective-permute-done | bytes 262176 | tf_op jit(solution)/shard_map/ppermute | solution.py:18
  31.5 1.0 %collective-permute-start.4 = (f32[2,128,256]{2,1,0:T(8,128)S(1)}, f32[2,128,256]{2,1,0:T(8,128)S(1)}, u32[]{:S(2)}, u32[]{:S(2)}) collective-permute-start(f32[2,128,256]{2,1,0:T(8,128)S(1)} %collective-permute-done.3.refs_2_), channel_id=1, source_target_pairs={{0,1},{1,0},{2,3},{3,2},{4,5},{5,4},{6,7},{7,6},{8,9},{9,8},{10,11... | collective-permute-start | bytes 786440 | tf_op jit(solution)/shard_map/ppermute | solution.py:18
  32.5 1.1 %collective-permute-done.4.refs_3_ = f32[2,128,256]{2,1,0:T(8,128)S(1)} collective-permute-done((f32[2,128,256]{2,1,0:T(8,128)S(1)}, f32[2,128,256]{2,1,0:T(8,128)S(1)}, u32[]{:S(2)}, u32[]{:S(2)}) %collective-permute-start.4) | collective-permute-done | bytes 262176 | tf_op jit(solution)/shard_map/ppermute | solution.py:18
  33.6 1.9 %shard_map.20 = (f32[2,32,256]{2,1,0:T(8,128)S(1)}, bf16[4,2,256,256]{3,2,1,0:T(8,128)(2,1)S(1)}, bf16[4,2,256,256]{3,2,1,0:T(8,128)(2,1)S(1)}) custom-call(f32[2,128,256]{2,1,0:T(8,128)S(1)} %shard_map.19.refs_0_, f32[2,128,256]{2,1,0:T(8,128)S(1)} %collective-permute-done.2.refs_1_, f32[2,128,256]{2,1,0:T(8,128)S(1)} %collective-permute-done.3.refs_2_, ...), custom_call_target="tpu_custom_call" | custom-call | flops 134217728 | bytes 4259840 | tf_op jit(solution)/shard_map/pallas_call | solution.py:59
  35.6 3.1 %collective-permute-done.9.came_ref.refs_0_ = f32[2,32,256]{2,1,0:T(8,128)S(1)} collective-permute-done((f32[2,32,256]{2,1,0:T(8,128)S(1)}, f32[2,32,256]{2,1,0:T(8,128)S(1)}, u32[]{:S(2)}, u32[]{:S(2)}) %collective-permute-start.9) | collective-permute-done | bytes 65568 | tf_op jit(solution)/shard_map/ppermute | solution.py:18
  38.7 1.8 %shard_map.21 = (f32[2,256,256]{2,1,0:T(8,128)S(1)}, f32[2,256,256]{2,1,0:T(8,128)S(1)}) custom-call(bf16[4,2,256,256]{3,2,1,0:T(8,128)(2,1)S(1)} %get-tuple-element.11.high_ref, bf16[4,2,256,256]{3,2,1,0:T(8,128)(2,1)S(1)} %get-tuple-element.12.low_ref, f32[2,256,256]{2,1,0:T(8,128)S(1)} %shard_map.18.own_ref), custom_call_target="tpu_custom_call" | custom-call | flops 1610612736 | bytes 3670016 | tf_op jit(solution)/shard_map/pallas_call | solution.py:59
  40.6 1.6 %collective-permute-start.21 = (f32[2,32,256]{2,1,0:T(8,128)S(1)}, f32[2,32,256]{2,1,0:T(8,128)S(1)}, u32[]{:S(2)}, u32[]{:S(2)}) collective-permute-start(f32[2,32,256]{2,1,0:T(8,128)S(1)} %collective-permute-done.9.came_ref.refs_0_), channel_id=1, source_target_pairs={{0,4},{1,5},{2,6},{3,7},{4,0},{5,1},{6,2},{7,3},{8,12},{9,13},{10,... | collective-permute-start | bytes 196616 | tf_op jit(solution)/shard_map/ppermute | solution.py:18
  42.1 0.3 shard_map.22
  42.6 1.2 %collective-permute-start.19 = (f32[2,32,256]{2,1,0:T(8,128)S(1)}, f32[2,32,256]{2,1,0:T(8,128)S(1)}, u32[]{:S(2)}, u32[]{:S(2)}) collective-permute-start(f32[2,32,256]{2,1,0:T(8,128)S(1)} %collective-permute-done.9.came_ref.refs_0_), channel_id=1, source_target_pairs={{0,2},{1,3},{2,0},{3,1},{4,6},{5,7},{6,4},{7,5},{8,10},{9,11},{10,... | collective-permute-start | bytes 196616 | tf_op jit(solution)/shard_map/ppermute | solution.py:18
  43.8 2.9 %collective-permute-start.18 = (f32[2,32,256]{2,1,0:T(8,128)S(1)}, f32[2,32,256]{2,1,0:T(8,128)S(1)}, u32[]{:S(2)}, u32[]{:S(2)}) collective-permute-start(f32[2,32,256]{2,1,0:T(8,128)S(1)} %collective-permute-done.9.came_ref.refs_0_), channel_id=1, source_target_pairs={{0,1},{1,0},{2,3},{3,2},{4,5},{5,4},{6,7},{7,6},{8,9},{9,8},{10,11... | collective-permute-start | bytes 196616 | tf_op jit(solution)/shard_map/ppermute | solution.py:18
  46.7 0.6 collective-permute-start.22
  47.3 2.3 %collective-permute-start.16 = (f32[2,32,256]{2,1,0:T(8,128)S(1)}, f32[2,32,256]{2,1,0:T(8,128)S(1)}, u32[]{:S(2)}, u32[]{:S(2)}) collective-permute-start(f32[2,32,256]{2,1,0:T(8,128)S(1)} %collective-permute-done.10.refs_0_), channel_id=1, source_target_pairs={{0,6},{1,7},{2,4},{3,5},{4,2},{5,3},{6,0},{7,1},{8,14},{9,15},{10,... | collective-permute-start | bytes 196616 | tf_op jit(solution)/shard_map/ppermute | solution.py:18
  50.0 4.2 %collective-permute-start.20 = (f32[2,32,256]{2,1,0:T(8,128)S(1)}, f32[2,32,256]{2,1,0:T(8,128)S(1)}, u32[]{:S(2)}, u32[]{:S(2)}) collective-permute-start(f32[2,32,256]{2,1,0:T(8,128)S(1)} %collective-permute-done.19.refs_2_), channel_id=1, source_target_pairs={{0,1},{1,0},{2,3},{3,2},{4,5},{5,4},{6,7},{7,6},{8,9},{9,8},{10,11... | collective-permute-start | bytes 196616 | tf_op jit(solution)/shard_map/ppermute | solution.py:18
  54.3 1.6 %collective-permute-start.17 = (f32[2,32,256]{2,1,0:T(8,128)S(1)}, f32[2,32,256]{2,1,0:T(8,128)S(1)}, u32[]{:S(2)}, u32[]{:S(2)}) collective-permute-start(f32[2,32,256]{2,1,0:T(8,128)S(1)} %collective-permute-done.16.refs_6_), channel_id=1, source_target_pairs={{0,1},{1,0},{2,3},{3,2},{4,5},{5,4},{6,7},{7,6},{8,9},{9,8},{10,11... | collective-permute-start | bytes 196616 | tf_op jit(solution)/shard_map/ppermute | solution.py:18
  56.0 0.7 %collective-permute-start.15 = (f32[2,32,256]{2,1,0:T(8,128)S(1)}, f32[2,32,256]{2,1,0:T(8,128)S(1)}, u32[]{:S(2)}, u32[]{:S(2)}) collective-permute-start(f32[2,32,256]{2,1,0:T(8,128)S(1)} %collective-permute-done.14.refs_4_), channel_id=1, source_target_pairs={{0,1},{1,0},{2,3},{3,2},{4,5},{5,4},{6,7},{7,6},{8,9},{9,8},{10,11... | collective-permute-start | bytes 196616 | tf_op jit(solution)/shard_map/ppermute | solution.py:18
  56.6 1.3 %collective-permute-start.13 = (f32[2,32,256]{2,1,0:T(8,128)S(1)}, f32[2,32,256]{2,1,0:T(8,128)S(1)}, u32[]{:S(2)}, u32[]{:S(2)}) collective-permute-start(f32[2,32,256]{2,1,0:T(8,128)S(1)} %collective-permute-done.12.refs_2_), channel_id=1, source_target_pairs={{0,1},{1,0},{2,3},{3,2},{4,5},{5,4},{6,7},{7,6},{8,9},{9,8},{10,11... | collective-permute-start | bytes 196616 | tf_op jit(solution)/shard_map/ppermute | solution.py:18
  57.9 0.8 %shard_map.23.refs_8_ = f32[2,256,256]{2,1,0:T(8,128)S(1)} custom-call(f32[2,32,256]{2,1,0:T(8,128)S(1)} %collective-permute-done.9.came_ref.refs_0_, f32[2,32,256]{2,1,0:T(8,128)S(1)} %collective-permute-done.18.refs_1_, f32[2,32,256]{2,1,0:T(8,128)S(1)} %collective-permute-done.19.refs_2_, f32[2,32,256]{2,1,0:T(8,128)S(1)} %collective-permute-done.20.refs_3_, ...), custom_call_target="tpu_custom_call" | custom-call | flops 402653184 | bytes 1572864 | tf_op jit(solution)/shard_map/pallas_call | solution.py:59
  58.8 1.4 %shard_map.24 = f32[1,2,256,256]{3,2,1,0:T(8,128)} custom-call(f32[2,32,256]{2,1,0:T(8,128)S(1)} %collective-permute-done.10.refs_0_, f32[2,32,256]{2,1,0:T(8,128)S(1)} %collective-permute-done.11.refs_1_, f32[2,32,256]{2,1,0:T(8,128)S(1)} %collective-permute-done.12.refs_2_, f32[2,32,256]{2,1,0:T(8,128)S(1)} %collective-permute-done.13.refs_3_, ...), custom_call_target="tpu_custom_call" | custom-call | flops 402653184 | bytes 1572864 | tf_op jit(solution)/shard_map/pallas_call | solution.py:59
  (28 shorter events, 1.0 us)
Async XLA Ops:
  0.0 1.0 %copy-start = (f32[1,2,256,256]{3,2,1,0:T(8,128)S(1)}, f32[1,2,256,256]{3,2,1,0:T(8,128)}, u32[]{:S(2)}) copy-start(f32[1,2,256,256]{3,2,1,0:T(8,128)} %drawn_ref.1) | copy-start | bytes 1572868
  1.2 6.7 %collective-permute-start = (f32[256,256]{1,0:T(8,128)S(1)}, f32[256,256]{1,0:T(8,128)S(1)}, u32[]{:S(2)}, u32[]{:S(2)}) collective-permute-start(f32[256,256]{1,0:T(8,128)S(1)} %shard_map.17.first_ref), channel_id=1, source_target_pairs={{0,31},{1,0},{2,1},{3,2},{4,3},{5,4},{6,5},{7,6},{8,7},{9,8},{10,9... | collective-permute-start | bytes 786440 | tf_op jit(solution)/shard_map/ppermute | solution.py:23
  12.0 2.0 %collective-permute-start.1 = (f32[2,256,256]{2,1,0:T(8,128)S(1)}, f32[2,256,256]{2,1,0:T(8,128)S(1)}, u32[]{:S(2)}, u32[]{:S(2)}) collective-permute-start(f32[2,256,256]{2,1,0:T(8,128)S(1)} %shard_map.18.own_ref), channel_id=1, source_target_pairs={{0,1},{1,0},{2,3},{3,2},{4,5},{5,4},{6,7},{7,6},{8,9},{9,8},{10,11... | collective-permute-start | bytes 1572872 | tf_op jit(solution)/shard_map/ppermute | solution.py:18
  14.3 8.7 %collective-permute-start.7 = (f32[2,128,256]{2,1,0:T(8,128)S(1)}, f32[2,128,256]{2,1,0:T(8,128)S(1)}, u32[]{:S(2)}, u32[]{:S(2)}) collective-permute-start(f32[2,128,256]{2,1,0:T(8,128)S(1)} %shard_map.19.refs_0_), channel_id=1, source_target_pairs={{0,6},{1,7},{2,4},{3,5},{4,2},{5,3},{6,0},{7,1},{8,14},{9,15},{10,... | collective-permute-start | bytes 786440 | tf_op jit(solution)/shard_map/ppermute | solution.py:18
  14.8 14.8 %collective-permute-start.5 = (f32[2,128,256]{2,1,0:T(8,128)S(1)}, f32[2,128,256]{2,1,0:T(8,128)S(1)}, u32[]{:S(2)}, u32[]{:S(2)}) collective-permute-start(f32[2,128,256]{2,1,0:T(8,128)S(1)} %shard_map.19.refs_0_), channel_id=1, source_target_pairs={{0,4},{1,5},{2,6},{3,7},{4,0},{5,1},{6,2},{7,3},{8,12},{9,13},{10,... | collective-permute-start | bytes 786440 | tf_op jit(solution)/shard_map/ppermute | solution.py:18
  18.4 13.0 %collective-permute-start.3 = (f32[2,128,256]{2,1,0:T(8,128)S(1)}, f32[2,128,256]{2,1,0:T(8,128)S(1)}, u32[]{:S(2)}, u32[]{:S(2)}) collective-permute-start(f32[2,128,256]{2,1,0:T(8,128)S(1)} %shard_map.19.refs_0_), channel_id=1, source_target_pairs={{0,2},{1,3},{2,0},{3,1},{4,6},{5,7},{6,4},{7,5},{8,10},{9,11},{10,... | collective-permute-start | bytes 786440 | tf_op jit(solution)/shard_map/ppermute | solution.py:18
  19.5 12.9 %collective-permute-start.2 = (f32[2,128,256]{2,1,0:T(8,128)S(1)}, f32[2,128,256]{2,1,0:T(8,128)S(1)}, u32[]{:S(2)}, u32[]{:S(2)}) collective-permute-start(f32[2,128,256]{2,1,0:T(8,128)S(1)} %shard_map.19.refs_0_), channel_id=1, source_target_pairs={{0,1},{1,0},{2,3},{3,2},{4,5},{5,4},{6,7},{7,6},{8,9},{9,8},{10,11... | collective-permute-start | bytes 786440 | tf_op jit(solution)/shard_map/ppermute | solution.py:18
  23.1 9.4 %collective-permute-start.8 = (f32[2,128,256]{2,1,0:T(8,128)S(1)}, f32[2,128,256]{2,1,0:T(8,128)S(1)}, u32[]{:S(2)}, u32[]{:S(2)}) collective-permute-start(f32[2,128,256]{2,1,0:T(8,128)S(1)} %collective-permute-done.7.refs_6_), channel_id=1, source_target_pairs={{0,1},{1,0},{2,3},{3,2},{4,5},{5,4},{6,7},{7,6},{8,9},{9,8},{10,11... | collective-permute-start | bytes 786440 | tf_op jit(solution)/shard_map/ppermute | solution.py:18
  29.6 2.9 %collective-permute-start.6 = (f32[2,128,256]{2,1,0:T(8,128)S(1)}, f32[2,128,256]{2,1,0:T(8,128)S(1)}, u32[]{:S(2)}, u32[]{:S(2)}) collective-permute-start(f32[2,128,256]{2,1,0:T(8,128)S(1)} %collective-permute-done.5.refs_4_), channel_id=1, source_target_pairs={{0,1},{1,0},{2,3},{3,2},{4,5},{5,4},{6,7},{7,6},{8,9},{9,8},{10,11... | collective-permute-start | bytes 786440 | tf_op jit(solution)/shard_map/ppermute | solution.py:18
  31.5 2.2 %collective-permute-start.4 = (f32[2,128,256]{2,1,0:T(8,128)S(1)}, f32[2,128,256]{2,1,0:T(8,128)S(1)}, u32[]{:S(2)}, u32[]{:S(2)}) collective-permute-start(f32[2,128,256]{2,1,0:T(8,128)S(1)} %collective-permute-done.3.refs_2_), channel_id=1, source_target_pairs={{0,1},{1,0},{2,3},{3,2},{4,5},{5,4},{6,7},{7,6},{8,9},{9,8},{10,11... | collective-permute-start | bytes 786440 | tf_op jit(solution)/shard_map/ppermute | solution.py:18
  35.5 3.2 %collective-permute-start.9 = (f32[2,32,256]{2,1,0:T(8,128)S(1)}, f32[2,32,256]{2,1,0:T(8,128)S(1)}, u32[]{:S(2)}, u32[]{:S(2)}) collective-permute-start(f32[2,32,256]{2,1,0:T(8,128)S(1)} %get-tuple-element.10), channel_id=1, source_target_pairs={{0,8},{1,9},{2,10},{3,11},{4,12},{5,13},{6,14},{7,15},{8,0},{9,1},... | collective-permute-start | bytes 196616 | tf_op jit(solution)/shard_map/ppermute | solution.py:18
  38.7 8.0 %collective-permute-start.23 = (f32[2,32,256]{2,1,0:T(8,128)S(1)}, f32[2,32,256]{2,1,0:T(8,128)S(1)}, u32[]{:S(2)}, u32[]{:S(2)}) collective-permute-start(f32[2,32,256]{2,1,0:T(8,128)S(1)} %collective-permute-done.9.came_ref.refs_0_), channel_id=1, source_target_pairs={{0,6},{1,7},{2,4},{3,5},{4,2},{5,3},{6,0},{7,1},{8,14},{9,15},{10,... | collective-permute-start | bytes 196616 | tf_op jit(solution)/shard_map/ppermute | solution.py:18
  40.6 6.1 %collective-permute-start.21 = (f32[2,32,256]{2,1,0:T(8,128)S(1)}, f32[2,32,256]{2,1,0:T(8,128)S(1)}, u32[]{:S(2)}, u32[]{:S(2)}) collective-permute-start(f32[2,32,256]{2,1,0:T(8,128)S(1)} %collective-permute-done.9.came_ref.refs_0_), channel_id=1, source_target_pairs={{0,4},{1,5},{2,6},{3,7},{4,0},{5,1},{6,2},{7,3},{8,12},{9,13},{10,... | collective-permute-start | bytes 196616 | tf_op jit(solution)/shard_map/ppermute | solution.py:18
  42.5 4.8 %collective-permute-start.10 = (f32[2,32,256]{2,1,0:T(8,128)S(1)}, f32[2,32,256]{2,1,0:T(8,128)S(1)}, u32[]{:S(2)}, u32[]{:S(2)}) collective-permute-start(f32[2,32,256]{2,1,0:T(8,128)S(1)} %shard_map.22), channel_id=1, source_target_pairs={{0,16},{1,17},{2,18},{3,19},{4,20},{5,21},{6,22},{7,23},{8,24},{9,... | collective-permute-start | bytes 196616 | tf_op jit(solution)/shard_map/ppermute | solution.py:18
  42.6 7.0 %collective-permute-start.19 = (f32[2,32,256]{2,1,0:T(8,128)S(1)}, f32[2,32,256]{2,1,0:T(8,128)S(1)}, u32[]{:S(2)}, u32[]{:S(2)}) collective-permute-start(f32[2,32,256]{2,1,0:T(8,128)S(1)} %collective-permute-done.9.came_ref.refs_0_), channel_id=1, source_target_pairs={{0,2},{1,3},{2,0},{3,1},{4,6},{5,7},{6,4},{7,5},{8,10},{9,11},{10,... | collective-permute-start | bytes 196616 | tf_op jit(solution)/shard_map/ppermute | solution.py:18
  43.8 6.0 %collective-permute-start.18 = (f32[2,32,256]{2,1,0:T(8,128)S(1)}, f32[2,32,256]{2,1,0:T(8,128)S(1)}, u32[]{:S(2)}, u32[]{:S(2)}) collective-permute-start(f32[2,32,256]{2,1,0:T(8,128)S(1)} %collective-permute-done.9.came_ref.refs_0_), channel_id=1, source_target_pairs={{0,1},{1,0},{2,3},{3,2},{4,5},{5,4},{6,7},{7,6},{8,9},{9,8},{10,11... | collective-permute-start | bytes 196616 | tf_op jit(solution)/shard_map/ppermute | solution.py:18
  46.7 3.3 %collective-permute-start.24 = (f32[2,32,256]{2,1,0:T(8,128)S(1)}, f32[2,32,256]{2,1,0:T(8,128)S(1)}, u32[]{:S(2)}, u32[]{:S(2)}) collective-permute-start(f32[2,32,256]{2,1,0:T(8,128)S(1)} %collective-permute-done.23.refs_6_), channel_id=1, source_target_pairs={{0,1},{1,0},{2,3},{3,2},{4,5},{5,4},{6,7},{7,6},{8,9},{9,8},{10,11... | collective-permute-start | bytes 196616 | tf_op jit(solution)/shard_map/ppermute | solution.py:18
  46.7 7.6 %collective-permute-start.22 = (f32[2,32,256]{2,1,0:T(8,128)S(1)}, f32[2,32,256]{2,1,0:T(8,128)S(1)}, u32[]{:S(2)}, u32[]{:S(2)}) collective-permute-start(f32[2,32,256]{2,1,0:T(8,128)S(1)} %collective-permute-done.21.refs_4_), channel_id=1, source_target_pairs={{0,1},{1,0},{2,3},{3,2},{4,5},{5,4},{6,7},{7,6},{8,9},{9,8},{10,11... | collective-permute-start | bytes 196616 | tf_op jit(solution)/shard_map/ppermute | solution.py:18
  47.3 7.1 %collective-permute-start.16 = (f32[2,32,256]{2,1,0:T(8,128)S(1)}, f32[2,32,256]{2,1,0:T(8,128)S(1)}, u32[]{:S(2)}, u32[]{:S(2)}) collective-permute-start(f32[2,32,256]{2,1,0:T(8,128)S(1)} %collective-permute-done.10.refs_0_), channel_id=1, source_target_pairs={{0,6},{1,7},{2,4},{3,5},{4,2},{5,3},{6,0},{7,1},{8,14},{9,15},{10,... | collective-permute-start | bytes 196616 | tf_op jit(solution)/shard_map/ppermute | solution.py:18
  49.6 6.3 %collective-permute-start.14 = (f32[2,32,256]{2,1,0:T(8,128)S(1)}, f32[2,32,256]{2,1,0:T(8,128)S(1)}, u32[]{:S(2)}, u32[]{:S(2)}) collective-permute-start(f32[2,32,256]{2,1,0:T(8,128)S(1)} %collective-permute-done.10.refs_0_), channel_id=1, source_target_pairs={{0,4},{1,5},{2,6},{3,7},{4,0},{5,1},{6,2},{7,3},{8,12},{9,13},{10,... | collective-permute-start | bytes 196616 | tf_op jit(solution)/shard_map/ppermute | solution.py:18
  49.7 6.9 %collective-permute-start.12 = (f32[2,32,256]{2,1,0:T(8,128)S(1)}, f32[2,32,256]{2,1,0:T(8,128)S(1)}, u32[]{:S(2)}, u32[]{:S(2)}) collective-permute-start(f32[2,32,256]{2,1,0:T(8,128)S(1)} %collective-permute-done.10.refs_0_), channel_id=1, source_target_pairs={{0,2},{1,3},{2,0},{3,1},{4,6},{5,7},{6,4},{7,5},{8,10},{9,11},{10,... | collective-permute-start | bytes 196616 | tf_op jit(solution)/shard_map/ppermute | solution.py:18
  50.0 7.9 %collective-permute-start.20 = (f32[2,32,256]{2,1,0:T(8,128)S(1)}, f32[2,32,256]{2,1,0:T(8,128)S(1)}, u32[]{:S(2)}, u32[]{:S(2)}) collective-permute-start(f32[2,32,256]{2,1,0:T(8,128)S(1)} %collective-permute-done.19.refs_2_), channel_id=1, source_target_pairs={{0,1},{1,0},{2,3},{3,2},{4,5},{5,4},{6,7},{7,6},{8,9},{9,8},{10,11... | collective-permute-start | bytes 196616 | tf_op jit(solution)/shard_map/ppermute | solution.py:18
  54.3 4.4 %collective-permute-start.11 = (f32[2,32,256]{2,1,0:T(8,128)S(1)}, f32[2,32,256]{2,1,0:T(8,128)S(1)}, u32[]{:S(2)}, u32[]{:S(2)}) collective-permute-start(f32[2,32,256]{2,1,0:T(8,128)S(1)} %collective-permute-done.10.refs_0_), channel_id=1, source_target_pairs={{0,1},{1,0},{2,3},{3,2},{4,5},{5,4},{6,7},{7,6},{8,9},{9,8},{10,11... | collective-permute-start | bytes 196616 | tf_op jit(solution)/shard_map/ppermute | solution.py:18
  54.3 4.3 %collective-permute-start.17 = (f32[2,32,256]{2,1,0:T(8,128)S(1)}, f32[2,32,256]{2,1,0:T(8,128)S(1)}, u32[]{:S(2)}, u32[]{:S(2)}) collective-permute-start(f32[2,32,256]{2,1,0:T(8,128)S(1)} %collective-permute-done.16.refs_6_), channel_id=1, source_target_pairs={{0,1},{1,0},{2,3},{3,2},{4,5},{5,4},{6,7},{7,6},{8,9},{9,8},{10,11... | collective-permute-start | bytes 196616 | tf_op jit(solution)/shard_map/ppermute | solution.py:18
  56.0 2.7 %collective-permute-start.15 = (f32[2,32,256]{2,1,0:T(8,128)S(1)}, f32[2,32,256]{2,1,0:T(8,128)S(1)}, u32[]{:S(2)}, u32[]{:S(2)}) collective-permute-start(f32[2,32,256]{2,1,0:T(8,128)S(1)} %collective-permute-done.14.refs_4_), channel_id=1, source_target_pairs={{0,1},{1,0},{2,3},{3,2},{4,5},{5,4},{6,7},{7,6},{8,9},{9,8},{10,11... | collective-permute-start | bytes 196616 | tf_op jit(solution)/shard_map/ppermute | solution.py:18
  56.6 2.2 %collective-permute-start.13 = (f32[2,32,256]{2,1,0:T(8,128)S(1)}, f32[2,32,256]{2,1,0:T(8,128)S(1)}, u32[]{:S(2)}, u32[]{:S(2)}) collective-permute-start(f32[2,32,256]{2,1,0:T(8,128)S(1)} %collective-permute-done.12.refs_2_), channel_id=1, source_target_pairs={{0,1},{1,0},{2,3},{3,2},{4,5},{5,4},{6,7},{7,6},{8,9},{9,8},{10,11... | collective-permute-start | bytes 196616 | tf_op jit(solution)/shard_map/ppermute | solution.py:18

commit v3 on v2

--- a/solution.py
+++ b/solution.py
@@ -20,7 +20,15 @@
 
 def from_next(x, axis):
     size = lax.axis_size(axis)
-    return lax.ppermute(x, axis, [(i, (i - 1) % size) for i in range(size)])
+    target = {i: i - 1 for i in range(1, size)}
+    target[0] = size - plane
+    target[size - plane + 1] = size - 1
+    return lax.ppermute(x, axis, sorted(target.items()))
+
+
+def to_last(x, axis):
+    size = lax.axis_size(axis)
+    return lax.ppermute(x, axis, [(size - plane, size - 1)])
 
 
 def split(x):
@@ -50,7 +58,7 @@
     return by_real[:rows] - by_imag[rows:], by_imag[:rows] + by_real[rows:]
 
 
-def call(kernel, outs, scratch, flops, *args):
+def call(kernel, outs, scratch, flops, *args, aliases={}):
     as_list = isinstance(outs, list)
     shapes = outs if as_list else [outs]
     moved = sum(a.size * a.dtype.itemsize for a in args)
@@ -62,6 +70,7 @@
         in_specs=[vmem] * len(args),
         out_specs=[vmem] * len(shapes) if as_list else vmem,
         scratch_shapes=scratch,
+        input_output_aliases=aliases,
         compiler_params=pltpu.CompilerParams(vmem_limit_bytes=24 * 1024 * 1024),
         cost_estimate=pl.CostEstimate(flops=flops, bytes_accessed=moved, transcendentals=0),
     )(*args)
@@ -92,27 +101,60 @@
     return real, imag
 
 
-def factor_kernel(first_ref, second_ref, factor_ref):
-    first = unpacked(first_ref[...])
-    second = unpacked(second_ref[...])
-    row, col = index_grid(first[0].shape[0])
+def thirds(pair):
+    return split(pair[0]), split(pair[1]), split(pair[0] + pair[1])
+
+
+def three_products(left, right):
+    def real(l, r):
+        return dot(l[0], r[0], False) + (dot(l[0], r[1], False) + dot(l[1], r[0], False))
+
+    ac, bd = real(left[0], right[0]), real(left[1], right[1])
+    return ac - bd, real(left[2], right[2]) - (ac + bd)
+
+
+def prepare_kernel(packed_ref, parts_ref, high_ref, low_ref):
+    pair = unpacked(packed_ref[...])
+    store(parts_ref, pair)
+    for k, (high, low) in enumerate(thirds(pair)):
+        high_ref[k] = high
+        low_ref[k] = low
+
+
+def magnus(parts_ref, high_ref, low_ref, packed, factor_ref):
+    first = parts_ref[0], parts_ref[1]
+    second = unpacked(packed)
+    row, col = index_grid(packed.shape[0])
     identity = jnp.where(row == col, 1.0, 0.0).astype(jnp.float32)
-    both = product(halves(second), halves(first))
+    prepared = [(high_ref[k], low_ref[k]) for k in range(3)]
+    both = three_products(thirds(second), prepared)
     comm_real = both[0] - both[0].T
     comm_imag = both[1] + both[1].T
     shrink = time_step * time_step / 12.0
-    real = 0.5 * time_step * (first[1] + second[1]) - shrink * comm_real
+    real = shrink * comm_real - 0.5 * time_step * (first[1] + second[1])
     imag = -0.5 * time_step * (first[0] + second[0]) - shrink * comm_imag
-    real = -real
-    exponent = halves((real, imag))
+    exponent = thirds((real, imag))
     nested = (identity + real * 0.25, imag * 0.25)
     for order in (3.0, 2.0, 1.0):
-        grown = product(exponent, halves(nested))
+        grown = three_products(thirds(nested), exponent)
         nested = (identity + grown[0] * (1.0 / order), grown[1] * (1.0 / order))
     factor_ref[0] = nested[0]
     factor_ref[1] = nested[1]
 
 
+def factor_kernel(axis, parts_ref, high_ref, low_ref, pair_ref, next_ref, factor_ref):
+    odd = lax.axis_index(axis) & 1
+    magnus(parts_ref, high_ref, low_ref, jnp.where(odd == 0, pair_ref[...], next_ref[...]), factor_ref)
+
+
+def late_kernel(axis, parts_ref, high_ref, low_ref, next_ref, factor_ref):
+    me = lax.axis_index(axis)
+
+    @pl.when(me == lax.axis_size(axis) - 1)
+    def _():
+        magnus(parts_ref, high_ref, low_ref, next_ref[...], factor_ref)
+
+
 def load(ref, rows=slice(None)):
     return ref[0, rows, :], ref[1, rows, :]
 
@@ -122,18 +164,24 @@
     ref[1, rows, :] = pair[1]
 
 
-def chip_kernel(axis, own_ref, other_ref, half_ref):
+def chip_kernel(axis, own_ref, other_ref, half_ref, real_ref, imag_ref):
     odd = lax.axis_index(axis) & 1
     rows = half_ref.shape[1]
     half = pl.ds(pl.multiple_of(odd * rows, rows), rows)
 
+    def put(left, right):
+        pair = product(halves(left), halves(right))
+        store(half_ref, pair)
+        real_ref[...] = pair[0]
+        imag_ref[...] = pair[1]
+
     @pl.when(odd == 0)
     def _():
-        store(half_ref, product(halves(load(own_ref, half)), halves(load(other_ref))))
+        put(load(own_ref, half), load(other_ref))
 
     @pl.when(odd == 1)
     def _():
-        store(half_ref, product(halves(load(other_ref, half)), halves(load(own_ref))))
+        put(load(other_ref, half), load(own_ref))
 
 
 def get(high_ref, low_ref, q, rows=slice(None)):
@@ -143,56 +191,97 @@
     )
 
 
-def picked(pair, chosen):
-    high, low = pair
-    return tuple(
-        dot(chosen, high[k], True) + dot(chosen, low[k], True) for k in range(2)
-    )
-
-
-def one_hot_rows(count, size, begin):
-    row = lax.broadcasted_iota(jnp.int32, (count, size), 0)
-    col = lax.broadcasted_iota(jnp.int32, (count, size), 1)
-    return jnp.where(row + begin == col, 1.0, 0.0).astype(jnp.bfloat16)
-
-
-def gather_kernel(axis, level, *refs):
-    in_refs, (slice_ref, high_ref, low_ref) = refs[:8], refs[8:]
+def get_pair(high_ref, low_ref, rows=slice(None)):
+    return (
+        (high_ref[0, rows, :], high_ref[1, rows, :]),
+        (low_ref[0, rows, :], low_ref[1, rows, :]),
+    )
+
+
+def hold(axis, rel, other, k, piece, high_ref, low_ref):
+    me = lax.axis_index(axis)
+    rows = piece.shape[0]
+    begin = pl.multiple_of(((me & 1) ^ other) * rows, rows)
+    high, low = split(piece)
+    high_ref[((me >> 1) & 3) ^ rel, k, pl.ds(begin, rows), :] = high
+    low_ref[((me >> 1) & 3) ^ rel, k, pl.ds(begin, rows), :] = low
+
+
+def near_kernel(axis, *refs):
+    own, rest, (high_ref, low_ref, row_high_ref, row_low_ref) = refs[:2], refs[2:10], refs[10:]
+    for k in range(2):
+        for other in range(2):
+            hold(axis, 0, other, k, own[other][k], high_ref, low_ref)
+            hold(axis, 1, other, k, rest[2 * k + other][...], high_ref, low_ref)
+            hold(axis, 2, other, k, rest[4 + 2 * k + other][...], high_ref, low_ref)
+    begin = (lax.axis_index(axis) >> 1) & 2
+    grown = product(get(high_ref, low_ref, begin), get(high_ref, low_ref, begin + 1))
+    for k in range(2):
+        row_high_ref[k], row_low_ref[k] = split(grown[k])
+
+
+def core_rows(me, count):
+    return pl.ds(pl.multiple_of((me & 1) * count, count), count)
+
+
+def own_rows(me, count):
+    return pl.ds(pl.multiple_of((me & (parts - 1)) * count, count), count)
+
+
+def own_turned(me, count, columns, room_ref):
+    begin = (me & (parts - 1)) * count
+    width = room_ref.shape[0]
+    block = pl.ds(pl.multiple_of(begin // width * width, width), width)
+    inside = pl.ds(pl.multiple_of(begin % width, count), count)
+    out = []
+    for k in range(2):
+        room_ref[...] = columns(k, block).T
+        out.append(room_ref[inside, :])
+    return out
+
+
+def summed(high, low):
+    return high.astype(jnp.float32) + low.astype(jnp.float32)
+
+
+def total_kernel(axis, level, *refs):
+    pieces, (row_high_ref, row_low_ref) = refs[:4], refs[6:8]
+    slice_ref, high_ref, low_ref, room_ref = refs[8:]
+    for k in range(2):
+        for other in range(2):
+            hold(axis, 3, other, k, pieces[2 * k + other][...], high_ref, low_ref)
+    me = lax.axis_index(axis)
+    rows = own_rows(me, slice_ref.shape[1])
+    upper, second_row = (me // level) & 1, (me >> 2) & 1
+    row = get_pair(row_high_ref, row_low_ref)
+
+    @pl.when((upper == 0) & (second_row == 0))
+    def _():
+        value = product(get_pair(row_high_ref, row_low_ref, rows), get(high_ref, low_ref, 2))
+        store(slice_ref, product(halves(value), get(high_ref, low_ref, 3)))
+
+    @pl.when((upper == 0) & (second_row == 1))
+    def _():
+        value = product(get(high_ref, low_ref, 0, rows), get(high_ref, low_ref, 1))
+        store(slice_ref, product(halves(value), row))
+
+    @pl.when((upper == 1) & (second_row == 1))
+    def _():
+        value = own_turned(me, slice_ref.shape[1], lambda k, c: summed(row_high_ref[k, :, c], row_low_ref[k, :, c]), room_ref)
+        value = product(halves(value), get(high_ref, low_ref, 1), True)
+        store(slice_ref, product(halves(value), get(high_ref, low_ref, 0), True))
+
+    @pl.when((upper == 1) & (second_row == 0))
+    def _():
+        value = own_turned(me, slice_ref.shape[1], lambda k, c: summed(high_ref[3, k, :, c], low_ref[3, k, :, c]), room_ref)
+        value = product(halves(value), get(high_ref, low_ref, 2), True)
+        store(slice_ref, product(halves(value), row, True))
+
+
+def prefix_kernel(axis, high_ref, low_ref, own_ref, other_ref, total_ref, local_ref, half_ref):
     me = lax.axis_index(axis)
     odd, chip = me & 1, (me >> 1) & 3
-    size = high_ref.shape[-1]
-    half = size // 2
-    for rel in range(4):
-        for other in range(2):
-            begin = pl.multiple_of((odd ^ other) * half, half)
-            for k in range(2):
-                high, low = split(in_refs[2 * rel + other][k])
-                high_ref[chip ^ rel, k, pl.ds(begin, half), :] = high
-                low_ref[chip ^ rel, k, pl.ds(begin, half), :] = low
-    count = size // parts
-    begin = pl.multiple_of((me & (parts - 1)) * count, count)
-    upper = (me // level) & 1
-
-    @pl.when(upper == 0)
-    def _():
-        value = get(high_ref, low_ref, 0, pl.ds(begin, count))
-        for q in (1, 2, 3):
-            grown = product(value, get(high_ref, low_ref, q))
-            value = halves(grown)
-        store(slice_ref, grown)
-
-    @pl.when(upper == 1)
-    def _():
-        chosen = one_hot_rows(count, size, begin)
-        grown = picked(get(high_ref, low_ref, 3), chosen)
-        for q in (2, 1, 0):
-            grown = product(halves(grown), get(high_ref, low_ref, q), True)
-        store(slice_ref, grown)
-
-
-def prefix_kernel(axis, high_ref, low_ref, own_ref, total_ref, local_ref):
-    me = lax.axis_index(axis)
-    odd, chip = me & 1, (me >> 1) & 3
+    last = me == lax.axis_size(axis) - 1
     first = get(high_ref, low_ref, 0)
 
     @pl.when((chip == 0) & (odd == 1))
@@ -211,28 +300,36 @@
         def _(value=value):
             store(local_ref, product(value, halves(load(own_ref))))
 
+        if q == 3:
+
+            @pl.when(last)
+            def _(value=value):
+                store(local_ref, product(value, halves(load(other_ref))))
+
         grown = product(value, get(high_ref, low_ref, q))
         store(total_ref, grown)
         value = halves(load(total_ref))
 
-        @pl.when((chip == q) & (odd == 1))
+        @pl.when((chip == q) & (odd == 1) & jnp.logical_not(last))
         def _():
             store(local_ref, load(total_ref))
 
-
-def cut_kernel(axis, level, total_ref, slice_ref):
-    me = lax.axis_index(axis)
-    count, size = slice_ref.shape[1], slice_ref.shape[2]
-    begin = pl.multiple_of((me & (parts - 1)) * count, count)
+    store(half_ref, load(total_ref, core_rows(me, half_ref.shape[1])))
+
+
+def cut_kernel(axis, level, total_ref, slice_ref, half_ref, room_ref):
+    me = lax.axis_index(axis)
+    count = slice_ref.shape[1]
     upper = (me // level) & 1
+    store(half_ref, load(total_ref, core_rows(me, half_ref.shape[1])))
 
     @pl.when(upper == 0)
     def _():
-        store(slice_ref, load(total_ref, pl.ds(begin, count)))
+        store(slice_ref, load(total_ref, own_rows(me, count)))
 
     @pl.when(upper == 1)
     def _():
-        store(slice_ref, picked(halves(load(total_ref)), one_hot_rows(count, size, begin)))
+        store(slice_ref, own_turned(me, count, lambda k, c: total_ref[k, :, c], room_ref))
 
 
 def double_kernel(axis, level, total_ref, local_ref, mine_ref, other_ref, next_total_ref, next_local_ref):
@@ -276,9 +373,11 @@
         store(whole_ref, load(ref), pl.ds(begin, count))
 
 
-def local_kernel(axis, level, *refs):
-    in_refs, local_ref, out_ref, whole_ref = refs[:8], refs[8], refs[9], refs[10]
-    upper = (lax.axis_index(axis) // level) & 1
+def local_kernel(axis, level, mine_ref, twin_ref, local_ref, late_ref, out_ref, whole_ref):
+    me = lax.axis_index(axis)
+    half = mine_ref.shape[1]
+    upper = (me // level) & 1
+    last = me == lax.axis_size(axis) - 1
 
     @pl.when(upper == 0)
     def _():
@@ -287,10 +386,18 @@
 
     @pl.when(upper == 1)
     def _():
-        assemble(axis, in_refs, whole_ref)
-        grown = product(halves(load(whole_ref)), halves(load(local_ref)))
+        store(whole_ref, load(mine_ref), core_rows(me, half))
+        store(whole_ref, load(twin_ref), core_rows(me ^ 1, half))
+        store(whole_ref, product(halves(load(whole_ref)), halves(load(local_ref))))
+
+    @pl.when(last)
+    def _():
+        store(whole_ref, product(halves(load(whole_ref)), halves(load(late_ref))))
+
+    @pl.when(upper == 1)
+    def _():
         for k in range(2):
-            out_ref[k] = grown[k].T
+            out_ref[k] = whole_ref[k].T
 
 
 def final_kernel(axis, level, *refs):
@@ -334,18 +441,59 @@
     strip = f32(2, part, size)
 
     packed = call(pack_kernel, f32(size, size), [], size * size, samples)
-    factor = call(factor_kernel, whole, [], 12 * cube, packed, from_next(packed, axis))
+    near_next = from_next(packed, axis)
+    even_next = exchanged(packed, axis, 1)
+    last_next = to_last(near_next, axis)
+    third_shape = jax.ShapeDtypeStruct((3, size, size), jnp.bfloat16)
+    prepared = call(prepare_kernel, [whole, third_shape, third_shape], [], size * size, packed)
+    factor = call(functools.partial(factor_kernel, axis), whole, [], 9 * cube, *prepared, even_next, near_next)
     other = exchanged(factor, axis, 1)
-    half = call(functools.partial(chip_kernel, axis), f32(2, size // 2, size), [], 3 * cube // 2, factor, other)
-    received = [half] + [exchanged(half, axis, mask) for mask in (2, 4, 6)]
-    pieces = [p for piece in received for p in (piece, exchanged(piece, axis, 1))]
+    quarter = f32(size // 2, size)
+    half, real, imag = call(
+        functools.partial(chip_kernel, axis),
+        [f32(2, size // 2, size), quarter, quarter],
+        [],
+        3 * cube // 2,
+        factor,
+        other,
+    )
+
+    y_real = exchanged(real, axis, 4)
+    x_imag = exchanged(imag, axis, 2)
+    y_imag = exchanged(imag, axis, 4)
+    x_real = exchanged(real, axis, 2)
+    far_real = exchanged(y_real, axis, 2)
+    far_imag = exchanged(x_imag, axis, 4)
+    both = [half, exchanged(half, axis, 1)]
+    for piece in (x_real, x_imag, y_real, y_imag):
+        both += [piece, exchanged(piece, axis, 1)]
+    far = []
+    for piece in (far_real, far_imag):
+        far += [piece, exchanged(piece, axis, 1)]
 
     level = plane
     split_shape = jax.ShapeDtypeStruct((4, 2, size, size), jnp.bfloat16)
+    row_shape = jax.ShapeDtypeStruct((2, size, size), jnp.bfloat16)
+    high, low, row_high, row_low = call(
+        functools.partial(near_kernel, axis), [split_shape, split_shape, row_shape, row_shape], [], 3 * cube, *both
+    )
+    turning = [pltpu.VMEM((128, size), jnp.float32)]
     mine, high, low = call(
-        functools.partial(gather_kernel, axis, level), [strip, split_shape, split_shape], [], cube, *pieces
-    )
-    total, local = call(functools.partial(prefix_kernel, axis), [whole, whole], [], 12 * cube, high, low, factor)
+        functools.partial(total_kernel, axis, level),
+        [strip, split_shape, split_shape],
+        turning,
+        cube,
+        *far,
+        high,
+        low,
+        row_high,
+        row_low,
+        aliases={4: 1, 5: 2},
+    )
+    half_shape = f32(2, size // 2, size)
+    total, local, bulk = call(
+        functools.partial(prefix_kernel, axis), [whole, whole, half_shape], [], 12 * cube, high, low, factor, other
+    )
     if devices > 4 * plane:
         while 4 * level < devices:
             half_of = lax.dynamic_slice_in_dim(total, (lax.axis_index(axis) & 1) * (size // 2), size // 2, 1)
@@ -355,12 +503,15 @@
                 functools.partial(double_kernel, axis, level), [whole, whole], [], 6 * cube, total, local, came, paired
             )
             level = 2 * level
-        mine = call(functools.partial(cut_kernel, axis, level), strip, [], cube, total)
+        mine, bulk = call(functools.partial(cut_kernel, axis, level), [strip, half_shape], turning, cube, total)
     came = exchanged(mine, axis, level)
     step = call(functools.partial(step_kernel, axis, level), strip, [], 3 * cube // parts, came, total)
     below = exchanged(step, axis, 2 * level)
+    came_bulk = exchanged(bulk, axis, level)
+    twin_bulk = exchanged(came_bulk, axis, 1)
     room = [pltpu.VMEM((2, size, size), jnp.float32)]
-    local = call(functools.partial(local_kernel, axis, level), whole, room, 3 * cube, *plane_slices(came, axis), local)
+    late = call(functools.partial(late_kernel, axis), whole, [], cube, *prepared, last_next)
+    local = call(functools.partial(local_kernel, axis, level), whole, room, 3 * cube, came_bulk, twin_bulk, local, late)
     return call(
         functools.partial(final_kernel, axis, level),
         f32(1, 2, size, size),

time: 60.6 us -> 63.1 us (1.041)
  the two profiles are of different devices: /device:TPU:27 before, /device:TPU:31 now
where the time goes in v3:
time: 63.1 us; the launch traced here: 62.9 us
  starting transfers between devices  26.5 us (42%)
  waiting for transfers between devices  23.1 us (37%)
  Pallas kernels  12.2 us (19%)
  local copies, waits for them, and re-layouts  1.04 us (2%)
    ppermute x26, starting transfers between devices, exchanged(): return lax.ppermute(x, axis, [(i, i ^ mask) for i in range(size)])  24.5 us
    ppermute x26, waiting for transfers between devices, exchanged(): return lax.ppermute(x, axis, [(i, i ^ mask) for i in range(size)])  17.9 us
    pallas_call x11, Pallas kernels, call(): pl.pallas_call(kernel, out_shape=outs, in_specs=[vmem] * len(args), out_s...  12.2 us
    ppermute x1, waiting for transfers between devices, from_next(): return lax.ppermute(x, axis, sorted(target.items()))  5.16 us
    ppermute x1, starting transfers between devices, to_last(): return lax.ppermute(x, axis, [(size - plane, size - 1)])  1.28 us
  transfers between devices with their start and end apart: 28, of which 10 were waited for; matrix products, arithmetic and copies ran while one was open for 0% of the time, Pallas kernels for 7%

profile of v3, /device:TPU:31, one launch (start us, length us, event | category | flops | bytes accessed | tf_op | source)
XLA Modules:
  0.0 62.9 jit_solution(8920229446929131396)
XLA Ops:
  0.0 1.0 %copy-done = f32[1,2,256,256]{3,2,1,0:T(8,128)S(1)} copy-done((f32[1,2,256,256]{3,2,1,0:T(8,128)S(1)}, f32[1,2,256,256]{3,2,1,0:T(8,128)}, u32[]{:S(2)}) %copy-start) | copy-done | bytes 524312
  1.2 0.7 %collective-permute-start.1 = (f32[256,256]{1,0:T(8,128)S(1)}, f32[256,256]{1,0:T(8,128)S(1)}, u32[]{:S(2)}, u32[]{:S(2)}) collective-permute-start(f32[256,256]{1,0:T(8,128)S(1)} %shard_map.17.packed_ref), channel_id=1, source_target_pairs={{0,24},{1,0},{2,1},{3,2},{4,3},{5,4},{6,5},{7,6},{8,7},{9,8},{10,9... | collective-permute-start | bytes 786440 | tf_op jit(solution)/shard_map/ppermute | solution.py:26
  2.2 5.2 %collective-permute-done.1.next_ref = f32[256,256]{1,0:T(8,128)S(1)} collective-permute-done((f32[256,256]{1,0:T(8,128)S(1)}, f32[256,256]{1,0:T(8,128)S(1)}, u32[]{:S(2)}, u32[]{:S(2)}) %collective-permute-start.1) | collective-permute-done | bytes 262176 | tf_op jit(solution)/shard_map/ppermute | solution.py:26
  7.4 1.9 %shard_map.19.own_ref = f32[2,256,256]{2,1,0:T(8,128)S(1)} custom-call(f32[2,256,256]{2,1,0:T(8,128)S(1)} %get-tuple-element.21.parts_ref, bf16[3,256,256]{2,1,0:T(8,128)(2,1)S(1)} %get-tuple-element.22.high_ref, bf16[3,256,256]{2,1,0:T(8,128)(2,1)S(1)} %get-tuple-element.23.low_ref, f32[256,256]{1,0:T(8,128)S(1)} %collective-permute-done.pair_ref, ...), custom_call_target="tpu_custom_call" | custom-call | flops 1207959552 | bytes 2359296 | tf_op jit(solution)/shard_map/pallas_call | solution.py:67
  9.4 1.9 %collective-permute-done.2.other_ref = f32[2,256,256]{2,1,0:T(8,128)S(1)} collective-permute-done((f32[2,256,256]{2,1,0:T(8,128)S(1)}, f32[2,256,256]{2,1,0:T(8,128)S(1)}, u32[]{:S(2)}, u32[]{:S(2)}) %collective-permute-start.2) | collective-permute-done | bytes 524320 | tf_op jit(solution)/shard_map/ppermute | solution.py:18
  11.7 2.8 %collective-permute-start.3 = (f32[128,256]{1,0:T(8,128)S(1)}, f32[128,256]{1,0:T(8,128)S(1)}, u32[]{:S(2)}, u32[]{:S(2)}) collective-permute-start(f32[128,256]{1,0:T(8,128)S(1)} %get-tuple-element.24), channel_id=1, source_target_pairs={{0,4},{1,5},{2,6},{3,7},{4,0},{5,1},{6,2},{7,3},{8,12},{9,13},{10,... | collective-permute-start | bytes 393224 | tf_op jit(solution)/shard_map/ppermute | solution.py:18
  14.7 1.9 %collective-permute-done.10.refs_2_ = f32[128,256]{1,0:T(8,128)S(1)} collective-permute-done((f32[128,256]{1,0:T(8,128)S(1)}, f32[128,256]{1,0:T(8,128)S(1)}, u32[]{:S(2)}, u32[]{:S(2)}) %collective-permute-start.10) | collective-permute-done | bytes 131104 | tf_op jit(solution)/shard_map/ppermute | solution.py:18
  16.6 1.0 %collective-permute-start.11 = (f32[128,256]{1,0:T(8,128)S(1)}, f32[128,256]{1,0:T(8,128)S(1)}, u32[]{:S(2)}, u32[]{:S(2)}) collective-permute-start(f32[128,256]{1,0:T(8,128)S(1)} %collective-permute-done.10.refs_2_), channel_id=1, source_target_pairs={{0,1},{1,0},{2,3},{3,2},{4,5},{5,4},{6,7},{7,6},{8,9},{9,8},{10,11... | collective-permute-start | bytes 393224 | tf_op jit(solution)/shard_map/ppermute | solution.py:18
  17.8 2.1 %collective-permute-start.13 = (f32[128,256]{1,0:T(8,128)S(1)}, f32[128,256]{1,0:T(8,128)S(1)}, u32[]{:S(2)}, u32[]{:S(2)}) collective-permute-start(f32[128,256]{1,0:T(8,128)S(1)} %collective-permute-done.3.refs_6_), channel_id=1, source_target_pairs={{0,1},{1,0},{2,3},{3,2},{4,5},{5,4},{6,7},{7,6},{8,9},{9,8},{10,11... | collective-permute-start | bytes 393224 | tf_op jit(solution)/shard_map/ppermute | solution.py:18
  19.9 0.7 %collective-permute-done.14.refs_8_ = f32[128,256]{1,0:T(8,128)S(1)} collective-permute-done((f32[128,256]{1,0:T(8,128)S(1)}, f32[128,256]{1,0:T(8,128)S(1)}, u32[]{:S(2)}, u32[]{:S(2)}) %collective-permute-start.14) | collective-permute-done | bytes 131104 | tf_op jit(solution)/shard_map/ppermute | solution.py:18
  20.6 1.5 %collective-permute-start.7 = (f32[128,256]{1,0:T(8,128)S(1)}, f32[128,256]{1,0:T(8,128)S(1)}, u32[]{:S(2)}, u32[]{:S(2)}) collective-permute-start(f32[128,256]{1,0:T(8,128)S(1)} %collective-permute-done.6.refs_4_), channel_id=1, source_target_pairs={{0,4},{1,5},{2,6},{3,7},{4,0},{5,1},{6,2},{7,3},{8,12},{9,13},{10,... | collective-permute-start | bytes 393224 | tf_op jit(solution)/shard_map/ppermute | solution.py:18
  22.1 1.8 %collective-permute-start.15 = (f32[128,256]{1,0:T(8,128)S(1)}, f32[128,256]{1,0:T(8,128)S(1)}, u32[]{:S(2)}, u32[]{:S(2)}) collective-permute-start(f32[128,256]{1,0:T(8,128)S(1)} %collective-permute-done.14.refs_8_), channel_id=1, source_target_pairs={{0,1},{1,0},{2,3},{3,2},{4,5},{5,4},{6,7},{7,6},{8,9},{9,8},{10,11... | collective-permute-start | bytes 393224 | tf_op jit(solution)/shard_map/ppermute | solution.py:18
  24.4 2.4 %collective-permute-start.5 = (f32[128,256]{1,0:T(8,128)S(1)}, f32[128,256]{1,0:T(8,128)S(1)}, u32[]{:S(2)}, u32[]{:S(2)}) collective-permute-start(f32[128,256]{1,0:T(8,128)S(1)} %collective-permute-done.4.refs_0_), channel_id=1, source_target_pairs={{0,1},{1,0},{2,3},{3,2},{4,5},{5,4},{6,7},{7,6},{8,9},{9,8},{10,11... | collective-permute-start | bytes 393224 | tf_op jit(solution)/shard_map/ppermute | solution.py:18
  27.2 0.8 %shard_map.21 = (bf16[4,2,256,256]{3,2,1,0:T(8,128)(2,1)S(1)}, bf16[4,2,256,256]{3,2,1,0:T(8,128)(2,1)S(1)}, bf16[2,256,256]{2,1,0:T(8,128)(2,1)S(1)}, bf16[2,256,256]{2,1,0:T(8,128)(2,1)S(1)}) custom-call(f32[2,128,256]{2,1,0:T(8,128)S(1)} %get-tuple-element.26.refs_0_, f32[2,128,256]{2,1,0:T(8,128)S(1)} %collective-permute-done.9.refs_1_, ...), custom_call_target="tpu_custom_call" | custom-call | flops 402653184 | bytes 4194304 | tf_op jit(solution)/shard_map/pallas_call | solution.py:67
  28.2 1.1 %shard_map.22 = (f32[2,32,256]{2,1,0:T(8,128)S(1)}, bf16[4,2,256,256]{3,2,1,0:T(8,128)(2,1)S(1)}, bf16[4,2,256,256]{3,2,1,0:T(8,128)(2,1)S(1)}) custom-call(f32[128,256]{1,0:T(8,128)S(1)} %collective-permute-done.4.refs_0_, f32[128,256]{1,0:T(8,128)S(1)} %collective-permute-done.5.refs_1_, ...), custom_call_target="tpu_custom_call", output_to_operand_aliasing={{1}: (4, {}), {2}: (5, {})} | custom-call | flops 134217728 | bytes 5308416 | tf_op jit(solution)/shard_map/pallas_call | solution.py:67
  29.3 2.4 %shard_map.23 = (f32[2,256,256]{2,1,0:T(8,128)S(1)}, f32[2,256,256]{2,1,0:T(8,128)S(1)}, f32[2,128,256]{2,1,0:T(8,128)S(1)}) custom-call(bf16[4,2,256,256]{3,2,1,0:T(8,128)(2,1)S(1)} %get-tuple-element.32.high_ref, bf16[4,2,256,256]{3,2,1,0:T(8,128)(2,1)S(1)} %get-tuple-element.33.low_ref, f32[2,256,256]{2,1,0:T(8,128)S(1)} %shard_map.19.own_ref, ...), custom_call_target="tpu_custom_call" | custom-call | flops 1610612736 | bytes 4456448 | tf_op jit(solution)/shard_map/pallas_call | solution.py:67
  31.7 0.8 %collective-permute-start.25 = (f32[2,128,256]{2,1,0:T(8,128)S(1)}, f32[2,128,256]{2,1,0:T(8,128)S(1)}, u32[]{:S(2)}, u32[]{:S(2)}) collective-permute-start(f32[2,128,256]{2,1,0:T(8,128)S(1)} %get-tuple-element.35), channel_id=1, source_target_pairs={{0,8},{1,9},{2,10},{3,11},{4,12},{5,13},{6,14},{7,15},{8,0},{9,1},... | collective-permute-start | bytes 786440 | tf_op jit(solution)/shard_map/ppermute | solution.py:18
  32.5 1.3 %collective-permute-start.27 = (f32[256,256]{1,0:T(8,128)S(1)}, f32[256,256]{1,0:T(8,128)S(1)}, u32[]{:S(2)}, u32[]{:S(2)}) collective-permute-start(f32[256,256]{1,0:T(8,128)S(1)} %collective-permute-done.1.next_ref), channel_id=1, source_target_pairs={{24,31}} | collective-permute-start | bytes 786440 | tf_op jit(solution)/shard_map/ppermute | solution.py:31
  33.8 5.5 %collective-permute-done.25.mine_ref = f32[2,128,256]{2,1,0:T(8,128)S(1)} collective-permute-done((f32[2,128,256]{2,1,0:T(8,128)S(1)}, f32[2,128,256]{2,1,0:T(8,128)S(1)}, u32[]{:S(2)}, u32[]{:S(2)}) %collective-permute-start.25) | collective-permute-done | bytes 262176 | tf_op jit(solution)/shard_map/ppermute | solution.py:18
  39.3 1.2 %collective-permute-start.26 = (f32[2,128,256]{2,1,0:T(8,128)S(1)}, f32[2,128,256]{2,1,0:T(8,128)S(1)}, u32[]{:S(2)}, u32[]{:S(2)}) collective-permute-start(f32[2,128,256]{2,1,0:T(8,128)S(1)} %collective-permute-done.25.mine_ref), channel_id=1, source_target_pairs={{0,1},{1,0},{2,3},{3,2},{4,5},{5,4},{6,7},{7,6},{8,9},{9,8},{10,11... | collective-permute-start | bytes 786440 | tf_op jit(solution)/shard_map/ppermute | solution.py:18
  40.5 0.7 %collective-permute-start.16 = (f32[2,32,256]{2,1,0:T(8,128)S(1)}, f32[2,32,256]{2,1,0:T(8,128)S(1)}, u32[]{:S(2)}, u32[]{:S(2)}) collective-permute-start(f32[2,32,256]{2,1,0:T(8,128)S(1)} %get-tuple-element.31), channel_id=1, source_target_pairs={{0,8},{1,9},{2,10},{3,11},{4,12},{5,13},{6,14},{7,15},{8,0},{9,1},... | collective-permute-start | bytes 196616 | tf_op jit(solution)/shard_map/ppermute | solution.py:18
  41.2 3.0 %collective-permute-done.16.came_ref = f32[2,32,256]{2,1,0:T(8,128)S(1)} collective-permute-done((f32[2,32,256]{2,1,0:T(8,128)S(1)}, f32[2,32,256]{2,1,0:T(8,128)S(1)}, u32[]{:S(2)}, u32[]{:S(2)}) %collective-permute-start.16) | collective-permute-done | bytes 65568 | tf_op jit(solution)/shard_map/ppermute | solution.py:18
  44.5 1.0 %collective-permute-start.17 = (f32[2,32,256]{2,1,0:T(8,128)S(1)}, f32[2,32,256]{2,1,0:T(8,128)S(1)}, u32[]{:S(2)}, u32[]{:S(2)}) collective-permute-start(f32[2,32,256]{2,1,0:T(8,128)S(1)} %shard_map.24), channel_id=1, source_target_pairs={{0,16},{1,17},{2,18},{3,19},{4,20},{5,21},{6,22},{7,23},{8,24},{9,... | collective-permute-start | bytes 196616 | tf_op jit(solution)/shard_map/ppermute | solution.py:18
  45.6 4.1 %collective-permute-done.17.refs_0_ = f32[2,32,256]{2,1,0:T(8,128)S(1)} collective-permute-done((f32[2,32,256]{2,1,0:T(8,128)S(1)}, f32[2,32,256]{2,1,0:T(8,128)S(1)}, u32[]{:S(2)}, u32[]{:S(2)}) %collective-permute-start.17) | collective-permute-done | bytes 65568 | tf_op jit(solution)/shard_map/ppermute | solution.py:18
  49.7 1.5 %collective-permute-start.23 = (f32[2,32,256]{2,1,0:T(8,128)S(1)}, f32[2,32,256]{2,1,0:T(8,128)S(1)}, u32[]{:S(2)}, u32[]{:S(2)}) collective-permute-start(f32[2,32,256]{2,1,0:T(8,128)S(1)} %collective-permute-done.17.refs_0_), channel_id=1, source_target_pairs={{0,6},{1,7},{2,4},{3,5},{4,2},{5,3},{6,0},{7,1},{8,14},{9,15},{10,... | collective-permute-start | bytes 196616 | tf_op jit(solution)/shard_map/ppermute | solution.py:18
  51.2 1.2 %collective-permute-start.19 = (f32[2,32,256]{2,1,0:T(8,128)S(1)}, f32[2,32,256]{2,1,0:T(8,128)S(1)}, u32[]{:S(2)}, u32[]{:S(2)}) collective-permute-start(f32[2,32,256]{2,1,0:T(8,128)S(1)} %collective-permute-done.17.refs_0_), channel_id=1, source_target_pairs={{0,2},{1,3},{2,0},{3,1},{4,6},{5,7},{6,4},{7,5},{8,10},{9,11},{10,... | collective-permute-start | bytes 196616 | tf_op jit(solution)/shard_map/ppermute | solution.py:18
  52.3 2.6 %collective-permute-start.18 = (f32[2,32,256]{2,1,0:T(8,128)S(1)}, f32[2,32,256]{2,1,0:T(8,128)S(1)}, u32[]{:S(2)}, u32[]{:S(2)}) collective-permute-start(f32[2,32,256]{2,1,0:T(8,128)S(1)} %collective-permute-done.17.refs_0_), channel_id=1, source_target_pairs={{0,1},{1,0},{2,3},{3,2},{4,5},{5,4},{6,7},{7,6},{8,9},{9,8},{10,11... | collective-permute-start | bytes 196616 | tf_op jit(solution)/shard_map/ppermute | solution.py:18
  54.9 2.0 %collective-permute-start.24 = (f32[2,32,256]{2,1,0:T(8,128)S(1)}, f32[2,32,256]{2,1,0:T(8,128)S(1)}, u32[]{:S(2)}, u32[]{:S(2)}) collective-permute-start(f32[2,32,256]{2,1,0:T(8,128)S(1)} %collective-permute-done.23.refs_6_), channel_id=1, source_target_pairs={{0,1},{1,0},{2,3},{3,2},{4,5},{5,4},{6,7},{7,6},{8,9},{9,8},{10,11... | collective-permute-start | bytes 196616 | tf_op jit(solution)/shard_map/ppermute | solution.py:18
  56.8 0.9 %collective-permute-start.22 = (f32[2,32,256]{2,1,0:T(8,128)S(1)}, f32[2,32,256]{2,1,0:T(8,128)S(1)}, u32[]{:S(2)}, u32[]{:S(2)}) collective-permute-start(f32[2,32,256]{2,1,0:T(8,128)S(1)} %collective-permute-done.21.refs_4_), channel_id=1, source_target_pairs={{0,1},{1,0},{2,3},{3,2},{4,5},{5,4},{6,7},{7,6},{8,9},{9,8},{10,11... | collective-permute-start | bytes 196616 | tf_op jit(solution)/shard_map/ppermute | solution.py:18
  58.0 1.9 %shard_map.25.late_ref = f32[2,256,256]{2,1,0:T(8,128)S(1)} custom-call(f32[2,256,256]{2,1,0:T(8,128)S(1)} %get-tuple-element.21.parts_ref, bf16[3,256,256]{2,1,0:T(8,128)(2,1)S(1)} %get-tuple-element.22.high_ref, bf16[3,256,256]{2,1,0:T(8,128)(2,1)S(1)} %get-tuple-element.23.low_ref, f32[256,256]{1,0:T(8,128)S(1)} %collective-permute-done.27.next_ref), custom_call_target="tpu_custom_call" | custom-call | flops 134217728 | bytes 2097152 | tf_op jit(solution)/shard_map/pallas_call | solution.py:67
  60.0 1.4 %shard_map.26.refs_8_ = f32[2,256,256]{2,1,0:T(8,128)S(1)} custom-call(f32[2,128,256]{2,1,0:T(8,128)S(1)} %collective-permute-done.25.mine_ref, f32[2,128,256]{2,1,0:T(8,128)S(1)} %collective-permute-done.26.twin_ref, f32[2,256,256]{2,1,0:T(8,128)S(1)} %get-tuple-element.36.local_ref, f32[2,256,256]{2,1,0:T(8,128)S(1)} %shard_map.25.late_ref), custom_call_target="tpu_custom_call" | custom-call | flops 402653184 | bytes 2097152 | tf_op jit(solution)/shard_map/pallas_call | solution.py:67
  61.5 1.5 %shard_map.27 = f32[1,2,256,256]{3,2,1,0:T(8,128)} custom-call(f32[2,32,256]{2,1,0:T(8,128)S(1)} %collective-permute-done.17.refs_0_, f32[2,32,256]{2,1,0:T(8,128)S(1)} %collective-permute-done.18.refs_1_, f32[2,32,256]{2,1,0:T(8,128)S(1)} %collective-permute-done.19.refs_2_, f32[2,32,256]{2,1,0:T(8,128)S(1)} %collective-permute-done.20.refs_3_, ...), custom_call_target="tpu_custom_call" | custom-call | flops 402653184 | bytes 1572864 | tf_op jit(solution)/shard_map/pallas_call | solution.py:67
  (37 shorter events, 2.9 us)
Async XLA Ops:
  0.0 1.0 %copy-start = (f32[1,2,256,256]{3,2,1,0:T(8,128)S(1)}, f32[1,2,256,256]{3,2,1,0:T(8,128)}, u32[]{:S(2)}) copy-start(f32[1,2,256,256]{3,2,1,0:T(8,128)} %drawn_ref.1) | copy-start | bytes 1572868
  1.2 6.2 %collective-permute-start.1 = (f32[256,256]{1,0:T(8,128)S(1)}, f32[256,256]{1,0:T(8,128)S(1)}, u32[]{:S(2)}, u32[]{:S(2)}) collective-permute-start(f32[256,256]{1,0:T(8,128)S(1)} %shard_map.17.packed_ref), channel_id=1, source_target_pairs={{0,24},{1,0},{2,1},{3,2},{4,3},{5,4},{6,5},{7,6},{8,7},{9,8},{10,9... | collective-permute-start | bytes 786440 | tf_op jit(solution)/shard_map/ppermute | solution.py:26
  1.9 5.4 %collective-permute-start = (f32[256,256]{1,0:T(8,128)S(1)}, f32[256,256]{1,0:T(8,128)S(1)}, u32[]{:S(2)}, u32[]{:S(2)}) collective-permute-start(f32[256,256]{1,0:T(8,128)S(1)} %shard_map.17.packed_ref), channel_id=1, source_target_pairs={{0,1},{1,0},{2,3},{3,2},{4,5},{5,4},{6,7},{7,6},{8,9},{9,8},{10,11... | collective-permute-start | bytes 786440 | tf_op jit(solution)/shard_map/ppermute | solution.py:18
  9.3 2.0 %collective-permute-start.2 = (f32[2,256,256]{2,1,0:T(8,128)S(1)}, f32[2,256,256]{2,1,0:T(8,128)S(1)}, u32[]{:S(2)}, u32[]{:S(2)}) collective-permute-start(f32[2,256,256]{2,1,0:T(8,128)S(1)} %shard_map.19.own_ref), channel_id=1, source_target_pairs={{0,1},{1,0},{2,3},{3,2},{4,5},{5,4},{6,7},{7,6},{8,9},{9,8},{10,11... | collective-permute-start | bytes 1572872 | tf_op jit(solution)/shard_map/ppermute | solution.py:18
  11.7 5.0 %collective-permute-start.10 = (f32[128,256]{1,0:T(8,128)S(1)}, f32[128,256]{1,0:T(8,128)S(1)}, u32[]{:S(2)}, u32[]{:S(2)}) collective-permute-start(f32[128,256]{1,0:T(8,128)S(1)} %get-tuple-element.24), channel_id=1, source_target_pairs={{0,2},{1,3},{2,0},{3,1},{4,6},{5,7},{6,4},{7,5},{8,10},{9,11},{10,... | collective-permute-start | bytes 393224 | tf_op jit(solution)/shard_map/ppermute | solution.py:18
  11.7 6.0 %collective-permute-start.3 = (f32[128,256]{1,0:T(8,128)S(1)}, f32[128,256]{1,0:T(8,128)S(1)}, u32[]{:S(2)}, u32[]{:S(2)}) collective-permute-start(f32[128,256]{1,0:T(8,128)S(1)} %get-tuple-element.24), channel_id=1, source_target_pairs={{0,4},{1,5},{2,6},{3,7},{4,0},{5,1},{6,2},{7,3},{8,12},{9,13},{10,... | collective-permute-start | bytes 393224 | tf_op jit(solution)/shard_map/ppermute | solution.py:18
  14.6 6.0 %collective-permute-start.14 = (f32[128,256]{1,0:T(8,128)S(1)}, f32[128,256]{1,0:T(8,128)S(1)}, u32[]{:S(2)}, u32[]{:S(2)}) collective-permute-start(f32[128,256]{1,0:T(8,128)S(1)} %get-tuple-element.25), channel_id=1, source_target_pairs={{0,4},{1,5},{2,6},{3,7},{4,0},{5,1},{6,2},{7,3},{8,12},{9,13},{10,... | collective-permute-start | bytes 393224 | tf_op jit(solution)/shard_map/ppermute | solution.py:18
  14.6 6.1 %collective-permute-start.6 = (f32[128,256]{1,0:T(8,128)S(1)}, f32[128,256]{1,0:T(8,128)S(1)}, u32[]{:S(2)}, u32[]{:S(2)}) collective-permute-start(f32[128,256]{1,0:T(8,128)S(1)} %get-tuple-element.25), channel_id=1, source_target_pairs={{0,2},{1,3},{2,0},{3,1},{4,6},{5,7},{6,4},{7,5},{8,10},{9,11},{10,... | collective-permute-start | bytes 393224 | tf_op jit(solution)/shard_map/ppermute | solution.py:18
  16.6 5.5 %collective-permute-start.11 = (f32[128,256]{1,0:T(8,128)S(1)}, f32[128,256]{1,0:T(8,128)S(1)}, u32[]{:S(2)}, u32[]{:S(2)}) collective-permute-start(f32[128,256]{1,0:T(8,128)S(1)} %collective-permute-done.10.refs_2_), channel_id=1, source_target_pairs={{0,1},{1,0},{2,3},{3,2},{4,5},{5,4},{6,7},{7,6},{8,9},{9,8},{10,11... | collective-permute-start | bytes 393224 | tf_op jit(solution)/shard_map/ppermute | solution.py:18
  17.8 6.2 %collective-permute-start.13 = (f32[128,256]{1,0:T(8,128)S(1)}, f32[128,256]{1,0:T(8,128)S(1)}, u32[]{:S(2)}, u32[]{:S(2)}) collective-permute-start(f32[128,256]{1,0:T(8,128)S(1)} %collective-permute-done.3.refs_6_), channel_id=1, source_target_pairs={{0,1},{1,0},{2,3},{3,2},{4,5},{5,4},{6,7},{7,6},{8,9},{9,8},{10,11... | collective-permute-start | bytes 393224 | tf_op jit(solution)/shard_map/ppermute | solution.py:18
  19.9 7.3 %collective-permute-start.9 = (f32[2,128,256]{2,1,0:T(8,128)S(1)}, f32[2,128,256]{2,1,0:T(8,128)S(1)}, u32[]{:S(2)}, u32[]{:S(2)}) collective-permute-start(f32[2,128,256]{2,1,0:T(8,128)S(1)} %get-tuple-element.26.refs_0_), channel_id=1, source_target_pairs={{0,1},{1,0},{2,3},{3,2},{4,5},{5,4},{6,7},{7,6},{8,9},{9,8},{10,11... | collective-permute-start | bytes 786440 | tf_op jit(solution)/shard_map/ppermute | solution.py:18
  20.6 3.8 %collective-permute-start.4 = (f32[128,256]{1,0:T(8,128)S(1)}, f32[128,256]{1,0:T(8,128)S(1)}, u32[]{:S(2)}, u32[]{:S(2)}) collective-permute-start(f32[128,256]{1,0:T(8,128)S(1)} %collective-permute-done.3.refs_6_), channel_id=1, source_target_pairs={{0,2},{1,3},{2,0},{3,1},{4,6},{5,7},{6,4},{7,5},{8,10},{9,11},{10,... | collective-permute-start | bytes 393224 | tf_op jit(solution)/shard_map/ppermute | solution.py:18
  20.6 6.2 %collective-permute-start.7 = (f32[128,256]{1,0:T(8,128)S(1)}, f32[128,256]{1,0:T(8,128)S(1)}, u32[]{:S(2)}, u32[]{:S(2)}) collective-permute-start(f32[128,256]{1,0:T(8,128)S(1)} %collective-permute-done.6.refs_4_), channel_id=1, source_target_pairs={{0,4},{1,5},{2,6},{3,7},{4,0},{5,1},{6,2},{7,3},{8,12},{9,13},{10,... | collective-permute-start | bytes 393224 | tf_op jit(solution)/shard_map/ppermute | solution.py:18
  22.1 5.0 %collective-permute-start.15 = (f32[128,256]{1,0:T(8,128)S(1)}, f32[128,256]{1,0:T(8,128)S(1)}, u32[]{:S(2)}, u32[]{:S(2)}) collective-permute-start(f32[128,256]{1,0:T(8,128)S(1)} %collective-permute-done.14.refs_8_), channel_id=1, source_target_pairs={{0,1},{1,0},{2,3},{3,2},{4,5},{5,4},{6,7},{7,6},{8,9},{9,8},{10,11... | collective-permute-start | bytes 393224 | tf_op jit(solution)/shard_map/ppermute | solution.py:18
  23.9 3.2 %collective-permute-start.12 = (f32[128,256]{1,0:T(8,128)S(1)}, f32[128,256]{1,0:T(8,128)S(1)}, u32[]{:S(2)}, u32[]{:S(2)}) collective-permute-start(f32[128,256]{1,0:T(8,128)S(1)} %collective-permute-done.6.refs_4_), channel_id=1, source_target_pairs={{0,1},{1,0},{2,3},{3,2},{4,5},{5,4},{6,7},{7,6},{8,9},{9,8},{10,11... | collective-permute-start | bytes 393224 | tf_op jit(solution)/shard_map/ppermute | solution.py:18
  24.4 3.6 %collective-permute-start.5 = (f32[128,256]{1,0:T(8,128)S(1)}, f32[128,256]{1,0:T(8,128)S(1)}, u32[]{:S(2)}, u32[]{:S(2)}) collective-permute-start(f32[128,256]{1,0:T(8,128)S(1)} %collective-permute-done.4.refs_0_), channel_id=1, source_target_pairs={{0,1},{1,0},{2,3},{3,2},{4,5},{5,4},{6,7},{7,6},{8,9},{9,8},{10,11... | collective-permute-start | bytes 393224 | tf_op jit(solution)/shard_map/ppermute | solution.py:18
  26.8 1.4 %collective-permute-start.8 = (f32[128,256]{1,0:T(8,128)S(1)}, f32[128,256]{1,0:T(8,128)S(1)}, u32[]{:S(2)}, u32[]{:S(2)}) collective-permute-start(f32[128,256]{1,0:T(8,128)S(1)} %collective-permute-done.7.refs_2_), channel_id=1, source_target_pairs={{0,1},{1,0},{2,3},{3,2},{4,5},{5,4},{6,7},{7,6},{8,9},{9,8},{10,11... | collective-permute-start | bytes 393224 | tf_op jit(solution)/shard_map/ppermute | solution.py:18
  31.7 7.6 %collective-permute-start.25 = (f32[2,128,256]{2,1,0:T(8,128)S(1)}, f32[2,128,256]{2,1,0:T(8,128)S(1)}, u32[]{:S(2)}, u32[]{:S(2)}) collective-permute-start(f32[2,128,256]{2,1,0:T(8,128)S(1)} %get-tuple-element.35), channel_id=1, source_target_pairs={{0,8},{1,9},{2,10},{3,11},{4,12},{5,13},{6,14},{7,15},{8,0},{9,1},... | collective-permute-start | bytes 786440 | tf_op jit(solution)/shard_map/ppermute | solution.py:18
  32.5 19.8 %collective-permute-start.27 = (f32[256,256]{1,0:T(8,128)S(1)}, f32[256,256]{1,0:T(8,128)S(1)}, u32[]{:S(2)}, u32[]{:S(2)}) collective-permute-start(f32[256,256]{1,0:T(8,128)S(1)} %collective-permute-done.1.next_ref), channel_id=1, source_target_pairs={{24,31}} | collective-permute-start | bytes 786440 | tf_op jit(solution)/shard_map/ppermute | solution.py:31
  39.3 20.7 %collective-permute-start.26 = (f32[2,128,256]{2,1,0:T(8,128)S(1)}, f32[2,128,256]{2,1,0:T(8,128)S(1)}, u32[]{:S(2)}, u32[]{:S(2)}) collective-permute-start(f32[2,128,256]{2,1,0:T(8,128)S(1)} %collective-permute-done.25.mine_ref), channel_id=1, source_target_pairs={{0,1},{1,0},{2,3},{3,2},{4,5},{5,4},{6,7},{7,6},{8,9},{9,8},{10,11... | collective-permute-start | bytes 786440 | tf_op jit(solution)/shard_map/ppermute | solution.py:18
  40.5 3.6 %collective-permute-start.16 = (f32[2,32,256]{2,1,0:T(8,128)S(1)}, f32[2,32,256]{2,1,0:T(8,128)S(1)}, u32[]{:S(2)}, u32[]{:S(2)}) collective-permute-start(f32[2,32,256]{2,1,0:T(8,128)S(1)} %get-tuple-element.31), channel_id=1, source_target_pairs={{0,8},{1,9},{2,10},{3,11},{4,12},{5,13},{6,14},{7,15},{8,0},{9,1},... | collective-permute-start | bytes 196616 | tf_op jit(solution)/shard_map/ppermute | solution.py:18
  44.5 5.2 %collective-permute-start.17 = (f32[2,32,256]{2,1,0:T(8,128)S(1)}, f32[2,32,256]{2,1,0:T(8,128)S(1)}, u32[]{:S(2)}, u32[]{:S(2)}) collective-permute-start(f32[2,32,256]{2,1,0:T(8,128)S(1)} %shard_map.24), channel_id=1, source_target_pairs={{0,16},{1,17},{2,18},{3,19},{4,20},{5,21},{6,22},{7,23},{8,24},{9,... | collective-permute-start | bytes 196616 | tf_op jit(solution)/shard_map/ppermute | solution.py:18
  49.7 5.2 %collective-permute-start.23 = (f32[2,32,256]{2,1,0:T(8,128)S(1)}, f32[2,32,256]{2,1,0:T(8,128)S(1)}, u32[]{:S(2)}, u32[]{:S(2)}) collective-permute-start(f32[2,32,256]{2,1,0:T(8,128)S(1)} %collective-permute-done.17.refs_0_), channel_id=1, source_target_pairs={{0,6},{1,7},{2,4},{3,5},{4,2},{5,3},{6,0},{7,1},{8,14},{9,15},{10,... | collective-permute-start | bytes 196616 | tf_op jit(solution)/shard_map/ppermute | solution.py:18
  51.2 5.7 %collective-permute-start.21 = (f32[2,32,256]{2,1,0:T(8,128)S(1)}, f32[2,32,256]{2,1,0:T(8,128)S(1)}, u32[]{:S(2)}, u32[]{:S(2)}) collective-permute-start(f32[2,32,256]{2,1,0:T(8,128)S(1)} %collective-permute-done.17.refs_0_), channel_id=1, source_target_pairs={{0,4},{1,5},{2,6},{3,7},{4,0},{5,1},{6,2},{7,3},{8,12},{9,13},{10,... | collective-permute-start | bytes 196616 | tf_op jit(solution)/shard_map/ppermute | solution.py:18
  51.2 6.6 %collective-permute-start.19 = (f32[2,32,256]{2,1,0:T(8,128)S(1)}, f32[2,32,256]{2,1,0:T(8,128)S(1)}, u32[]{:S(2)}, u32[]{:S(2)}) collective-permute-start(f32[2,32,256]{2,1,0:T(8,128)S(1)} %collective-permute-done.17.refs_0_), channel_id=1, source_target_pairs={{0,2},{1,3},{2,0},{3,1},{4,6},{5,7},{6,4},{7,5},{8,10},{9,11},{10,... | collective-permute-start | bytes 196616 | tf_op jit(solution)/shard_map/ppermute | solution.py:18
  52.3 9.1 %collective-permute-start.18 = (f32[2,32,256]{2,1,0:T(8,128)S(1)}, f32[2,32,256]{2,1,0:T(8,128)S(1)}, u32[]{:S(2)}, u32[]{:S(2)}) collective-permute-start(f32[2,32,256]{2,1,0:T(8,128)S(1)} %collective-permute-done.17.refs_0_), channel_id=1, source_target_pairs={{0,1},{1,0},{2,3},{3,2},{4,5},{5,4},{6,7},{7,6},{8,9},{9,8},{10,11... | collective-permute-start | bytes 196616 | tf_op jit(solution)/shard_map/ppermute | solution.py:18
  54.9 6.5 %collective-permute-start.24 = (f32[2,32,256]{2,1,0:T(8,128)S(1)}, f32[2,32,256]{2,1,0:T(8,128)S(1)}, u32[]{:S(2)}, u32[]{:S(2)}) collective-permute-start(f32[2,32,256]{2,1,0:T(8,128)S(1)} %collective-permute-done.23.refs_6_), channel_id=1, source_target_pairs={{0,1},{1,0},{2,3},{3,2},{4,5},{5,4},{6,7},{7,6},{8,9},{9,8},{10,11... | collective-permute-start | bytes 196616 | tf_op jit(solution)/shard_map/ppermute | solution.py:18
  56.8 4.6 %collective-permute-start.22 = (f32[2,32,256]{2,1,0:T(8,128)S(1)}, f32[2,32,256]{2,1,0:T(8,128)S(1)}, u32[]{:S(2)}, u32[]{:S(2)}) collective-permute-start(f32[2,32,256]{2,1,0:T(8,128)S(1)} %collective-permute-done.21.refs_4_), channel_id=1, source_target_pairs={{0,1},{1,0},{2,3},{3,2},{4,5},{5,4},{6,7},{7,6},{8,9},{9,8},{10,11... | collective-permute-start | bytes 196616 | tf_op jit(solution)/shard_map/ppermute | solution.py:18
  57.8 3.7 %collective-permute-start.20 = (f32[2,32,256]{2,1,0:T(8,128)S(1)}, f32[2,32,256]{2,1,0:T(8,128)S(1)}, u32[]{:S(2)}, u32[]{:S(2)}) collective-permute-start(f32[2,32,256]{2,1,0:T(8,128)S(1)} %collective-permute-done.19.refs_2_), channel_id=1, source_target_pairs={{0,1},{1,0},{2,3},{3,2},{4,5},{5,4},{6,7},{7,6},{8,9},{9,8},{10,11... | collective-permute-start | bytes 196616 | tf_op jit(solution)/shard_map/ppermute | solution.py:18

commit v4 on v3

--- a/solution.py
+++ b/solution.py
@@ -16,6 +16,16 @@
 def exchanged(x, axis, mask):
     size = lax.axis_size(axis)
     return lax.ppermute(x, axis, [(i, i ^ mask) for i in range(size)])
+
+
+def lower_exchanged(x, axis, level):
+    size = lax.axis_size(axis)
+    return lax.ppermute(x, axis, [(i, i ^ (level if (i // level) & 2 == 0 else 1)) for i in range(size)])
+
+
+def upper_exchanged(x, axis, level, mask):
+    size = lax.axis_size(axis)
+    return lax.ppermute(x, axis, [(i, i ^ (mask if (i // level) & 2 else 1)) for i in range(size)])
 
 
 def from_next(x, axis):
@@ -58,17 +68,17 @@
     return by_real[:rows] - by_imag[rows:], by_imag[:rows] + by_real[rows:]
 
 
-def call(kernel, outs, scratch, flops, *args, aliases={}):
-    as_list = isinstance(outs, list)
-    shapes = outs if as_list else [outs]
+def call(kernel, outs, scratch, flops, *args, aliases={}, places=None, out_places=None):
+    shapes = outs if isinstance(outs, list) else [outs]
     moved = sum(a.size * a.dtype.itemsize for a in args)
     moved += sum(s.size * s.dtype.itemsize for s in shapes)
-    vmem = pl.BlockSpec(memory_space=pltpu.VMEM)
+    in_specs = [pl.BlockSpec(memory_space=p) for p in places or (pltpu.VMEM,) * len(args)]
+    out_specs = [pl.BlockSpec(memory_space=p) for p in out_places or (pltpu.VMEM,) * len(shapes)]
     return pl.pallas_call(
         kernel,
         out_shape=outs,
-        in_specs=[vmem] * len(args),
-        out_specs=[vmem] * len(shapes) if as_list else vmem,
+        in_specs=in_specs,
+        out_specs=out_specs if isinstance(outs, list) else out_specs[0],
         scratch_shapes=scratch,
         input_output_aliases=aliases,
         compiler_params=pltpu.CompilerParams(vmem_limit_bytes=24 * 1024 * 1024),
@@ -365,70 +375,93 @@
         store(slice_ref, product(came, total))
 
 
-def assemble(axis, in_refs, whole_ref):
-    me = lax.axis_index(axis) & (parts - 1)
-    count = in_refs[0].shape[1]
-    for k, ref in enumerate(in_refs):
-        begin = pl.multiple_of((me ^ k) * count, count)
-        store(whole_ref, load(ref), pl.ds(begin, count))
-
-
-def local_kernel(axis, level, mine_ref, twin_ref, local_ref, late_ref, out_ref, whole_ref):
+def join_kernel(*refs):
+    for place, ref in enumerate(refs[:4]):
+        refs[4][place] = ref[...]
+
+
+def assemble(axis, mine_ref, twin_ref, whole_ref):
+    me = lax.axis_index(axis)
+    for other, ref in enumerate((mine_ref, twin_ref)):
+        for place in range(4):
+            rows = own_rows(me ^ (2 * place + other), ref.shape[2])
+            store(whole_ref, (ref[place, 0], ref[place, 1]), rows)
+
+
+def local_kernel(axis, level, mine_ref, twin_ref, local_ref, late_ref, out_ref, high_ref, low_ref, whole_ref, sent):
     me = lax.axis_index(axis)
     half = mine_ref.shape[1]
     upper = (me // level) & 1
+    block = (me // level) & 3
     last = me == lax.axis_size(axis) - 1
 
     @pl.when(upper == 0)
     def _():
-        for k in range(2):
-            out_ref[k] = local_ref[k].T
+        store(whole_ref, [local_ref[k].T for k in range(2)])
 
     @pl.when(upper == 1)
     def _():
         store(whole_ref, load(mine_ref), core_rows(me, half))
         store(whole_ref, load(twin_ref), core_rows(me ^ 1, half))
-        store(whole_ref, product(halves(load(whole_ref)), halves(load(local_ref))))
-
-    @pl.when(last)
-    def _():
-        store(whole_ref, product(halves(load(whole_ref)), halves(load(late_ref))))
-
-    @pl.when(upper == 1)
-    def _():
-        for k in range(2):
-            out_ref[k] = whole_ref[k].T
-
-
-def final_kernel(axis, level, *refs):
-    in_refs, local_ref, out_ref, whole_ref = refs[:8], refs[8], refs[9], refs[10]
+        grown = three_products(thirds(load(whole_ref)), thirds(load(local_ref)))
+
+        @pl.when(jnp.logical_not(last))
+        def _():
+            store(whole_ref, [grown[k].T for k in range(2)])
+
+        @pl.when(last)
+        def _():
+            ended = three_products(thirds(grown), thirds(load(late_ref)))
+            store(whole_ref, [ended[k].T for k in range(2)])
+
+    @pl.when(block < 2)
+    def _():
+        copy = pltpu.make_async_copy(whole_ref, out_ref.at[0], sent)
+        copy.start()
+        copy.wait()
+
+    @pl.when(block >= 2)
+    def _():
+        for k, (high, low) in enumerate(thirds(load(whole_ref))):
+            high_ref[k] = high
+            low_ref[k] = low
+
+
+def final_kernel(axis, level, mine_ref, twin_ref, high_ref, low_ref, done_ref, out_ref, whole_ref, result_ref, sent):
     block = (lax.axis_index(axis) // level) & 3
-
-    def put(pair):
-        out_ref[0, 0] = pair[0]
-        out_ref[0, 1] = pair[1]
-
-    @pl.when(block < 2)
-    def _():
-        put(load(local_ref))
-
-    @pl.when(block >= 2)
-    def _():
-        assemble(axis, in_refs, whole_ref)
+    steps = sent.shape[0]
+    count = whole_ref.shape[1] // steps
+
+    def put(turned):
+        assemble(axis, mine_ref, twin_ref, whole_ref)
+        whole = load(whole_ref)
+        right = thirds([part.T for part in whole] if turned else whole)
+        copies = []
+        for step in range(steps):
+            rows = pl.ds(step * count, count)
+            left = [(high_ref[k, rows, :], low_ref[k, rows, :]) for k in range(3)]
+            store(result_ref, three_products(left, right), rows)
+            copies.append(
+                pltpu.make_async_copy(result_ref.at[:, rows], out_ref.at[0, :, rows], sent.at[step])
+            )
+            copies[-1].start()
+        for copy in copies:
+            copy.wait()
 
     @pl.when(block == 2)
     def _():
-        put(product(halves(load(local_ref)), halves(load(whole_ref))))
+        put(False)
 
     @pl.when(block == 3)
     def _():
-        put(product(halves(load(local_ref)), halves(load(whole_ref)), True))
-
-
-def plane_slices(mine, axis):
-    even = [mine] + [exchanged(mine, axis, mask) for mask in (2, 4, 6)]
-    odd = [exchanged(piece, axis, 1) for piece in even]
-    return [piece for both in zip(even, odd) for piece in both]
+        put(True)
+
+
+def plane_slices(mine, axis, level):
+    even = [mine] + [upper_exchanged(mine, axis, level, mask) for mask in (2, 4, 6)]
+    shape = jax.ShapeDtypeStruct((4,) + mine.shape, mine.dtype)
+    joined = call(join_kernel, shape, [], mine.size, *even)
+    return joined, exchanged(joined, axis, 1)
 
 
 def cumulative(samples):
@@ -504,21 +537,37 @@
             )
             level = 2 * level
         mine, bulk = call(functools.partial(cut_kernel, axis, level), [strip, half_shape], turning, cube, total)
-    came = exchanged(mine, axis, level)
+    came = lower_exchanged(mine, axis, level)
     step = call(functools.partial(step_kernel, axis, level), strip, [], 3 * cube // parts, came, total)
     below = exchanged(step, axis, 2 * level)
     came_bulk = exchanged(bulk, axis, level)
     twin_bulk = exchanged(came_bulk, axis, 1)
     room = [pltpu.VMEM((2, size, size), jnp.float32)]
     late = call(functools.partial(late_kernel, axis), whole, [], cube, *prepared, last_next)
-    local = call(functools.partial(local_kernel, axis, level), whole, room, 3 * cube, came_bulk, twin_bulk, local, late)
+    out_shape = f32(1, 2, size, size)
+    out, high, low = call(
+        functools.partial(local_kernel, axis, level),
+        [out_shape, third_shape, third_shape],
+        room + [pltpu.SemaphoreType.DMA(())],
+        3 * cube,
+        came_bulk,
+        twin_bulk,
+        local,
+        late,
+        out_places=(pl.ANY, pltpu.VMEM, pltpu.VMEM),
+    )
     return call(
         functools.partial(final_kernel, axis, level),
-        f32(1, 2, size, size),
-        room,
+        out_shape,
+        room + room + [pltpu.SemaphoreType.DMA((2,))],
         3 * cube,
-        *plane_slices(below, axis),
-        local,
+        *plane_slices(below, axis, level),
+        high,
+        low,
+        out,
+        places=(pltpu.VMEM,) * 4 + (pl.ANY,),
+        out_places=(pl.ANY,),
+        aliases={4: 0},
     )
 
 

time: 63.1 us -> 60 us (0.951)
  waiting for transfers between devices: 23.1 us -> 16.3 us
  starting transfers between devices: 26.5 us -> 30.3 us
    ppermute x26 -> x19, waiting for transfers between devices: 17.9 us -> 7.63 us  [exchanged(): return lax.ppermute(x, axis, [(i, i ^ mask) for i in range(size)])]
    ppermute x0 -> x4, starting transfers between devices: none -> 3.84 us  [the longest x3 2.65 us: upper_exchanged(): lax.ppermute(x, axis, [(i, i ^ (mask if i // level & 2 else 1)) for i in...]
    ppermute x1, waiting for transfers between devices: 0.01 us -> 2.59 us  [to_last(): return lax.ppermute(x, axis, [(size - plane, size - 1)])]
    ppermute x0 -> x4, waiting for transfers between devices: none -> 0.91 us  [the longest x1 0.9 us: lower_exchanged(): lax.ppermute(x, axis, [(i, i ^ (level if i // level & 2 == 0 else 1)) for...]
    pallas_call x11 -> x12, Pallas kernels: 12.2 us -> 12.1 us  [call(): pl.pallas_call(kernel, out_shape=outs, in_specs=in_specs, out_specs=out_s...]
    ppermute x26 -> x19, starting transfers between devices: 24.5 us -> 24.5 us  [exchanged(): return lax.ppermute(x, axis, [(i, i ^ mask) for i in range(size)])]
  transfers between devices with their start and end apart: 28 -> 25, of which waited for: 10 -> 10; matrix products, arithmetic and copies ran while one was open for 0% -> 0% of each run, Pallas kernels for 7% -> 8%
where the time goes in v4:
time: 60 us; the launch traced here: 59.9 us
  starting transfers between devices  30.3 us (50%)
  waiting for transfers between devices  16.3 us (27%)
  Pallas kernels  12.1 us (20%)
  local copies, waits for them, and re-layouts  1.04 us (2%)
    ppermute x19, starting transfers between devices, exchanged(): return lax.ppermute(x, axis, [(i, i ^ mask) for i in range(size)])  24.5 us
    pallas_call x12, Pallas kernels, call(): pl.pallas_call(kernel, out_shape=outs, in_specs=in_specs, out_specs=out_s...  12.1 us
    ppermute x19, waiting for transfers between devices, exchanged(): return lax.ppermute(x, axis, [(i, i ^ mask) for i in range(size)])  7.63 us
    ppermute x1, waiting for transfers between devices, from_next(): return lax.ppermute(x, axis, sorted(target.items()))  5.16 us
    ppermute x3, starting transfers between devices, upper_exchanged(): lax.ppermute(x, axis, [(i, i ^ (mask if i // level & 2 else 1)) for i in...  2.65 us
    ppermute x1, waiting for transfers between devices, to_last(): return lax.ppermute(x, axis, [(size - plane, size - 1)])  2.59 us
    ppermute x1, starting transfers between devices, to_last(): return lax.ppermute(x, axis, [(size - plane, size - 1)])  1.28 us
  transfers between devices with their start and end apart: 25, of which 10 were waited for; matrix products, arithmetic and copies ran while one was open for 0% of the time, Pallas kernels for 8%

profile of v4, /device:TPU:31, one launch (start us, length us, event | category | flops | bytes accessed | tf_op | source)
XLA Modules:
  0.0 59.9 jit_solution(16588042071536748245)
XLA Ops:
  0.0 1.0 %copy-done = f32[1,2,256,256]{3,2,1,0:T(8,128)S(1)} copy-done((f32[1,2,256,256]{3,2,1,0:T(8,128)S(1)}, f32[1,2,256,256]{3,2,1,0:T(8,128)}, u32[]{:S(2)}) %copy-start) | copy-done | bytes 524312
  1.2 0.7 %collective-permute-start.1 = (f32[256,256]{1,0:T(8,128)S(1)}, f32[256,256]{1,0:T(8,128)S(1)}, u32[]{:S(2)}, u32[]{:S(2)}) collective-permute-start(f32[256,256]{1,0:T(8,128)S(1)} %shard_map.17.packed_ref), channel_id=1, source_target_pairs={{0,24},{1,0},{2,1},{3,2},{4,3},{5,4},{6,5},{7,6},{8,7},{9,8},{10,9... | collective-permute-start | bytes 786440 | tf_op jit(solution)/shard_map/ppermute | solution.py:36
  2.2 5.2 %collective-permute-done.1.next_ref = f32[256,256]{1,0:T(8,128)S(1)} collective-permute-done((f32[256,256]{1,0:T(8,128)S(1)}, f32[256,256]{1,0:T(8,128)S(1)}, u32[]{:S(2)}, u32[]{:S(2)}) %collective-permute-start.1) | collective-permute-done | bytes 262176 | tf_op jit(solution)/shard_map/ppermute | solution.py:36
  7.4 1.9 %shard_map.19.own_ref = f32[2,256,256]{2,1,0:T(8,128)S(1)} custom-call(f32[2,256,256]{2,1,0:T(8,128)S(1)} %get-tuple-element.24.parts_ref, bf16[3,256,256]{2,1,0:T(8,128)(2,1)S(1)} %get-tuple-element.25.high_ref, bf16[3,256,256]{2,1,0:T(8,128)(2,1)S(1)} %get-tuple-element.26.low_ref, f32[256,256]{1,0:T(8,128)S(1)} %collective-permute-done.pair_ref, ...), custom_call_target="tpu_custom_call" | custom-call | flops 1207959552 | bytes 2359296 | tf_op jit(solution)/shard_map/pallas_call | solution.py:77
  9.4 1.9 %collective-permute-done.2.other_ref = f32[2,256,256]{2,1,0:T(8,128)S(1)} collective-permute-done((f32[2,256,256]{2,1,0:T(8,128)S(1)}, f32[2,256,256]{2,1,0:T(8,128)S(1)}, u32[]{:S(2)}, u32[]{:S(2)}) %collective-permute-start.2) | collective-permute-done | bytes 524320 | tf_op jit(solution)/shard_map/ppermute | solution.py:18
  11.7 2.8 %collective-permute-start.3 = (f32[128,256]{1,0:T(8,128)S(1)}, f32[128,256]{1,0:T(8,128)S(1)}, u32[]{:S(2)}, u32[]{:S(2)}) collective-permute-start(f32[128,256]{1,0:T(8,128)S(1)} %get-tuple-element.27), channel_id=1, source_target_pairs={{0,4},{1,5},{2,6},{3,7},{4,0},{5,1},{6,2},{7,3},{8,12},{9,13},{10,... | collective-permute-start | bytes 393224 | tf_op jit(solution)/shard_map/ppermute | solution.py:18
  14.7 1.9 %collective-permute-done.10.refs_2_ = f32[128,256]{1,0:T(8,128)S(1)} collective-permute-done((f32[128,256]{1,0:T(8,128)S(1)}, f32[128,256]{1,0:T(8,128)S(1)}, u32[]{:S(2)}, u32[]{:S(2)}) %collective-permute-start.10) | collective-permute-done | bytes 131104 | tf_op jit(solution)/shard_map/ppermute | solution.py:18
  16.6 1.0 %collective-permute-start.11 = (f32[128,256]{1,0:T(8,128)S(1)}, f32[128,256]{1,0:T(8,128)S(1)}, u32[]{:S(2)}, u32[]{:S(2)}) collective-permute-start(f32[128,256]{1,0:T(8,128)S(1)} %collective-permute-done.10.refs_2_), channel_id=1, source_target_pairs={{0,1},{1,0},{2,3},{3,2},{4,5},{5,4},{6,7},{7,6},{8,9},{9,8},{10,11... | collective-permute-start | bytes 393224 | tf_op jit(solution)/shard_map/ppermute | solution.py:18
  17.8 2.1 %collective-permute-start.13 = (f32[128,256]{1,0:T(8,128)S(1)}, f32[128,256]{1,0:T(8,128)S(1)}, u32[]{:S(2)}, u32[]{:S(2)}) collective-permute-start(f32[128,256]{1,0:T(8,128)S(1)} %collective-permute-done.3.refs_6_), channel_id=1, source_target_pairs={{0,1},{1,0},{2,3},{3,2},{4,5},{5,4},{6,7},{7,6},{8,9},{9,8},{10,11... | collective-permute-start | bytes 393224 | tf_op jit(solution)/shard_map/ppermute | solution.py:18
  19.9 0.7 %collective-permute-done.14.refs_8_ = f32[128,256]{1,0:T(8,128)S(1)} collective-permute-done((f32[128,256]{1,0:T(8,128)S(1)}, f32[128,256]{1,0:T(8,128)S(1)}, u32[]{:S(2)}, u32[]{:S(2)}) %collective-permute-start.14) | collective-permute-done | bytes 131104 | tf_op jit(solution)/shard_map/ppermute | solution.py:18
  20.6 1.5 %collective-permute-start.7 = (f32[128,256]{1,0:T(8,128)S(1)}, f32[128,256]{1,0:T(8,128)S(1)}, u32[]{:S(2)}, u32[]{:S(2)}) collective-permute-start(f32[128,256]{1,0:T(8,128)S(1)} %collective-permute-done.6.refs_4_), channel_id=1, source_target_pairs={{0,4},{1,5},{2,6},{3,7},{4,0},{5,1},{6,2},{7,3},{8,12},{9,13},{10,... | collective-permute-start | bytes 393224 | tf_op jit(solution)/shard_map/ppermute | solution.py:18
  22.1 1.8 %collective-permute-start.15 = (f32[128,256]{1,0:T(8,128)S(1)}, f32[128,256]{1,0:T(8,128)S(1)}, u32[]{:S(2)}, u32[]{:S(2)}) collective-permute-start(f32[128,256]{1,0:T(8,128)S(1)} %collective-permute-done.14.refs_8_), channel_id=1, source_target_pairs={{0,1},{1,0},{2,3},{3,2},{4,5},{5,4},{6,7},{7,6},{8,9},{9,8},{10,11... | collective-permute-start | bytes 393224 | tf_op jit(solution)/shard_map/ppermute | solution.py:18
  24.0 0.4 collective-permute-done.4.refs_0_
  24.4 2.4 %collective-permute-start.5 = (f32[128,256]{1,0:T(8,128)S(1)}, f32[128,256]{1,0:T(8,128)S(1)}, u32[]{:S(2)}, u32[]{:S(2)}) collective-permute-start(f32[128,256]{1,0:T(8,128)S(1)} %collective-permute-done.4.refs_0_), channel_id=1, source_target_pairs={{0,1},{1,0},{2,3},{3,2},{4,5},{5,4},{6,7},{7,6},{8,9},{9,8},{10,11... | collective-permute-start | bytes 393224 | tf_op jit(solution)/shard_map/ppermute | solution.py:18
  27.2 0.8 %shard_map.21 = (bf16[4,2,256,256]{3,2,1,0:T(8,128)(2,1)S(1)}, bf16[4,2,256,256]{3,2,1,0:T(8,128)(2,1)S(1)}, bf16[2,256,256]{2,1,0:T(8,128)(2,1)S(1)}, bf16[2,256,256]{2,1,0:T(8,128)(2,1)S(1)}) custom-call(f32[2,128,256]{2,1,0:T(8,128)S(1)} %get-tuple-element.29.refs_0_, f32[2,128,256]{2,1,0:T(8,128)S(1)} %collective-permute-done.9.refs_1_, ...), custom_call_target="tpu_custom_call" | custom-call | flops 402653184 | bytes 4194304 | tf_op jit(solution)/shard_map/pallas_call | solution.py:77
  28.2 1.1 %shard_map.22 = (f32[2,32,256]{2,1,0:T(8,128)S(1)}, bf16[4,2,256,256]{3,2,1,0:T(8,128)(2,1)S(1)}, bf16[4,2,256,256]{3,2,1,0:T(8,128)(2,1)S(1)}) custom-call(f32[128,256]{1,0:T(8,128)S(1)} %collective-permute-done.4.refs_0_, f32[128,256]{1,0:T(8,128)S(1)} %collective-permute-done.5.refs_1_, ...), custom_call_target="tpu_custom_call", output_to_operand_aliasing={{1}: (4, {}), {2}: (5, {})} | custom-call | flops 134217728 | bytes 5308416 | tf_op jit(solution)/shard_map/pallas_call | solution.py:77
  29.3 2.4 %shard_map.23 = (f32[2,256,256]{2,1,0:T(8,128)S(1)}, f32[2,256,256]{2,1,0:T(8,128)S(1)}, f32[2,128,256]{2,1,0:T(8,128)S(1)}) custom-call(bf16[4,2,256,256]{3,2,1,0:T(8,128)(2,1)S(1)} %get-tuple-element.35.high_ref, bf16[4,2,256,256]{3,2,1,0:T(8,128)(2,1)S(1)} %get-tuple-element.36.low_ref, f32[2,256,256]{2,1,0:T(8,128)S(1)} %shard_map.19.own_ref, ...), custom_call_target="tpu_custom_call" | custom-call | flops 1610612736 | bytes 4456448 | tf_op jit(solution)/shard_map/pallas_call | solution.py:77
  31.7 0.8 %collective-permute-start.22 = (f32[2,128,256]{2,1,0:T(8,128)S(1)}, f32[2,128,256]{2,1,0:T(8,128)S(1)}, u32[]{:S(2)}, u32[]{:S(2)}) collective-permute-start(f32[2,128,256]{2,1,0:T(8,128)S(1)} %get-tuple-element.38), channel_id=1, source_target_pairs={{0,8},{1,9},{2,10},{3,11},{4,12},{5,13},{6,14},{7,15},{8,0},{9,1},... | collective-permute-start | bytes 786440 | tf_op jit(solution)/shard_map/ppermute | solution.py:18
  32.5 1.2 %collective-permute-start.16 = (f32[2,32,256]{2,1,0:T(8,128)S(1)}, f32[2,32,256]{2,1,0:T(8,128)S(1)}, u32[]{:S(2)}, u32[]{:S(2)}) collective-permute-start(f32[2,32,256]{2,1,0:T(8,128)S(1)} %get-tuple-element.34), channel_id=1, source_target_pairs={{0,8},{1,9},{2,10},{3,11},{4,12},{5,13},{6,14},{7,15},{8,0},{9,1},... | collective-permute-start | bytes 196616 | tf_op jit(solution)/shard_map/ppermute | solution.py:23
  33.7 0.9 %collective-permute-done.16.came_ref = f32[2,32,256]{2,1,0:T(8,128)S(1)} collective-permute-done((f32[2,32,256]{2,1,0:T(8,128)S(1)}, f32[2,32,256]{2,1,0:T(8,128)S(1)}, u32[]{:S(2)}, u32[]{:S(2)}) %collective-permute-start.16) | collective-permute-done | bytes 65568 | tf_op jit(solution)/shard_map/ppermute | solution.py:23
  34.9 6.6 %collective-permute-start.17 = (f32[2,32,256]{2,1,0:T(8,128)S(1)}, f32[2,32,256]{2,1,0:T(8,128)S(1)}, u32[]{:S(2)}, u32[]{:S(2)}) collective-permute-start(f32[2,32,256]{2,1,0:T(8,128)S(1)} %shard_map.24), channel_id=1, source_target_pairs={{0,16},{1,17},{2,18},{3,19},{4,20},{5,21},{6,22},{7,23},{8,24},{9,... | collective-permute-start | bytes 196616 | tf_op jit(solution)/shard_map/ppermute | solution.py:18
  41.5 2.4 %collective-permute-done.17.refs_0_ = f32[2,32,256]{2,1,0:T(8,128)S(1)} collective-permute-done((f32[2,32,256]{2,1,0:T(8,128)S(1)}, f32[2,32,256]{2,1,0:T(8,128)S(1)}, u32[]{:S(2)}, u32[]{:S(2)}) %collective-permute-start.17) | collective-permute-done | bytes 65568 | tf_op jit(solution)/shard_map/ppermute | solution.py:18
  43.9 0.7 %collective-permute-start.20 = (f32[2,32,256]{2,1,0:T(8,128)S(1)}, f32[2,32,256]{2,1,0:T(8,128)S(1)}, u32[]{:S(2)}, u32[]{:S(2)}) collective-permute-start(f32[2,32,256]{2,1,0:T(8,128)S(1)} %collective-permute-done.17.refs_0_), channel_id=1, source_target_pairs={{0,1},{1,0},{2,3},{3,2},{4,5},{5,4},{6,7},{7,6},{8,9},{9,8},{10,11... | collective-permute-start | bytes 196616 | tf_op jit(solution)/shard_map/ppermute | solution.py:28
  44.6 0.6 collective-permute-start.19
  45.2 1.4 %collective-permute-start.18 = (f32[2,32,256]{2,1,0:T(8,128)S(1)}, f32[2,32,256]{2,1,0:T(8,128)S(1)}, u32[]{:S(2)}, u32[]{:S(2)}) collective-permute-start(f32[2,32,256]{2,1,0:T(8,128)S(1)} %collective-permute-done.17.refs_0_), channel_id=1, source_target_pairs={{0,1},{1,0},{2,3},{3,2},{4,5},{5,4},{6,7},{7,6},{8,9},{9,8},{10,11... | collective-permute-start | bytes 196616 | tf_op jit(solution)/shard_map/ppermute | solution.py:28
  46.6 1.3 %collective-permute-start.24 = (f32[256,256]{1,0:T(8,128)S(1)}, f32[256,256]{1,0:T(8,128)S(1)}, u32[]{:S(2)}, u32[]{:S(2)}) collective-permute-start(f32[256,256]{1,0:T(8,128)S(1)} %collective-permute-done.1.next_ref), channel_id=1, source_target_pairs={{24,31}} | collective-permute-start | bytes 786440 | tf_op jit(solution)/shard_map/ppermute | solution.py:41
  47.9 2.7 %collective-permute-start.23 = (f32[2,128,256]{2,1,0:T(8,128)S(1)}, f32[2,128,256]{2,1,0:T(8,128)S(1)}, u32[]{:S(2)}, u32[]{:S(2)}) collective-permute-start(f32[2,128,256]{2,1,0:T(8,128)S(1)} %collective-permute-done.22.mine_ref), channel_id=1, source_target_pairs={{0,1},{1,0},{2,3},{3,2},{4,5},{5,4},{6,7},{7,6},{8,9},{9,8},{10,11... | collective-permute-start | bytes 786440 | tf_op jit(solution)/shard_map/ppermute | solution.py:18
  50.6 1.9 %collective-permute-start.21 = (f32[4,2,32,256]{3,2,1,0:T(8,128)S(1)}, f32[4,2,32,256]{3,2,1,0:T(8,128)S(1)}, u32[]{:S(2)}, u32[]{:S(2)}) collective-permute-start(f32[4,2,32,256]{3,2,1,0:T(8,128)S(1)} %shard_map.25.mine_ref), channel_id=1, source_target_pairs={{0,1},{1,0},{2,3},{3,2},{4,5},{5,4},{6,7},{7,6},{8,9},{9,8},{10,11... | collective-permute-start | bytes 786440 | tf_op jit(solution)/shard_map/ppermute | solution.py:18
  52.5 2.6 %collective-permute-done.24.next_ref = f32[256,256]{1,0:T(8,128)S(1)} collective-permute-done((f32[256,256]{1,0:T(8,128)S(1)}, f32[256,256]{1,0:T(8,128)S(1)}, u32[]{:S(2)}, u32[]{:S(2)}) %collective-permute-start.24) | collective-permute-done | bytes 262176 | tf_op jit(solution)/shard_map/ppermute | solution.py:41
  55.1 1.9 %shard_map.26.late_ref = f32[2,256,256]{2,1,0:T(8,128)S(1)} custom-call(f32[2,256,256]{2,1,0:T(8,128)S(1)} %get-tuple-element.24.parts_ref, bf16[3,256,256]{2,1,0:T(8,128)(2,1)S(1)} %get-tuple-element.25.high_ref, bf16[3,256,256]{2,1,0:T(8,128)(2,1)S(1)} %get-tuple-element.26.low_ref, f32[256,256]{1,0:T(8,128)S(1)} %collective-permute-done.24.next_ref), custom_call_target="tpu_custom_call" | custom-call | flops 134217728 | bytes 2097152 | tf_op jit(solution)/shard_map/pallas_call | solution.py:77
  57.1 1.3 %shard_map.27 = (f32[1,2,256,256]{3,2,1,0:T(8,128)}, bf16[3,256,256]{2,1,0:T(8,128)(2,1)S(1)}, bf16[3,256,256]{2,1,0:T(8,128)(2,1)S(1)}) custom-call(f32[2,128,256]{2,1,0:T(8,128)S(1)} %collective-permute-done.22.mine_ref, f32[2,128,256]{2,1,0:T(8,128)S(1)} %collective-permute-done.23.twin_ref, f32[2,256,256]{2,1,0:T(8,128)S(1)} %get-tuple-element.39.local_ref, ...), custom_call_target="tpu_custom_call" | custom-call | flops 402653184 | bytes 2883584 | tf_op jit(solution)/shard_map/pallas_call | solution.py:77
  58.4 1.4 %shard_map.28 = f32[1,2,256,256]{3,2,1,0:T(8,128)} custom-call(f32[4,2,32,256]{3,2,1,0:T(8,128)S(1)} %shard_map.25.mine_ref, f32[4,2,32,256]{3,2,1,0:T(8,128)S(1)} %collective-permute-done.21.twin_ref, bf16[3,256,256]{2,1,0:T(8,128)(2,1)S(1)} %get-tuple-element.40.high_ref, ...), custom_call_target="tpu_custom_call", output_to_operand_aliasing={{}: (4, {})} | custom-call | flops 402653184 | bytes 2359296 | tf_op jit(solution)/shard_map/pallas_call | solution.py:77
  (32 shorter events, 2.3 us)
Async XLA Ops:
  0.0 1.0 %copy-start = (f32[1,2,256,256]{3,2,1,0:T(8,128)S(1)}, f32[1,2,256,256]{3,2,1,0:T(8,128)}, u32[]{:S(2)}) copy-start(f32[1,2,256,256]{3,2,1,0:T(8,128)} %drawn_ref.1) | copy-start | bytes 1572868
  1.2 6.2 %collective-permute-start.1 = (f32[256,256]{1,0:T(8,128)S(1)}, f32[256,256]{1,0:T(8,128)S(1)}, u32[]{:S(2)}, u32[]{:S(2)}) collective-permute-start(f32[256,256]{1,0:T(8,128)S(1)} %shard_map.17.packed_ref), channel_id=1, source_target_pairs={{0,24},{1,0},{2,1},{3,2},{4,3},{5,4},{6,5},{7,6},{8,7},{9,8},{10,9... | collective-permute-start | bytes 786440 | tf_op jit(solution)/shard_map/ppermute | solution.py:36
  1.9 5.4 %collective-permute-start = (f32[256,256]{1,0:T(8,128)S(1)}, f32[256,256]{1,0:T(8,128)S(1)}, u32[]{:S(2)}, u32[]{:S(2)}) collective-permute-start(f32[256,256]{1,0:T(8,128)S(1)} %shard_map.17.packed_ref), channel_id=1, source_target_pairs={{0,1},{1,0},{2,3},{3,2},{4,5},{5,4},{6,7},{7,6},{8,9},{9,8},{10,11... | collective-permute-start | bytes 786440 | tf_op jit(solution)/shard_map/ppermute | solution.py:18
  9.3 2.0 %collective-permute-start.2 = (f32[2,256,256]{2,1,0:T(8,128)S(1)}, f32[2,256,256]{2,1,0:T(8,128)S(1)}, u32[]{:S(2)}, u32[]{:S(2)}) collective-permute-start(f32[2,256,256]{2,1,0:T(8,128)S(1)} %shard_map.19.own_ref), channel_id=1, source_target_pairs={{0,1},{1,0},{2,3},{3,2},{4,5},{5,4},{6,7},{7,6},{8,9},{9,8},{10,11... | collective-permute-start | bytes 1572872 | tf_op jit(solution)/shard_map/ppermute | solution.py:18
  11.7 5.0 %collective-permute-start.10 = (f32[128,256]{1,0:T(8,128)S(1)}, f32[128,256]{1,0:T(8,128)S(1)}, u32[]{:S(2)}, u32[]{:S(2)}) collective-permute-start(f32[128,256]{1,0:T(8,128)S(1)} %get-tuple-element.27), channel_id=1, source_target_pairs={{0,2},{1,3},{2,0},{3,1},{4,6},{5,7},{6,4},{7,5},{8,10},{9,11},{10,... | collective-permute-start | bytes 393224 | tf_op jit(solution)/shard_map/ppermute | solution.py:18
  11.7 6.0 %collective-permute-start.3 = (f32[128,256]{1,0:T(8,128)S(1)}, f32[128,256]{1,0:T(8,128)S(1)}, u32[]{:S(2)}, u32[]{:S(2)}) collective-permute-start(f32[128,256]{1,0:T(8,128)S(1)} %get-tuple-element.27), channel_id=1, source_target_pairs={{0,4},{1,5},{2,6},{3,7},{4,0},{5,1},{6,2},{7,3},{8,12},{9,13},{10,... | collective-permute-start | bytes 393224 | tf_op jit(solution)/shard_map/ppermute | solution.py:18
  14.6 6.0 %collective-permute-start.14 = (f32[128,256]{1,0:T(8,128)S(1)}, f32[128,256]{1,0:T(8,128)S(1)}, u32[]{:S(2)}, u32[]{:S(2)}) collective-permute-start(f32[128,256]{1,0:T(8,128)S(1)} %get-tuple-element.28), channel_id=1, source_target_pairs={{0,4},{1,5},{2,6},{3,7},{4,0},{5,1},{6,2},{7,3},{8,12},{9,13},{10,... | collective-permute-start | bytes 393224 | tf_op jit(solution)/shard_map/ppermute | solution.py:18
  14.6 6.1 %collective-permute-start.6 = (f32[128,256]{1,0:T(8,128)S(1)}, f32[128,256]{1,0:T(8,128)S(1)}, u32[]{:S(2)}, u32[]{:S(2)}) collective-permute-start(f32[128,256]{1,0:T(8,128)S(1)} %get-tuple-element.28), channel_id=1, source_target_pairs={{0,2},{1,3},{2,0},{3,1},{4,6},{5,7},{6,4},{7,5},{8,10},{9,11},{10,... | collective-permute-start | bytes 393224 | tf_op jit(solution)/shard_map/ppermute | solution.py:18
  16.6 5.5 %collective-permute-start.11 = (f32[128,256]{1,0:T(8,128)S(1)}, f32[128,256]{1,0:T(8,128)S(1)}, u32[]{:S(2)}, u32[]{:S(2)}) collective-permute-start(f32[128,256]{1,0:T(8,128)S(1)} %collective-permute-done.10.refs_2_), channel_id=1, source_target_pairs={{0,1},{1,0},{2,3},{3,2},{4,5},{5,4},{6,7},{7,6},{8,9},{9,8},{10,11... | collective-permute-start | bytes 393224 | tf_op jit(solution)/shard_map/ppermute | solution.py:18
  17.8 6.2 %collective-permute-start.13 = (f32[128,256]{1,0:T(8,128)S(1)}, f32[128,256]{1,0:T(8,128)S(1)}, u32[]{:S(2)}, u32[]{:S(2)}) collective-permute-start(f32[128,256]{1,0:T(8,128)S(1)} %collective-permute-done.3.refs_6_), channel_id=1, source_target_pairs={{0,1},{1,0},{2,3},{3,2},{4,5},{5,4},{6,7},{7,6},{8,9},{9,8},{10,11... | collective-permute-start | bytes 393224 | tf_op jit(solution)/shard_map/ppermute | solution.py:18
  19.9 7.3 %collective-permute-start.9 = (f32[2,128,256]{2,1,0:T(8,128)S(1)}, f32[2,128,256]{2,1,0:T(8,128)S(1)}, u32[]{:S(2)}, u32[]{:S(2)}) collective-permute-start(f32[2,128,256]{2,1,0:T(8,128)S(1)} %get-tuple-element.29.refs_0_), channel_id=1, source_target_pairs={{0,1},{1,0},{2,3},{3,2},{4,5},{5,4},{6,7},{7,6},{8,9},{9,8},{10,11... | collective-permute-start | bytes 786440 | tf_op jit(solution)/shard_map/ppermute | solution.py:18
  20.6 3.8 %collective-permute-start.4 = (f32[128,256]{1,0:T(8,128)S(1)}, f32[128,256]{1,0:T(8,128)S(1)}, u32[]{:S(2)}, u32[]{:S(2)}) collective-permute-start(f32[128,256]{1,0:T(8,128)S(1)} %collective-permute-done.3.refs_6_), channel_id=1, source_target_pairs={{0,2},{1,3},{2,0},{3,1},{4,6},{5,7},{6,4},{7,5},{8,10},{9,11},{10,... | collective-permute-start | bytes 393224 | tf_op jit(solution)/shard_map/ppermute | solution.py:18
  20.6 6.2 %collective-permute-start.7 = (f32[128,256]{1,0:T(8,128)S(1)}, f32[128,256]{1,0:T(8,128)S(1)}, u32[]{:S(2)}, u32[]{:S(2)}) collective-permute-start(f32[128,256]{1,0:T(8,128)S(1)} %collective-permute-done.6.refs_4_), channel_id=1, source_target_pairs={{0,4},{1,5},{2,6},{3,7},{4,0},{5,1},{6,2},{7,3},{8,12},{9,13},{10,... | collective-permute-start | bytes 393224 | tf_op jit(solution)/shard_map/ppermute | solution.py:18
  22.1 5.0 %collective-permute-start.15 = (f32[128,256]{1,0:T(8,128)S(1)}, f32[128,256]{1,0:T(8,128)S(1)}, u32[]{:S(2)}, u32[]{:S(2)}) collective-permute-start(f32[128,256]{1,0:T(8,128)S(1)} %collective-permute-done.14.refs_8_), channel_id=1, source_target_pairs={{0,1},{1,0},{2,3},{3,2},{4,5},{5,4},{6,7},{7,6},{8,9},{9,8},{10,11... | collective-permute-start | bytes 393224 | tf_op jit(solution)/shard_map/ppermute | solution.py:18
  23.9 3.2 %collective-permute-start.12 = (f32[128,256]{1,0:T(8,128)S(1)}, f32[128,256]{1,0:T(8,128)S(1)}, u32[]{:S(2)}, u32[]{:S(2)}) collective-permute-start(f32[128,256]{1,0:T(8,128)S(1)} %collective-permute-done.6.refs_4_), channel_id=1, source_target_pairs={{0,1},{1,0},{2,3},{3,2},{4,5},{5,4},{6,7},{7,6},{8,9},{9,8},{10,11... | collective-permute-start | bytes 393224 | tf_op jit(solution)/shard_map/ppermute | solution.py:18
  24.4 3.6 %collective-permute-start.5 = (f32[128,256]{1,0:T(8,128)S(1)}, f32[128,256]{1,0:T(8,128)S(1)}, u32[]{:S(2)}, u32[]{:S(2)}) collective-permute-start(f32[128,256]{1,0:T(8,128)S(1)} %collective-permute-done.4.refs_0_), channel_id=1, source_target_pairs={{0,1},{1,0},{2,3},{3,2},{4,5},{5,4},{6,7},{7,6},{8,9},{9,8},{10,11... | collective-permute-start | bytes 393224 | tf_op jit(solution)/shard_map/ppermute | solution.py:18
  26.8 1.4 %collective-permute-start.8 = (f32[128,256]{1,0:T(8,128)S(1)}, f32[128,256]{1,0:T(8,128)S(1)}, u32[]{:S(2)}, u32[]{:S(2)}) collective-permute-start(f32[128,256]{1,0:T(8,128)S(1)} %collective-permute-done.7.refs_2_), channel_id=1, source_target_pairs={{0,1},{1,0},{2,3},{3,2},{4,5},{5,4},{6,7},{7,6},{8,9},{9,8},{10,11... | collective-permute-start | bytes 393224 | tf_op jit(solution)/shard_map/ppermute | solution.py:18
  31.7 16.1 %collective-permute-start.22 = (f32[2,128,256]{2,1,0:T(8,128)S(1)}, f32[2,128,256]{2,1,0:T(8,128)S(1)}, u32[]{:S(2)}, u32[]{:S(2)}) collective-permute-start(f32[2,128,256]{2,1,0:T(8,128)S(1)} %get-tuple-element.38), channel_id=1, source_target_pairs={{0,8},{1,9},{2,10},{3,11},{4,12},{5,13},{6,14},{7,15},{8,0},{9,1},... | collective-permute-start | bytes 786440 | tf_op jit(solution)/shard_map/ppermute | solution.py:18
  32.5 2.1 %collective-permute-start.16 = (f32[2,32,256]{2,1,0:T(8,128)S(1)}, f32[2,32,256]{2,1,0:T(8,128)S(1)}, u32[]{:S(2)}, u32[]{:S(2)}) collective-permute-start(f32[2,32,256]{2,1,0:T(8,128)S(1)} %get-tuple-element.34), channel_id=1, source_target_pairs={{0,8},{1,9},{2,10},{3,11},{4,12},{5,13},{6,14},{7,15},{8,0},{9,1},... | collective-permute-start | bytes 196616 | tf_op jit(solution)/shard_map/ppermute | solution.py:23
  34.9 9.0 %collective-permute-start.17 = (f32[2,32,256]{2,1,0:T(8,128)S(1)}, f32[2,32,256]{2,1,0:T(8,128)S(1)}, u32[]{:S(2)}, u32[]{:S(2)}) collective-permute-start(f32[2,32,256]{2,1,0:T(8,128)S(1)} %shard_map.24), channel_id=1, source_target_pairs={{0,16},{1,17},{2,18},{3,19},{4,20},{5,21},{6,22},{7,23},{8,24},{9,... | collective-permute-start | bytes 196616 | tf_op jit(solution)/shard_map/ppermute | solution.py:18
  43.9 6.7 %collective-permute-start.20 = (f32[2,32,256]{2,1,0:T(8,128)S(1)}, f32[2,32,256]{2,1,0:T(8,128)S(1)}, u32[]{:S(2)}, u32[]{:S(2)}) collective-permute-start(f32[2,32,256]{2,1,0:T(8,128)S(1)} %collective-permute-done.17.refs_0_), channel_id=1, source_target_pairs={{0,1},{1,0},{2,3},{3,2},{4,5},{5,4},{6,7},{7,6},{8,9},{9,8},{10,11... | collective-permute-start | bytes 196616 | tf_op jit(solution)/shard_map/ppermute | solution.py:28
  44.6 6.0 %collective-permute-start.19 = (f32[2,32,256]{2,1,0:T(8,128)S(1)}, f32[2,32,256]{2,1,0:T(8,128)S(1)}, u32[]{:S(2)}, u32[]{:S(2)}) collective-permute-start(f32[2,32,256]{2,1,0:T(8,128)S(1)} %collective-permute-done.17.refs_0_), channel_id=1, source_target_pairs={{0,1},{1,0},{2,3},{3,2},{4,5},{5,4},{6,7},{7,6},{8,9},{9,8},{10,11... | collective-permute-start | bytes 196616 | tf_op jit(solution)/shard_map/ppermute | solution.py:28
  45.2 5.4 %collective-permute-start.18 = (f32[2,32,256]{2,1,0:T(8,128)S(1)}, f32[2,32,256]{2,1,0:T(8,128)S(1)}, u32[]{:S(2)}, u32[]{:S(2)}) collective-permute-start(f32[2,32,256]{2,1,0:T(8,128)S(1)} %collective-permute-done.17.refs_0_), channel_id=1, source_target_pairs={{0,1},{1,0},{2,3},{3,2},{4,5},{5,4},{6,7},{7,6},{8,9},{9,8},{10,11... | collective-permute-start | bytes 196616 | tf_op jit(solution)/shard_map/ppermute | solution.py:28
  46.6 8.6 %collective-permute-start.24 = (f32[256,256]{1,0:T(8,128)S(1)}, f32[256,256]{1,0:T(8,128)S(1)}, u32[]{:S(2)}, u32[]{:S(2)}) collective-permute-start(f32[256,256]{1,0:T(8,128)S(1)} %collective-permute-done.1.next_ref), channel_id=1, source_target_pairs={{24,31}} | collective-permute-start | bytes 786440 | tf_op jit(solution)/shard_map/ppermute | solution.py:41
  47.9 9.2 %collective-permute-start.23 = (f32[2,128,256]{2,1,0:T(8,128)S(1)}, f32[2,128,256]{2,1,0:T(8,128)S(1)}, u32[]{:S(2)}, u32[]{:S(2)}) collective-permute-start(f32[2,128,256]{2,1,0:T(8,128)S(1)} %collective-permute-done.22.mine_ref), channel_id=1, source_target_pairs={{0,1},{1,0},{2,3},{3,2},{4,5},{5,4},{6,7},{7,6},{8,9},{9,8},{10,11... | collective-permute-start | bytes 786440 | tf_op jit(solution)/shard_map/ppermute | solution.py:18
  50.6 7.8 %collective-permute-start.21 = (f32[4,2,32,256]{3,2,1,0:T(8,128)S(1)}, f32[4,2,32,256]{3,2,1,0:T(8,128)S(1)}, u32[]{:S(2)}, u32[]{:S(2)}) collective-permute-start(f32[4,2,32,256]{3,2,1,0:T(8,128)S(1)} %shard_map.25.mine_ref), channel_id=1, source_target_pairs={{0,1},{1,0},{2,3},{3,2},{4,5},{5,4},{6,7},{7,6},{8,9},{9,8},{10,11... | collective-permute-start | bytes 786440 | tf_op jit(solution)/shard_map/ppermute | solution.py:18

commit v5 on v4

--- a/solution.py
+++ b/solution.py
@@ -66,6 +66,18 @@
     by_real = dot(high, rrh, turned) + (dot(high, rrl, turned) + dot(low, rrh, turned))
     by_imag = dot(high, rih, turned) + (dot(high, ril, turned) + dot(low, rih, turned))
     return by_real[:rows] - by_imag[rows:], by_imag[:rows] + by_real[rows:]
+
+
+def columns_product(left, right):
+    high, low = right
+    width = high.shape[1] // 2
+
+    def real(k):
+        by_high = dot(left[0][k], high, False) + dot(left[1][k], high, False)
+        return by_high + dot(left[0][k], low, False)
+
+    by_real, by_imag = real(0), real(1)
+    return by_real[:, :width] - by_imag[:, width:], by_real[:, width:] + by_imag[:, :width]
 
 
 def call(kernel, outs, scratch, flops, *args, aliases={}, places=None, out_places=None):
@@ -250,10 +262,6 @@
     return out
 
 
-def summed(high, low):
-    return high.astype(jnp.float32) + low.astype(jnp.float32)
-
-
 def total_kernel(axis, level, *refs):
     pieces, (row_high_ref, row_low_ref) = refs[:4], refs[6:8]
     slice_ref, high_ref, low_ref, room_ref = refs[8:]
@@ -275,17 +283,37 @@
         value = product(get(high_ref, low_ref, 0, rows), get(high_ref, low_ref, 1))
         store(slice_ref, product(halves(value), row))
 
+    begin = (me & (parts - 1)) * slice_ref.shape[1]
+    width = room_ref.shape[0]
+    block = pl.ds(pl.multiple_of(begin // width * width, width), width)
+
+    def columns(high, low):
+        return (
+            jnp.concatenate([high[0], high[1]], axis=1),
+            jnp.concatenate([low[0], low[1]], axis=1),
+        )
+
+    def put(first, second, right):
+        grown = columns_product(first, right)
+        grown = columns_product(second, columns(*zip(split(grown[0]), split(grown[1]))))
+        inside = pl.ds(pl.multiple_of(begin % width, slice_ref.shape[1]), slice_ref.shape[1])
+        for k in range(2):
+            room_ref[...] = grown[k].T
+            slice_ref[k] = room_ref[inside, :]
+
     @pl.when((upper == 1) & (second_row == 1))
     def _():
-        value = own_turned(me, slice_ref.shape[1], lambda k, c: summed(row_high_ref[k, :, c], row_low_ref[k, :, c]), room_ref)
-        value = product(halves(value), get(high_ref, low_ref, 1), True)
-        store(slice_ref, product(halves(value), get(high_ref, low_ref, 0), True))
+        right = columns(
+            [row_high_ref[k, :, block] for k in range(2)], [row_low_ref[k, :, block] for k in range(2)]
+        )
+        put(get(high_ref, low_ref, 1), get(high_ref, low_ref, 0), right)
 
     @pl.when((upper == 1) & (second_row == 0))
     def _():
-        value = own_turned(me, slice_ref.shape[1], lambda k, c: summed(high_ref[3, k, :, c], low_ref[3, k, :, c]), room_ref)
-        value = product(halves(value), get(high_ref, low_ref, 2), True)
-        store(slice_ref, product(halves(value), row, True))
+        right = columns(
+            [high_ref[3, k, :, block] for k in range(2)], [low_ref[3, k, :, block] for k in range(2)]
+        )
+        put(get(high_ref, low_ref, 2), row, right)
 
 
 def prefix_kernel(axis, high_ref, low_ref, own_ref, other_ref, total_ref, local_ref, half_ref):
@@ -380,24 +408,32 @@
         refs[4][place] = ref[...]
 
 
-def assemble(axis, mine_ref, twin_ref, whole_ref):
-    me = lax.axis_index(axis)
-    for other, ref in enumerate((mine_ref, twin_ref)):
-        for place in range(4):
-            rows = own_rows(me ^ (2 * place + other), ref.shape[2])
-            store(whole_ref, (ref[place, 0], ref[place, 1]), rows)
-
-
 def local_kernel(axis, level, mine_ref, twin_ref, local_ref, late_ref, out_ref, high_ref, low_ref, whole_ref, sent):
     me = lax.axis_index(axis)
-    half = mine_ref.shape[1]
+    half, size = mine_ref.shape[1], local_ref.shape[-1]
     upper = (me // level) & 1
     block = (me // level) & 3
     last = me == lax.axis_size(axis) - 1
 
-    @pl.when(upper == 0)
-    def _():
-        store(whole_ref, [local_ref[k].T for k in range(2)])
+    def give(pair):
+        for k, (high, low) in enumerate(thirds(pair)):
+            high_ref[k] = high
+            low_ref[k] = low
+
+    def finish(pair):
+        store(whole_ref, [part.T for part in pair])
+        copy = pltpu.make_async_copy(whole_ref, out_ref.at[0], sent)
+        copy.start()
+        copy.wait()
+
+    @pl.when(block == 0)
+    def _():
+        finish(load(local_ref))
+
+    @pl.when(block == 2)
+    def _():
+        order = [own_rows(me ^ mask, size // parts) for mask in (0, 2, 4, 6, 1, 3, 5, 7)]
+        give([jnp.concatenate([local_ref[k, rows, :] for rows in order], axis=0).T for k in range(2)])
 
     @pl.when(upper == 1)
     def _():
@@ -405,56 +441,77 @@
         store(whole_ref, load(twin_ref), core_rows(me ^ 1, half))
         grown = three_products(thirds(load(whole_ref)), thirds(load(local_ref)))
 
-        @pl.when(jnp.logical_not(last))
+        @pl.when(block == 1)
         def _():
-            store(whole_ref, [grown[k].T for k in range(2)])
+            finish(grown)
+
+        @pl.when((block == 3) & jnp.logical_not(last))
+        def _():
+            give(grown)
 
         @pl.when(last)
         def _():
-            ended = three_products(thirds(grown), thirds(load(late_ref)))
-            store(whole_ref, [ended[k].T for k in range(2)])
-
-    @pl.when(block < 2)
-    def _():
-        copy = pltpu.make_async_copy(whole_ref, out_ref.at[0], sent)
+            give(three_products(thirds(grown), thirds(load(late_ref))))
+
+
+def joined_pair(ref):
+    return [ref[:, k].reshape(-1, ref.shape[-1]) for k in range(2)]
+
+
+def early_kernel(axis, level, mine_ref, high_ref, low_ref, part_ref):
+    block = (lax.axis_index(axis) // level) & 3
+    half = part_ref.shape[1] // 2
+
+    @pl.when(block == 2)
+    def _():
+        left = [(high_ref[k, :, :half], low_ref[k, :, :half]) for k in range(3)]
+        store(part_ref, three_products(left, thirds(joined_pair(mine_ref))))
+
+    @pl.when(block == 3)
+    def _():
+        right = [(high_ref[k], low_ref[k]) for k in range(3)]
+        store(part_ref, three_products(thirds(joined_pair(mine_ref)), right), pl.ds(0, half))
+
+
+def final_kernel(axis, level, part_ref, twin_ref, high_ref, low_ref, done_ref, out_ref, whole_ref, result_ref, sent):
+    me = lax.axis_index(axis)
+    block = (me // level) & 3
+    size = whole_ref.shape[1]
+    half = size // 2
+    spans = [pl.ds(0, half), pl.ds(half, half)]
+
+    def send(step):
+        copy = pltpu.make_async_copy(result_ref.at[:, spans[step]], out_ref.at[0, :, spans[step]], sent.at[step])
         copy.start()
-        copy.wait()
-
-    @pl.when(block >= 2)
-    def _():
-        for k, (high, low) in enumerate(thirds(load(whole_ref))):
-            high_ref[k] = high
-            low_ref[k] = low
-
-
-def final_kernel(axis, level, mine_ref, twin_ref, high_ref, low_ref, done_ref, out_ref, whole_ref, result_ref, sent):
-    block = (lax.axis_index(axis) // level) & 3
-    steps = sent.shape[0]
-    count = whole_ref.shape[1] // steps
-
-    def put(turned):
-        assemble(axis, mine_ref, twin_ref, whole_ref)
-        whole = load(whole_ref)
-        right = thirds([part.T for part in whole] if turned else whole)
+        return copy
+
+    @pl.when(block == 2)
+    def _():
+        right = thirds(joined_pair(twin_ref))
         copies = []
-        for step in range(steps):
-            rows = pl.ds(step * count, count)
-            left = [(high_ref[k, rows, :], low_ref[k, rows, :]) for k in range(3)]
-            store(result_ref, three_products(left, right), rows)
-            copies.append(
-                pltpu.make_async_copy(result_ref.at[:, rows], out_ref.at[0, :, rows], sent.at[step])
-            )
-            copies[-1].start()
+        for step, rows in enumerate(spans):
+            left = [(high_ref[k, rows, half:], low_ref[k, rows, half:]) for k in range(3)]
+            grown = three_products(left, right)
+            store(result_ref, [part_ref[k, rows, :] + grown[k] for k in range(2)], rows)
+            copies.append(send(step))
         for copy in copies:
             copy.wait()
 
-    @pl.when(block == 2)
-    def _():
-        put(False)
-
     @pl.when(block == 3)
     def _():
-        put(True)
+        right = [(high_ref[k], low_ref[k]) for k in range(3)]
+        grown = three_products(thirds(joined_pair(twin_ref)), right)
+        count = size // parts
+        for place in range(4):
+            rows = slice(place * count, (place + 1) * count)
+            store(whole_ref, load(part_ref, rows), own_rows(me ^ (2 * place), count))
+            store(whole_ref, [part[rows] for part in grown], own_rows(me ^ (2 * place + 1), count))
+        copies = []
+        for step, columns in enumerate(spans):
+            store(result_ref, [whole_ref[k, :, columns].T for k in range(2)], columns)
+            copies.append(send(step))
+        for copy in copies:
+            copy.wait()
 
 
 def plane_slices(mine, axis, level):
@@ -556,12 +613,15 @@
         late,
         out_places=(pl.ANY, pltpu.VMEM, pltpu.VMEM),
     )
+    joined, twin = plane_slices(below, axis, level)
+    early = call(functools.partial(early_kernel, axis, level), whole, [], cube, joined, high, low)
     return call(
         functools.partial(final_kernel, axis, level),
         out_shape,
         room + room + [pltpu.SemaphoreType.DMA((2,))],
-        3 * cube,
-        *plane_slices(below, axis, level),
+        2 * cube,
+        early,
+        twin,
         high,
         low,
         out,

time: 60 us -> 59.8 us (level)
    pallas_call x12 -> x13, Pallas kernels: 12.1 us -> 11.9 us  [call(): pl.pallas_call(kernel, out_shape=outs, in_specs=in_specs, out_specs=out_s...]
where the time goes in v5:
time: 59.8 us; the launch traced here: 59.6 us
  starting transfers between devices  30.5 us (51%)
  waiting for transfers between devices  16.1 us (27%)
  Pallas kernels  11.9 us (20%)
  local copies, waits for them, and re-layouts  1.04 us (2%)
    ppermute x19, starting transfers between devices, exchanged(): return lax.ppermute(x, axis, [(i, i ^ mask) for i in range(size)])  24.6 us
    pallas_call x13, Pallas kernels, call(): pl.pallas_call(kernel, out_shape=outs, in_specs=in_specs, out_specs=out_s...  11.9 us
    ppermute x19, waiting for transfers between devices, exchanged(): return lax.ppermute(x, axis, [(i, i ^ mask) for i in range(size)])  7.47 us
    ppermute x1, waiting for transfers between devices, from_next(): return lax.ppermute(x, axis, sorted(target.items()))  5.16 us
    ppermute x3, starting transfers between devices, upper_exchanged(): lax.ppermute(x, axis, [(i, i ^ (mask if i // level & 2 else 1)) for i in...  2.65 us
    ppermute x1, waiting for transfers between devices, to_last(): return lax.ppermute(x, axis, [(size - plane, size - 1)])  2.52 us
    ppermute x1, starting transfers between devices, to_last(): return lax.ppermute(x, axis, [(size - plane, size - 1)])  1.28 us
  transfers between devices with their start and end apart: 25, of which 10 were waited for; matrix products, arithmetic and copies ran while one was open for 0% of the time, Pallas kernels for 8%

profile of v5, /device:TPU:31, one launch (start us, length us, event | category | flops | bytes accessed | tf_op | source)
XLA Modules:
  0.0 59.6 jit_solution(18130958265015500933)
XLA Ops:
  0.0 1.0 %copy-done = f32[1,2,256,256]{3,2,1,0:T(8,128)S(1)} copy-done((f32[1,2,256,256]{3,2,1,0:T(8,128)S(1)}, f32[1,2,256,256]{3,2,1,0:T(8,128)}, u32[]{:S(2)}) %copy-start) | copy-done | bytes 524312
  1.2 0.7 %collective-permute-start.1 = (f32[256,256]{1,0:T(8,128)S(1)}, f32[256,256]{1,0:T(8,128)S(1)}, u32[]{:S(2)}, u32[]{:S(2)}) collective-permute-start(f32[256,256]{1,0:T(8,128)S(1)} %shard_map.17.packed_ref), channel_id=1, source_target_pairs={{0,24},{1,0},{2,1},{3,2},{4,3},{5,4},{6,5},{7,6},{8,7},{9,8},{10,9... | collective-permute-start | bytes 786440 | tf_op jit(solution)/shard_map/ppermute | solution.py:36
  2.2 5.2 %collective-permute-done.1.next_ref = f32[256,256]{1,0:T(8,128)S(1)} collective-permute-done((f32[256,256]{1,0:T(8,128)S(1)}, f32[256,256]{1,0:T(8,128)S(1)}, u32[]{:S(2)}, u32[]{:S(2)}) %collective-permute-start.1) | collective-permute-done | bytes 262176 | tf_op jit(solution)/shard_map/ppermute | solution.py:36
  7.4 1.9 %shard_map.19.own_ref = f32[2,256,256]{2,1,0:T(8,128)S(1)} custom-call(f32[2,256,256]{2,1,0:T(8,128)S(1)} %get-tuple-element.24.parts_ref, bf16[3,256,256]{2,1,0:T(8,128)(2,1)S(1)} %get-tuple-element.25.high_ref, bf16[3,256,256]{2,1,0:T(8,128)(2,1)S(1)} %get-tuple-element.26.low_ref, f32[256,256]{1,0:T(8,128)S(1)} %collective-permute-done.pair_ref, ...), custom_call_target="tpu_custom_call" | custom-call | flops 1207959552 | bytes 2359296 | tf_op jit(solution)/shard_map/pallas_call | solution.py:89
  9.4 1.9 %collective-permute-done.2.other_ref = f32[2,256,256]{2,1,0:T(8,128)S(1)} collective-permute-done((f32[2,256,256]{2,1,0:T(8,128)S(1)}, f32[2,256,256]{2,1,0:T(8,128)S(1)}, u32[]{:S(2)}, u32[]{:S(2)}) %collective-permute-start.2) | collective-permute-done | bytes 524320 | tf_op jit(solution)/shard_map/ppermute | solution.py:18
  11.7 2.8 %collective-permute-start.3 = (f32[128,256]{1,0:T(8,128)S(1)}, f32[128,256]{1,0:T(8,128)S(1)}, u32[]{:S(2)}, u32[]{:S(2)}) collective-permute-start(f32[128,256]{1,0:T(8,128)S(1)} %get-tuple-element.27), channel_id=1, source_target_pairs={{0,4},{1,5},{2,6},{3,7},{4,0},{5,1},{6,2},{7,3},{8,12},{9,13},{10,... | collective-permute-start | bytes 393224 | tf_op jit(solution)/shard_map/ppermute | solution.py:18
  14.7 1.9 %collective-permute-done.10.refs_2_ = f32[128,256]{1,0:T(8,128)S(1)} collective-permute-done((f32[128,256]{1,0:T(8,128)S(1)}, f32[128,256]{1,0:T(8,128)S(1)}, u32[]{:S(2)}, u32[]{:S(2)}) %collective-permute-start.10) | collective-permute-done | bytes 131104 | tf_op jit(solution)/shard_map/ppermute | solution.py:18
  16.6 1.0 %collective-permute-start.11 = (f32[128,256]{1,0:T(8,128)S(1)}, f32[128,256]{1,0:T(8,128)S(1)}, u32[]{:S(2)}, u32[]{:S(2)}) collective-permute-start(f32[128,256]{1,0:T(8,128)S(1)} %collective-permute-done.10.refs_2_), channel_id=1, source_target_pairs={{0,1},{1,0},{2,3},{3,2},{4,5},{5,4},{6,7},{7,6},{8,9},{9,8},{10,11... | collective-permute-start | bytes 393224 | tf_op jit(solution)/shard_map/ppermute | solution.py:18
  17.8 2.1 %collective-permute-start.13 = (f32[128,256]{1,0:T(8,128)S(1)}, f32[128,256]{1,0:T(8,128)S(1)}, u32[]{:S(2)}, u32[]{:S(2)}) collective-permute-start(f32[128,256]{1,0:T(8,128)S(1)} %collective-permute-done.3.refs_6_), channel_id=1, source_target_pairs={{0,1},{1,0},{2,3},{3,2},{4,5},{5,4},{6,7},{7,6},{8,9},{9,8},{10,11... | collective-permute-start | bytes 393224 | tf_op jit(solution)/shard_map/ppermute | solution.py:18
  19.9 0.7 %collective-permute-done.14.refs_8_ = f32[128,256]{1,0:T(8,128)S(1)} collective-permute-done((f32[128,256]{1,0:T(8,128)S(1)}, f32[128,256]{1,0:T(8,128)S(1)}, u32[]{:S(2)}, u32[]{:S(2)}) %collective-permute-start.14) | collective-permute-done | bytes 131104 | tf_op jit(solution)/shard_map/ppermute | solution.py:18
  20.6 1.5 %collective-permute-start.7 = (f32[128,256]{1,0:T(8,128)S(1)}, f32[128,256]{1,0:T(8,128)S(1)}, u32[]{:S(2)}, u32[]{:S(2)}) collective-permute-start(f32[128,256]{1,0:T(8,128)S(1)} %collective-permute-done.6.refs_4_), channel_id=1, source_target_pairs={{0,4},{1,5},{2,6},{3,7},{4,0},{5,1},{6,2},{7,3},{8,12},{9,13},{10,... | collective-permute-start | bytes 393224 | tf_op jit(solution)/shard_map/ppermute | solution.py:18
  22.1 1.8 %collective-permute-start.15 = (f32[128,256]{1,0:T(8,128)S(1)}, f32[128,256]{1,0:T(8,128)S(1)}, u32[]{:S(2)}, u32[]{:S(2)}) collective-permute-start(f32[128,256]{1,0:T(8,128)S(1)} %collective-permute-done.14.refs_8_), channel_id=1, source_target_pairs={{0,1},{1,0},{2,3},{3,2},{4,5},{5,4},{6,7},{7,6},{8,9},{9,8},{10,11... | collective-permute-start | bytes 393224 | tf_op jit(solution)/shard_map/ppermute | solution.py:18
  24.0 0.4 collective-permute-done.4.refs_0_
  24.4 2.4 %collective-permute-start.5 = (f32[128,256]{1,0:T(8,128)S(1)}, f32[128,256]{1,0:T(8,128)S(1)}, u32[]{:S(2)}, u32[]{:S(2)}) collective-permute-start(f32[128,256]{1,0:T(8,128)S(1)} %collective-permute-done.4.refs_0_), channel_id=1, source_target_pairs={{0,1},{1,0},{2,3},{3,2},{4,5},{5,4},{6,7},{7,6},{8,9},{9,8},{10,11... | collective-permute-start | bytes 393224 | tf_op jit(solution)/shard_map/ppermute | solution.py:18
  27.2 0.8 %shard_map.21 = (bf16[4,2,256,256]{3,2,1,0:T(8,128)(2,1)S(1)}, bf16[4,2,256,256]{3,2,1,0:T(8,128)(2,1)S(1)}, bf16[2,256,256]{2,1,0:T(8,128)(2,1)S(1)}, bf16[2,256,256]{2,1,0:T(8,128)(2,1)S(1)}) custom-call(f32[2,128,256]{2,1,0:T(8,128)S(1)} %get-tuple-element.29.refs_0_, f32[2,128,256]{2,1,0:T(8,128)S(1)} %collective-permute-done.9.refs_1_, ...), custom_call_target="tpu_custom_call" | custom-call | flops 402653184 | bytes 4194304 | tf_op jit(solution)/shard_map/pallas_call | solution.py:89
  28.2 0.9 %shard_map.22 = (f32[2,32,256]{2,1,0:T(8,128)S(1)}, bf16[4,2,256,256]{3,2,1,0:T(8,128)(2,1)S(1)}, bf16[4,2,256,256]{3,2,1,0:T(8,128)(2,1)S(1)}) custom-call(f32[128,256]{1,0:T(8,128)S(1)} %collective-permute-done.4.refs_0_, f32[128,256]{1,0:T(8,128)S(1)} %collective-permute-done.5.refs_1_, ...), custom_call_target="tpu_custom_call", output_to_operand_aliasing={{1}: (4, {}), {2}: (5, {})} | custom-call | flops 134217728 | bytes 5308416 | tf_op jit(solution)/shard_map/pallas_call | solution.py:89
  29.1 2.4 %shard_map.23 = (f32[2,256,256]{2,1,0:T(8,128)S(1)}, f32[2,256,256]{2,1,0:T(8,128)S(1)}, f32[2,128,256]{2,1,0:T(8,128)S(1)}) custom-call(bf16[4,2,256,256]{3,2,1,0:T(8,128)(2,1)S(1)} %get-tuple-element.35.high_ref, bf16[4,2,256,256]{3,2,1,0:T(8,128)(2,1)S(1)} %get-tuple-element.36.low_ref, f32[2,256,256]{2,1,0:T(8,128)S(1)} %shard_map.19.own_ref, ...), custom_call_target="tpu_custom_call" | custom-call | flops 1610612736 | bytes 4456448 | tf_op jit(solution)/shard_map/pallas_call | solution.py:89
  31.5 1.0 %collective-permute-start.21 = (f32[2,128,256]{2,1,0:T(8,128)S(1)}, f32[2,128,256]{2,1,0:T(8,128)S(1)}, u32[]{:S(2)}, u32[]{:S(2)}) collective-permute-start(f32[2,128,256]{2,1,0:T(8,128)S(1)} %get-tuple-element.38), channel_id=1, source_target_pairs={{0,8},{1,9},{2,10},{3,11},{4,12},{5,13},{6,14},{7,15},{8,0},{9,1},... | collective-permute-start | bytes 786440 | tf_op jit(solution)/shard_map/ppermute | solution.py:18
  32.5 1.2 %collective-permute-start.16 = (f32[2,32,256]{2,1,0:T(8,128)S(1)}, f32[2,32,256]{2,1,0:T(8,128)S(1)}, u32[]{:S(2)}, u32[]{:S(2)}) collective-permute-start(f32[2,32,256]{2,1,0:T(8,128)S(1)} %get-tuple-element.34), channel_id=1, source_target_pairs={{0,8},{1,9},{2,10},{3,11},{4,12},{5,13},{6,14},{7,15},{8,0},{9,1},... | collective-permute-start | bytes 196616 | tf_op jit(solution)/shard_map/ppermute | solution.py:23
  33.7 0.9 %collective-permute-done.16.came_ref = f32[2,32,256]{2,1,0:T(8,128)S(1)} collective-permute-done((f32[2,32,256]{2,1,0:T(8,128)S(1)}, f32[2,32,256]{2,1,0:T(8,128)S(1)}, u32[]{:S(2)}, u32[]{:S(2)}) %collective-permute-start.16) | collective-permute-done | bytes 65568 | tf_op jit(solution)/shard_map/ppermute | solution.py:23
  34.9 6.4 %collective-permute-start.17 = (f32[2,32,256]{2,1,0:T(8,128)S(1)}, f32[2,32,256]{2,1,0:T(8,128)S(1)}, u32[]{:S(2)}, u32[]{:S(2)}) collective-permute-start(f32[2,32,256]{2,1,0:T(8,128)S(1)} %shard_map.24), channel_id=1, source_target_pairs={{0,16},{1,17},{2,18},{3,19},{4,20},{5,21},{6,22},{7,23},{8,24},{9,... | collective-permute-start | bytes 196616 | tf_op jit(solution)/shard_map/ppermute | solution.py:18
  41.3 2.2 %collective-permute-done.17.refs_0_ = f32[2,32,256]{2,1,0:T(8,128)S(1)} collective-permute-done((f32[2,32,256]{2,1,0:T(8,128)S(1)}, f32[2,32,256]{2,1,0:T(8,128)S(1)}, u32[]{:S(2)}, u32[]{:S(2)}) %collective-permute-start.17) | collective-permute-done | bytes 65568 | tf_op jit(solution)/shard_map/ppermute | solution.py:18
  43.5 0.9 %collective-permute-start.20 = (f32[2,32,256]{2,1,0:T(8,128)S(1)}, f32[2,32,256]{2,1,0:T(8,128)S(1)}, u32[]{:S(2)}, u32[]{:S(2)}) collective-permute-start(f32[2,32,256]{2,1,0:T(8,128)S(1)} %collective-permute-done.17.refs_0_), channel_id=1, source_target_pairs={{0,1},{1,0},{2,3},{3,2},{4,5},{5,4},{6,7},{7,6},{8,9},{9,8},{10,11... | collective-permute-start | bytes 196616 | tf_op jit(solution)/shard_map/ppermute | solution.py:28
  44.4 0.4 collective-permute-start.19
  44.8 1.4 %collective-permute-start.18 = (f32[2,32,256]{2,1,0:T(8,128)S(1)}, f32[2,32,256]{2,1,0:T(8,128)S(1)}, u32[]{:S(2)}, u32[]{:S(2)}) collective-permute-start(f32[2,32,256]{2,1,0:T(8,128)S(1)} %collective-permute-done.17.refs_0_), channel_id=1, source_target_pairs={{0,1},{1,0},{2,3},{3,2},{4,5},{5,4},{6,7},{7,6},{8,9},{9,8},{10,11... | collective-permute-start | bytes 196616 | tf_op jit(solution)/shard_map/ppermute | solution.py:28
  46.1 1.3 %collective-permute-start.23 = (f32[256,256]{1,0:T(8,128)S(1)}, f32[256,256]{1,0:T(8,128)S(1)}, u32[]{:S(2)}, u32[]{:S(2)}) collective-permute-start(f32[256,256]{1,0:T(8,128)S(1)} %collective-permute-done.1.next_ref), channel_id=1, source_target_pairs={{24,31}} | collective-permute-start | bytes 786440 | tf_op jit(solution)/shard_map/ppermute | solution.py:41
  47.4 2.9 %collective-permute-start.22 = (f32[2,128,256]{2,1,0:T(8,128)S(1)}, f32[2,128,256]{2,1,0:T(8,128)S(1)}, u32[]{:S(2)}, u32[]{:S(2)}) collective-permute-start(f32[2,128,256]{2,1,0:T(8,128)S(1)} %collective-permute-done.21.mine_ref), channel_id=1, source_target_pairs={{0,1},{1,0},{2,3},{3,2},{4,5},{5,4},{6,7},{7,6},{8,9},{9,8},{10,11... | collective-permute-start | bytes 786440 | tf_op jit(solution)/shard_map/ppermute | solution.py:18
  50.4 1.9 %collective-permute-start.24 = (f32[4,2,32,256]{3,2,1,0:T(8,128)S(1)}, f32[4,2,32,256]{3,2,1,0:T(8,128)S(1)}, u32[]{:S(2)}, u32[]{:S(2)}) collective-permute-start(f32[4,2,32,256]{3,2,1,0:T(8,128)S(1)} %shard_map.25.mine_ref), channel_id=1, source_target_pairs={{0,1},{1,0},{2,3},{3,2},{4,5},{5,4},{6,7},{7,6},{8,9},{9,8},{10,11... | collective-permute-start | bytes 786440 | tf_op jit(solution)/shard_map/ppermute | solution.py:18
  52.3 2.5 %collective-permute-done.23.next_ref = f32[256,256]{1,0:T(8,128)S(1)} collective-permute-done((f32[256,256]{1,0:T(8,128)S(1)}, f32[256,256]{1,0:T(8,128)S(1)}, u32[]{:S(2)}, u32[]{:S(2)}) %collective-permute-start.23) | collective-permute-done | bytes 262176 | tf_op jit(solution)/shard_map/ppermute | solution.py:41
  54.8 1.9 %shard_map.26.late_ref = f32[2,256,256]{2,1,0:T(8,128)S(1)} custom-call(f32[2,256,256]{2,1,0:T(8,128)S(1)} %get-tuple-element.24.parts_ref, bf16[3,256,256]{2,1,0:T(8,128)(2,1)S(1)} %get-tuple-element.25.high_ref, bf16[3,256,256]{2,1,0:T(8,128)(2,1)S(1)} %get-tuple-element.26.low_ref, f32[256,256]{1,0:T(8,128)S(1)} %collective-permute-done.23.next_ref), custom_call_target="tpu_custom_call" | custom-call | flops 134217728 | bytes 2097152 | tf_op jit(solution)/shard_map/pallas_call | solution.py:89
  56.8 1.2 %shard_map.27 = (f32[1,2,256,256]{3,2,1,0:T(8,128)}, bf16[3,256,256]{2,1,0:T(8,128)(2,1)S(1)}, bf16[3,256,256]{2,1,0:T(8,128)(2,1)S(1)}) custom-call(f32[2,128,256]{2,1,0:T(8,128)S(1)} %collective-permute-done.21.mine_ref, f32[2,128,256]{2,1,0:T(8,128)S(1)} %collective-permute-done.22.twin_ref, f32[2,256,256]{2,1,0:T(8,128)S(1)} %get-tuple-element.39.local_ref, ...), custom_call_target="tpu_custom_call" | custom-call | flops 402653184 | bytes 2883584 | tf_op jit(solution)/shard_map/pallas_call | solution.py:89
  58.3 1.3 %shard_map.29 = f32[1,2,256,256]{3,2,1,0:T(8,128)} custom-call(f32[2,256,256]{2,1,0:T(8,128)S(1)} %shard_map.28.part_ref, f32[4,2,32,256]{3,2,1,0:T(8,128)S(1)} %collective-permute-done.24.twin_ref, bf16[3,256,256]{2,1,0:T(8,128)(2,1)S(1)} %get-tuple-element.40.high_ref, ...), custom_call_target="tpu_custom_call", output_to_operand_aliasing={{}: (4, {})} | custom-call | flops 268435456 | bytes 2621440 | tf_op jit(solution)/shard_map/pallas_call | solution.py:89
  (33 shorter events, 2.6 us)
Async XLA Ops:
  0.0 1.0 %copy-start = (f32[1,2,256,256]{3,2,1,0:T(8,128)S(1)}, f32[1,2,256,256]{3,2,1,0:T(8,128)}, u32[]{:S(2)}) copy-start(f32[1,2,256,256]{3,2,1,0:T(8,128)} %drawn_ref.1) | copy-start | bytes 1572868
  1.2 6.2 %collective-permute-start.1 = (f32[256,256]{1,0:T(8,128)S(1)}, f32[256,256]{1,0:T(8,128)S(1)}, u32[]{:S(2)}, u32[]{:S(2)}) collective-permute-start(f32[256,256]{1,0:T(8,128)S(1)} %shard_map.17.packed_ref), channel_id=1, source_target_pairs={{0,24},{1,0},{2,1},{3,2},{4,3},{5,4},{6,5},{7,6},{8,7},{9,8},{10,9... | collective-permute-start | bytes 786440 | tf_op jit(solution)/shard_map/ppermute | solution.py:36
  1.9 5.4 %collective-permute-start = (f32[256,256]{1,0:T(8,128)S(1)}, f32[256,256]{1,0:T(8,128)S(1)}, u32[]{:S(2)}, u32[]{:S(2)}) collective-permute-start(f32[256,256]{1,0:T(8,128)S(1)} %shard_map.17.packed_ref), channel_id=1, source_target_pairs={{0,1},{1,0},{2,3},{3,2},{4,5},{5,4},{6,7},{7,6},{8,9},{9,8},{10,11... | collective-permute-start | bytes 786440 | tf_op jit(solution)/shard_map/ppermute | solution.py:18
  9.3 2.0 %collective-permute-start.2 = (f32[2,256,256]{2,1,0:T(8,128)S(1)}, f32[2,256,256]{2,1,0:T(8,128)S(1)}, u32[]{:S(2)}, u32[]{:S(2)}) collective-permute-start(f32[2,256,256]{2,1,0:T(8,128)S(1)} %shard_map.19.own_ref), channel_id=1, source_target_pairs={{0,1},{1,0},{2,3},{3,2},{4,5},{5,4},{6,7},{7,6},{8,9},{9,8},{10,11... | collective-permute-start | bytes 1572872 | tf_op jit(solution)/shard_map/ppermute | solution.py:18
  11.7 5.0 %collective-permute-start.10 = (f32[128,256]{1,0:T(8,128)S(1)}, f32[128,256]{1,0:T(8,128)S(1)}, u32[]{:S(2)}, u32[]{:S(2)}) collective-permute-start(f32[128,256]{1,0:T(8,128)S(1)} %get-tuple-element.27), channel_id=1, source_target_pairs={{0,2},{1,3},{2,0},{3,1},{4,6},{5,7},{6,4},{7,5},{8,10},{9,11},{10,... | collective-permute-start | bytes 393224 | tf_op jit(solution)/shard_map/ppermute | solution.py:18
  11.7 6.0 %collective-permute-start.3 = (f32[128,256]{1,0:T(8,128)S(1)}, f32[128,256]{1,0:T(8,128)S(1)}, u32[]{:S(2)}, u32[]{:S(2)}) collective-permute-start(f32[128,256]{1,0:T(8,128)S(1)} %get-tuple-element.27), channel_id=1, source_target_pairs={{0,4},{1,5},{2,6},{3,7},{4,0},{5,1},{6,2},{7,3},{8,12},{9,13},{10,... | collective-permute-start | bytes 393224 | tf_op jit(solution)/shard_map/ppermute | solution.py:18
  14.6 6.0 %collective-permute-start.14 = (f32[128,256]{1,0:T(8,128)S(1)}, f32[128,256]{1,0:T(8,128)S(1)}, u32[]{:S(2)}, u32[]{:S(2)}) collective-permute-start(f32[128,256]{1,0:T(8,128)S(1)} %get-tuple-element.28), channel_id=1, source_target_pairs={{0,4},{1,5},{2,6},{3,7},{4,0},{5,1},{6,2},{7,3},{8,12},{9,13},{10,... | collective-permute-start | bytes 393224 | tf_op jit(solution)/shard_map/ppermute | solution.py:18
  14.6 6.1 %collective-permute-start.6 = (f32[128,256]{1,0:T(8,128)S(1)}, f32[128,256]{1,0:T(8,128)S(1)}, u32[]{:S(2)}, u32[]{:S(2)}) collective-permute-start(f32[128,256]{1,0:T(8,128)S(1)} %get-tuple-element.28), channel_id=1, source_target_pairs={{0,2},{1,3},{2,0},{3,1},{4,6},{5,7},{6,4},{7,5},{8,10},{9,11},{10,... | collective-permute-start | bytes 393224 | tf_op jit(solution)/shard_map/ppermute | solution.py:18
  16.6 5.5 %collective-permute-start.11 = (f32[128,256]{1,0:T(8,128)S(1)}, f32[128,256]{1,0:T(8,128)S(1)}, u32[]{:S(2)}, u32[]{:S(2)}) collective-permute-start(f32[128,256]{1,0:T(8,128)S(1)} %collective-permute-done.10.refs_2_), channel_id=1, source_target_pairs={{0,1},{1,0},{2,3},{3,2},{4,5},{5,4},{6,7},{7,6},{8,9},{9,8},{10,11... | collective-permute-start | bytes 393224 | tf_op jit(solution)/shard_map/ppermute | solution.py:18
  17.8 6.2 %collective-permute-start.13 = (f32[128,256]{1,0:T(8,128)S(1)}, f32[128,256]{1,0:T(8,128)S(1)}, u32[]{:S(2)}, u32[]{:S(2)}) collective-permute-start(f32[128,256]{1,0:T(8,128)S(1)} %collective-permute-done.3.refs_6_), channel_id=1, source_target_pairs={{0,1},{1,0},{2,3},{3,2},{4,5},{5,4},{6,7},{7,6},{8,9},{9,8},{10,11... | collective-permute-start | bytes 393224 | tf_op jit(solution)/shard_map/ppermute | solution.py:18
  19.9 7.3 %collective-permute-start.9 = (f32[2,128,256]{2,1,0:T(8,128)S(1)}, f32[2,128,256]{2,1,0:T(8,128)S(1)}, u32[]{:S(2)}, u32[]{:S(2)}) collective-permute-start(f32[2,128,256]{2,1,0:T(8,128)S(1)} %get-tuple-element.29.refs_0_), channel_id=1, source_target_pairs={{0,1},{1,0},{2,3},{3,2},{4,5},{5,4},{6,7},{7,6},{8,9},{9,8},{10,11... | collective-permute-start | bytes 786440 | tf_op jit(solution)/shard_map/ppermute | solution.py:18
  20.6 3.8 %collective-permute-start.4 = (f32[128,256]{1,0:T(8,128)S(1)}, f32[128,256]{1,0:T(8,128)S(1)}, u32[]{:S(2)}, u32[]{:S(2)}) collective-permute-start(f32[128,256]{1,0:T(8,128)S(1)} %collective-permute-done.3.refs_6_), channel_id=1, source_target_pairs={{0,2},{1,3},{2,0},{3,1},{4,6},{5,7},{6,4},{7,5},{8,10},{9,11},{10,... | collective-permute-start | bytes 393224 | tf_op jit(solution)/shard_map/ppermute | solution.py:18
  20.6 6.2 %collective-permute-start.7 = (f32[128,256]{1,0:T(8,128)S(1)}, f32[128,256]{1,0:T(8,128)S(1)}, u32[]{:S(2)}, u32[]{:S(2)}) collective-permute-start(f32[128,256]{1,0:T(8,128)S(1)} %collective-permute-done.6.refs_4_), channel_id=1, source_target_pairs={{0,4},{1,5},{2,6},{3,7},{4,0},{5,1},{6,2},{7,3},{8,12},{9,13},{10,... | collective-permute-start | bytes 393224 | tf_op jit(solution)/shard_map/ppermute | solution.py:18
  22.1 5.0 %collective-permute-start.15 = (f32[128,256]{1,0:T(8,128)S(1)}, f32[128,256]{1,0:T(8,128)S(1)}, u32[]{:S(2)}, u32[]{:S(2)}) collective-permute-start(f32[128,256]{1,0:T(8,128)S(1)} %collective-permute-done.14.refs_8_), channel_id=1, source_target_pairs={{0,1},{1,0},{2,3},{3,2},{4,5},{5,4},{6,7},{7,6},{8,9},{9,8},{10,11... | collective-permute-start | bytes 393224 | tf_op jit(solution)/shard_map/ppermute | solution.py:18
  23.9 3.2 %collective-permute-start.12 = (f32[128,256]{1,0:T(8,128)S(1)}, f32[128,256]{1,0:T(8,128)S(1)}, u32[]{:S(2)}, u32[]{:S(2)}) collective-permute-start(f32[128,256]{1,0:T(8,128)S(1)} %collective-permute-done.6.refs_4_), channel_id=1, source_target_pairs={{0,1},{1,0},{2,3},{3,2},{4,5},{5,4},{6,7},{7,6},{8,9},{9,8},{10,11... | collective-permute-start | bytes 393224 | tf_op jit(solution)/shard_map/ppermute | solution.py:18
  24.4 3.6 %collective-permute-start.5 = (f32[128,256]{1,0:T(8,128)S(1)}, f32[128,256]{1,0:T(8,128)S(1)}, u32[]{:S(2)}, u32[]{:S(2)}) collective-permute-start(f32[128,256]{1,0:T(8,128)S(1)} %collective-permute-done.4.refs_0_), channel_id=1, source_target_pairs={{0,1},{1,0},{2,3},{3,2},{4,5},{5,4},{6,7},{7,6},{8,9},{9,8},{10,11... | collective-permute-start | bytes 393224 | tf_op jit(solution)/shard_map/ppermute | solution.py:18
  26.8 1.4 %collective-permute-start.8 = (f32[128,256]{1,0:T(8,128)S(1)}, f32[128,256]{1,0:T(8,128)S(1)}, u32[]{:S(2)}, u32[]{:S(2)}) collective-permute-start(f32[128,256]{1,0:T(8,128)S(1)} %collective-permute-done.7.refs_2_), channel_id=1, source_target_pairs={{0,1},{1,0},{2,3},{3,2},{4,5},{5,4},{6,7},{7,6},{8,9},{9,8},{10,11... | collective-permute-start | bytes 393224 | tf_op jit(solution)/shard_map/ppermute | solution.py:18
  31.5 15.9 %collective-permute-start.21 = (f32[2,128,256]{2,1,0:T(8,128)S(1)}, f32[2,128,256]{2,1,0:T(8,128)S(1)}, u32[]{:S(2)}, u32[]{:S(2)}) collective-permute-start(f32[2,128,256]{2,1,0:T(8,128)S(1)} %get-tuple-element.38), channel_id=1, source_target_pairs={{0,8},{1,9},{2,10},{3,11},{4,12},{5,13},{6,14},{7,15},{8,0},{9,1},... | collective-permute-start | bytes 786440 | tf_op jit(solution)/shard_map/ppermute | solution.py:18
  32.5 2.1 %collective-permute-start.16 = (f32[2,32,256]{2,1,0:T(8,128)S(1)}, f32[2,32,256]{2,1,0:T(8,128)S(1)}, u32[]{:S(2)}, u32[]{:S(2)}) collective-permute-start(f32[2,32,256]{2,1,0:T(8,128)S(1)} %get-tuple-element.34), channel_id=1, source_target_pairs={{0,8},{1,9},{2,10},{3,11},{4,12},{5,13},{6,14},{7,15},{8,0},{9,1},... | collective-permute-start | bytes 196616 | tf_op jit(solution)/shard_map/ppermute | solution.py:23
  34.9 8.6 %collective-permute-start.17 = (f32[2,32,256]{2,1,0:T(8,128)S(1)}, f32[2,32,256]{2,1,0:T(8,128)S(1)}, u32[]{:S(2)}, u32[]{:S(2)}) collective-permute-start(f32[2,32,256]{2,1,0:T(8,128)S(1)} %shard_map.24), channel_id=1, source_target_pairs={{0,16},{1,17},{2,18},{3,19},{4,20},{5,21},{6,22},{7,23},{8,24},{9,... | collective-permute-start | bytes 196616 | tf_op jit(solution)/shard_map/ppermute | solution.py:18
  43.5 6.9 %collective-permute-start.20 = (f32[2,32,256]{2,1,0:T(8,128)S(1)}, f32[2,32,256]{2,1,0:T(8,128)S(1)}, u32[]{:S(2)}, u32[]{:S(2)}) collective-permute-start(f32[2,32,256]{2,1,0:T(8,128)S(1)} %collective-permute-done.17.refs_0_), channel_id=1, source_target_pairs={{0,1},{1,0},{2,3},{3,2},{4,5},{5,4},{6,7},{7,6},{8,9},{9,8},{10,11... | collective-permute-start | bytes 196616 | tf_op jit(solution)/shard_map/ppermute | solution.py:28
  44.4 6.0 %collective-permute-start.19 = (f32[2,32,256]{2,1,0:T(8,128)S(1)}, f32[2,32,256]{2,1,0:T(8,128)S(1)}, u32[]{:S(2)}, u32[]{:S(2)}) collective-permute-start(f32[2,32,256]{2,1,0:T(8,128)S(1)} %collective-permute-done.17.refs_0_), channel_id=1, source_target_pairs={{0,1},{1,0},{2,3},{3,2},{4,5},{5,4},{6,7},{7,6},{8,9},{9,8},{10,11... | collective-permute-start | bytes 196616 | tf_op jit(solution)/shard_map/ppermute | solution.py:28
  44.8 5.6 %collective-permute-start.18 = (f32[2,32,256]{2,1,0:T(8,128)S(1)}, f32[2,32,256]{2,1,0:T(8,128)S(1)}, u32[]{:S(2)}, u32[]{:S(2)}) collective-permute-start(f32[2,32,256]{2,1,0:T(8,128)S(1)} %collective-permute-done.17.refs_0_), channel_id=1, source_target_pairs={{0,1},{1,0},{2,3},{3,2},{4,5},{5,4},{6,7},{7,6},{8,9},{9,8},{10,11... | collective-permute-start | bytes 196616 | tf_op jit(solution)/shard_map/ppermute | solution.py:28
  46.1 8.7 %collective-permute-start.23 = (f32[256,256]{1,0:T(8,128)S(1)}, f32[256,256]{1,0:T(8,128)S(1)}, u32[]{:S(2)}, u32[]{:S(2)}) collective-permute-start(f32[256,256]{1,0:T(8,128)S(1)} %collective-permute-done.1.next_ref), channel_id=1, source_target_pairs={{24,31}} | collective-permute-start | bytes 786440 | tf_op jit(solution)/shard_map/ppermute | solution.py:41
  47.4 9.3 %collective-permute-start.22 = (f32[2,128,256]{2,1,0:T(8,128)S(1)}, f32[2,128,256]{2,1,0:T(8,128)S(1)}, u32[]{:S(2)}, u32[]{:S(2)}) collective-permute-start(f32[2,128,256]{2,1,0:T(8,128)S(1)} %collective-permute-done.21.mine_ref), channel_id=1, source_target_pairs={{0,1},{1,0},{2,3},{3,2},{4,5},{5,4},{6,7},{7,6},{8,9},{9,8},{10,11... | collective-permute-start | bytes 786440 | tf_op jit(solution)/shard_map/ppermute | solution.py:18
  50.4 7.9 %collective-permute-start.24 = (f32[4,2,32,256]{3,2,1,0:T(8,128)S(1)}, f32[4,2,32,256]{3,2,1,0:T(8,128)S(1)}, u32[]{:S(2)}, u32[]{:S(2)}) collective-permute-start(f32[4,2,32,256]{3,2,1,0:T(8,128)S(1)} %shard_map.25.mine_ref), channel_id=1, source_target_pairs={{0,1},{1,0},{2,3},{3,2},{4,5},{5,4},{6,7},{7,6},{8,9},{9,8},{10,11... | collective-permute-start | bytes 786440 | tf_op jit(solution)/shard_map/ppermute | solution.py:18

commit v6 on v5

--- a/solution.py
+++ b/solution.py
@@ -192,7 +192,7 @@
     half = pl.ds(pl.multiple_of(odd * rows, rows), rows)
 
     def put(left, right):
-        pair = product(halves(left), halves(right))
+        pair = three_products(thirds(left), thirds(right))
         store(half_ref, pair)
         real_ref[...] = pair[0]
         imag_ref[...] = pair[1]
@@ -390,17 +390,19 @@
 
 
 def step_kernel(axis, level, came_ref, total_ref, slice_ref):
-    upper = (lax.axis_index(axis) // level) & 1
-    came = halves(load(came_ref))
-    total = halves(load(total_ref))
-
-    @pl.when(upper == 0)
-    def _():
-        store(slice_ref, product(came, total, True))
-
-    @pl.when(upper == 1)
-    def _():
-        store(slice_ref, product(came, total))
+    block = (lax.axis_index(axis) // level) & 3
+
+    @pl.when(block == 0)
+    def _():
+        store(slice_ref, product(halves(load(came_ref)), halves(load(total_ref)), True))
+
+    @pl.when(block == 1)
+    def _():
+        store(slice_ref, product(halves(load(came_ref)), halves(load(total_ref))))
+
+    @pl.when(block >= 2)
+    def _():
+        slice_ref[...] = came_ref[...]
 
 
 def join_kernel(*refs):

time: 59.8 us -> 60 us (level)
  no operation moved by 1% of the time
where the time goes in v6:
time: 60 us; the launch traced here: 59.9 us
  starting transfers between devices  30.7 us (51%)
  waiting for transfers between devices  16.1 us (27%)
  Pallas kernels  11.7 us (20%)
  local copies, waits for them, and re-layouts  1.04 us (2%)
    ppermute x19, starting transfers between devices, exchanged(): return lax.ppermute(x, axis, [(i, i ^ mask) for i in range(size)])  24.9 us
    pallas_call x13, Pallas kernels, call(): pl.pallas_call(kernel, out_shape=outs, in_specs=in_specs, out_specs=out_s...  11.7 us
    ppermute x19, waiting for transfers between devices, exchanged(): return lax.ppermute(x, axis, [(i, i ^ mask) for i in range(size)])  7.47 us
    ppermute x1, waiting for transfers between devices, from_next(): return lax.ppermute(x, axis, sorted(target.items()))  5.16 us
    ppermute x3, starting transfers between devices, upper_exchanged(): lax.ppermute(x, axis, [(i, i ^ (mask if i // level & 2 else 1)) for i in...  2.65 us
    ppermute x1, waiting for transfers between devices, to_last(): return lax.ppermute(x, axis, [(size - plane, size - 1)])  2.53 us
    ppermute x1, starting transfers between devices, to_last(): return lax.ppermute(x, axis, [(size - plane, size - 1)])  1.28 us
  transfers between devices with their start and end apart: 25, of which 10 were waited for; matrix products, arithmetic and copies ran while one was open for 0% of the time, Pallas kernels for 8%

profile of v6, /device:TPU:31, one launch (start us, length us, event | category | flops | bytes accessed | tf_op | source)
XLA Modules:
  0.0 59.9 jit_solution(9707528859371396027)
XLA Ops:
  0.0 1.0 %copy-done = f32[1,2,256,256]{3,2,1,0:T(8,128)S(1)} copy-done((f32[1,2,256,256]{3,2,1,0:T(8,128)S(1)}, f32[1,2,256,256]{3,2,1,0:T(8,128)}, u32[]{:S(2)}) %copy-start) | copy-done | bytes 524312
  1.2 0.7 %collective-permute-start.1 = (f32[256,256]{1,0:T(8,128)S(1)}, f32[256,256]{1,0:T(8,128)S(1)}, u32[]{:S(2)}, u32[]{:S(2)}) collective-permute-start(f32[256,256]{1,0:T(8,128)S(1)} %shard_map.17.packed_ref), channel_id=1, source_target_pairs={{0,24},{1,0},{2,1},{3,2},{4,3},{5,4},{6,5},{7,6},{8,7},{9,8},{10,9... | collective-permute-start | bytes 786440 | tf_op jit(solution)/shard_map/ppermute | solution.py:36
  2.2 5.2 %collective-permute-done.1.next_ref = f32[256,256]{1,0:T(8,128)S(1)} collective-permute-done((f32[256,256]{1,0:T(8,128)S(1)}, f32[256,256]{1,0:T(8,128)S(1)}, u32[]{:S(2)}, u32[]{:S(2)}) %collective-permute-start.1) | collective-permute-done | bytes 262176 | tf_op jit(solution)/shard_map/ppermute | solution.py:36
  7.4 1.9 %shard_map.19.own_ref = f32[2,256,256]{2,1,0:T(8,128)S(1)} custom-call(f32[2,256,256]{2,1,0:T(8,128)S(1)} %get-tuple-element.24.parts_ref, bf16[3,256,256]{2,1,0:T(8,128)(2,1)S(1)} %get-tuple-element.25.high_ref, bf16[3,256,256]{2,1,0:T(8,128)(2,1)S(1)} %get-tuple-element.26.low_ref, f32[256,256]{1,0:T(8,128)S(1)} %collective-permute-done.pair_ref, ...), custom_call_target="tpu_custom_call" | custom-call | flops 1207959552 | bytes 2359296 | tf_op jit(solution)/shard_map/pallas_call | solution.py:89
  9.4 1.9 %collective-permute-done.2.other_ref = f32[2,256,256]{2,1,0:T(8,128)S(1)} collective-permute-done((f32[2,256,256]{2,1,0:T(8,128)S(1)}, f32[2,256,256]{2,1,0:T(8,128)S(1)}, u32[]{:S(2)}, u32[]{:S(2)}) %collective-permute-start.2) | collective-permute-done | bytes 524320 | tf_op jit(solution)/shard_map/ppermute | solution.py:18
  11.7 2.8 %collective-permute-start.3 = (f32[128,256]{1,0:T(8,128)S(1)}, f32[128,256]{1,0:T(8,128)S(1)}, u32[]{:S(2)}, u32[]{:S(2)}) collective-permute-start(f32[128,256]{1,0:T(8,128)S(1)} %get-tuple-element.27), channel_id=1, source_target_pairs={{0,4},{1,5},{2,6},{3,7},{4,0},{5,1},{6,2},{7,3},{8,12},{9,13},{10,... | collective-permute-start | bytes 393224 | tf_op jit(solution)/shard_map/ppermute | solution.py:18
  14.7 1.9 %collective-permute-done.10.refs_2_ = f32[128,256]{1,0:T(8,128)S(1)} collective-permute-done((f32[128,256]{1,0:T(8,128)S(1)}, f32[128,256]{1,0:T(8,128)S(1)}, u32[]{:S(2)}, u32[]{:S(2)}) %collective-permute-start.10) | collective-permute-done | bytes 131104 | tf_op jit(solution)/shard_map/ppermute | solution.py:18
  16.6 1.0 %collective-permute-start.11 = (f32[128,256]{1,0:T(8,128)S(1)}, f32[128,256]{1,0:T(8,128)S(1)}, u32[]{:S(2)}, u32[]{:S(2)}) collective-permute-start(f32[128,256]{1,0:T(8,128)S(1)} %collective-permute-done.10.refs_2_), channel_id=1, source_target_pairs={{0,1},{1,0},{2,3},{3,2},{4,5},{5,4},{6,7},{7,6},{8,9},{9,8},{10,11... | collective-permute-start | bytes 393224 | tf_op jit(solution)/shard_map/ppermute | solution.py:18
  17.7 2.1 %collective-permute-start.13 = (f32[128,256]{1,0:T(8,128)S(1)}, f32[128,256]{1,0:T(8,128)S(1)}, u32[]{:S(2)}, u32[]{:S(2)}) collective-permute-start(f32[128,256]{1,0:T(8,128)S(1)} %collective-permute-done.3.refs_6_), channel_id=1, source_target_pairs={{0,1},{1,0},{2,3},{3,2},{4,5},{5,4},{6,7},{7,6},{8,9},{9,8},{10,11... | collective-permute-start | bytes 393224 | tf_op jit(solution)/shard_map/ppermute | solution.py:18
  19.8 0.7 %collective-permute-done.14.refs_8_ = f32[128,256]{1,0:T(8,128)S(1)} collective-permute-done((f32[128,256]{1,0:T(8,128)S(1)}, f32[128,256]{1,0:T(8,128)S(1)}, u32[]{:S(2)}, u32[]{:S(2)}) %collective-permute-start.14) | collective-permute-done | bytes 131104 | tf_op jit(solution)/shard_map/ppermute | solution.py:18
  20.6 1.5 %collective-permute-start.7 = (f32[128,256]{1,0:T(8,128)S(1)}, f32[128,256]{1,0:T(8,128)S(1)}, u32[]{:S(2)}, u32[]{:S(2)}) collective-permute-start(f32[128,256]{1,0:T(8,128)S(1)} %collective-permute-done.6.refs_4_), channel_id=1, source_target_pairs={{0,4},{1,5},{2,6},{3,7},{4,0},{5,1},{6,2},{7,3},{8,12},{9,13},{10,... | collective-permute-start | bytes 393224 | tf_op jit(solution)/shard_map/ppermute | solution.py:18
  22.1 1.8 %collective-permute-start.15 = (f32[128,256]{1,0:T(8,128)S(1)}, f32[128,256]{1,0:T(8,128)S(1)}, u32[]{:S(2)}, u32[]{:S(2)}) collective-permute-start(f32[128,256]{1,0:T(8,128)S(1)} %collective-permute-done.14.refs_8_), channel_id=1, source_target_pairs={{0,1},{1,0},{2,3},{3,2},{4,5},{5,4},{6,7},{7,6},{8,9},{9,8},{10,11... | collective-permute-start | bytes 393224 | tf_op jit(solution)/shard_map/ppermute | solution.py:18
  24.0 0.4 collective-permute-done.4.refs_0_
  24.4 2.4 %collective-permute-start.5 = (f32[128,256]{1,0:T(8,128)S(1)}, f32[128,256]{1,0:T(8,128)S(1)}, u32[]{:S(2)}, u32[]{:S(2)}) collective-permute-start(f32[128,256]{1,0:T(8,128)S(1)} %collective-permute-done.4.refs_0_), channel_id=1, source_target_pairs={{0,1},{1,0},{2,3},{3,2},{4,5},{5,4},{6,7},{7,6},{8,9},{9,8},{10,11... | collective-permute-start | bytes 393224 | tf_op jit(solution)/shard_map/ppermute | solution.py:18
  27.2 0.8 %shard_map.21 = (bf16[4,2,256,256]{3,2,1,0:T(8,128)(2,1)S(1)}, bf16[4,2,256,256]{3,2,1,0:T(8,128)(2,1)S(1)}, bf16[2,256,256]{2,1,0:T(8,128)(2,1)S(1)}, bf16[2,256,256]{2,1,0:T(8,128)(2,1)S(1)}) custom-call(f32[2,128,256]{2,1,0:T(8,128)S(1)} %get-tuple-element.29.refs_0_, f32[2,128,256]{2,1,0:T(8,128)S(1)} %collective-permute-done.9.refs_1_, ...), custom_call_target="tpu_custom_call" | custom-call | flops 402653184 | bytes 4194304 | tf_op jit(solution)/shard_map/pallas_call | solution.py:89
  28.1 0.9 %shard_map.22 = (f32[2,32,256]{2,1,0:T(8,128)S(1)}, bf16[4,2,256,256]{3,2,1,0:T(8,128)(2,1)S(1)}, bf16[4,2,256,256]{3,2,1,0:T(8,128)(2,1)S(1)}) custom-call(f32[128,256]{1,0:T(8,128)S(1)} %collective-permute-done.4.refs_0_, f32[128,256]{1,0:T(8,128)S(1)} %collective-permute-done.5.refs_1_, ...), custom_call_target="tpu_custom_call", output_to_operand_aliasing={{1}: (4, {}), {2}: (5, {})} | custom-call | flops 134217728 | bytes 5308416 | tf_op jit(solution)/shard_map/pallas_call | solution.py:89
  29.0 2.4 %shard_map.23 = (f32[2,256,256]{2,1,0:T(8,128)S(1)}, f32[2,256,256]{2,1,0:T(8,128)S(1)}, f32[2,128,256]{2,1,0:T(8,128)S(1)}) custom-call(bf16[4,2,256,256]{3,2,1,0:T(8,128)(2,1)S(1)} %get-tuple-element.35.high_ref, bf16[4,2,256,256]{3,2,1,0:T(8,128)(2,1)S(1)} %get-tuple-element.36.low_ref, f32[2,256,256]{2,1,0:T(8,128)S(1)} %shard_map.19.own_ref, ...), custom_call_target="tpu_custom_call" | custom-call | flops 1610612736 | bytes 4456448 | tf_op jit(solution)/shard_map/pallas_call | solution.py:89
  31.5 1.0 %collective-permute-start.21 = (f32[2,128,256]{2,1,0:T(8,128)S(1)}, f32[2,128,256]{2,1,0:T(8,128)S(1)}, u32[]{:S(2)}, u32[]{:S(2)}) collective-permute-start(f32[2,128,256]{2,1,0:T(8,128)S(1)} %get-tuple-element.38), channel_id=1, source_target_pairs={{0,8},{1,9},{2,10},{3,11},{4,12},{5,13},{6,14},{7,15},{8,0},{9,1},... | collective-permute-start | bytes 786440 | tf_op jit(solution)/shard_map/ppermute | solution.py:18
  32.4 1.2 %collective-permute-start.16 = (f32[2,32,256]{2,1,0:T(8,128)S(1)}, f32[2,32,256]{2,1,0:T(8,128)S(1)}, u32[]{:S(2)}, u32[]{:S(2)}) collective-permute-start(f32[2,32,256]{2,1,0:T(8,128)S(1)} %get-tuple-element.34), channel_id=1, source_target_pairs={{0,8},{1,9},{2,10},{3,11},{4,12},{5,13},{6,14},{7,15},{8,0},{9,1},... | collective-permute-start | bytes 196616 | tf_op jit(solution)/shard_map/ppermute | solution.py:23
  33.6 0.9 %collective-permute-done.16.came_ref = f32[2,32,256]{2,1,0:T(8,128)S(1)} collective-permute-done((f32[2,32,256]{2,1,0:T(8,128)S(1)}, f32[2,32,256]{2,1,0:T(8,128)S(1)}, u32[]{:S(2)}, u32[]{:S(2)}) %collective-permute-start.16) | collective-permute-done | bytes 65568 | tf_op jit(solution)/shard_map/ppermute | solution.py:23
  34.5 6.6 %collective-permute-start.17 = (f32[2,32,256]{2,1,0:T(8,128)S(1)}, f32[2,32,256]{2,1,0:T(8,128)S(1)}, u32[]{:S(2)}, u32[]{:S(2)}) collective-permute-start(f32[2,32,256]{2,1,0:T(8,128)S(1)} %shard_map.24), channel_id=1, source_target_pairs={{0,16},{1,17},{2,18},{3,19},{4,20},{5,21},{6,22},{7,23},{8,24},{9,... | collective-permute-start | bytes 196616 | tf_op jit(solution)/shard_map/ppermute | solution.py:18
  41.2 2.2 %collective-permute-done.17.refs_0_ = f32[2,32,256]{2,1,0:T(8,128)S(1)} collective-permute-done((f32[2,32,256]{2,1,0:T(8,128)S(1)}, f32[2,32,256]{2,1,0:T(8,128)S(1)}, u32[]{:S(2)}, u32[]{:S(2)}) %collective-permute-start.17) | collective-permute-done | bytes 65568 | tf_op jit(solution)/shard_map/ppermute | solution.py:18
  43.4 0.9 %collective-permute-start.20 = (f32[2,32,256]{2,1,0:T(8,128)S(1)}, f32[2,32,256]{2,1,0:T(8,128)S(1)}, u32[]{:S(2)}, u32[]{:S(2)}) collective-permute-start(f32[2,32,256]{2,1,0:T(8,128)S(1)} %collective-permute-done.17.refs_0_), channel_id=1, source_target_pairs={{0,1},{1,0},{2,3},{3,2},{4,5},{5,4},{6,7},{7,6},{8,9},{9,8},{10,11... | collective-permute-start | bytes 196616 | tf_op jit(solution)/shard_map/ppermute | solution.py:28
  44.2 0.4 collective-permute-start.19
  44.6 1.4 %collective-permute-start.18 = (f32[2,32,256]{2,1,0:T(8,128)S(1)}, f32[2,32,256]{2,1,0:T(8,128)S(1)}, u32[]{:S(2)}, u32[]{:S(2)}) collective-permute-start(f32[2,32,256]{2,1,0:T(8,128)S(1)} %collective-permute-done.17.refs_0_), channel_id=1, source_target_pairs={{0,1},{1,0},{2,3},{3,2},{4,5},{5,4},{6,7},{7,6},{8,9},{9,8},{10,11... | collective-permute-start | bytes 196616 | tf_op jit(solution)/shard_map/ppermute | solution.py:28
  46.0 1.3 %collective-permute-start.23 = (f32[256,256]{1,0:T(8,128)S(1)}, f32[256,256]{1,0:T(8,128)S(1)}, u32[]{:S(2)}, u32[]{:S(2)}) collective-permute-start(f32[256,256]{1,0:T(8,128)S(1)} %collective-permute-done.1.next_ref), channel_id=1, source_target_pairs={{24,31}} | collective-permute-start | bytes 786440 | tf_op jit(solution)/shard_map/ppermute | solution.py:41
  47.3 2.9 %collective-permute-start.22 = (f32[2,128,256]{2,1,0:T(8,128)S(1)}, f32[2,128,256]{2,1,0:T(8,128)S(1)}, u32[]{:S(2)}, u32[]{:S(2)}) collective-permute-start(f32[2,128,256]{2,1,0:T(8,128)S(1)} %collective-permute-done.21.mine_ref), channel_id=1, source_target_pairs={{0,1},{1,0},{2,3},{3,2},{4,5},{5,4},{6,7},{7,6},{8,9},{9,8},{10,11... | collective-permute-start | bytes 786440 | tf_op jit(solution)/shard_map/ppermute | solution.py:18
  50.3 1.9 %collective-permute-start.24 = (f32[4,2,32,256]{3,2,1,0:T(8,128)S(1)}, f32[4,2,32,256]{3,2,1,0:T(8,128)S(1)}, u32[]{:S(2)}, u32[]{:S(2)}) collective-permute-start(f32[4,2,32,256]{3,2,1,0:T(8,128)S(1)} %shard_map.25.mine_ref), channel_id=1, source_target_pairs={{0,1},{1,0},{2,3},{3,2},{4,5},{5,4},{6,7},{7,6},{8,9},{9,8},{10,11... | collective-permute-start | bytes 786440 | tf_op jit(solution)/shard_map/ppermute | solution.py:18
  52.2 2.5 %collective-permute-done.23.next_ref = f32[256,256]{1,0:T(8,128)S(1)} collective-permute-done((f32[256,256]{1,0:T(8,128)S(1)}, f32[256,256]{1,0:T(8,128)S(1)}, u32[]{:S(2)}, u32[]{:S(2)}) %collective-permute-start.23) | collective-permute-done | bytes 262176 | tf_op jit(solution)/shard_map/ppermute | solution.py:41
  54.7 1.9 %shard_map.26.late_ref = f32[2,256,256]{2,1,0:T(8,128)S(1)} custom-call(f32[2,256,256]{2,1,0:T(8,128)S(1)} %get-tuple-element.24.parts_ref, bf16[3,256,256]{2,1,0:T(8,128)(2,1)S(1)} %get-tuple-element.25.high_ref, bf16[3,256,256]{2,1,0:T(8,128)(2,1)S(1)} %get-tuple-element.26.low_ref, f32[256,256]{1,0:T(8,128)S(1)} %collective-permute-done.23.next_ref), custom_call_target="tpu_custom_call" | custom-call | flops 134217728 | bytes 2097152 | tf_op jit(solution)/shard_map/pallas_call | solution.py:89
  56.7 1.3 %shard_map.27 = (f32[1,2,256,256]{3,2,1,0:T(8,128)}, bf16[3,256,256]{2,1,0:T(8,128)(2,1)S(1)}, bf16[3,256,256]{2,1,0:T(8,128)(2,1)S(1)}) custom-call(f32[2,128,256]{2,1,0:T(8,128)S(1)} %collective-permute-done.21.mine_ref, f32[2,128,256]{2,1,0:T(8,128)S(1)} %collective-permute-done.22.twin_ref, f32[2,256,256]{2,1,0:T(8,128)S(1)} %get-tuple-element.39.local_ref, ...), custom_call_target="tpu_custom_call" | custom-call | flops 402653184 | bytes 2883584 | tf_op jit(solution)/shard_map/pallas_call | solution.py:89
  58.4 1.3 %shard_map.29 = f32[1,2,256,256]{3,2,1,0:T(8,128)} custom-call(f32[2,256,256]{2,1,0:T(8,128)S(1)} %shard_map.28.part_ref, f32[4,2,32,256]{3,2,1,0:T(8,128)S(1)} %collective-permute-done.24.twin_ref, bf16[3,256,256]{2,1,0:T(8,128)(2,1)S(1)} %get-tuple-element.40.high_ref, ...), custom_call_target="tpu_custom_call", output_to_operand_aliasing={{}: (4, {})} | custom-call | flops 268435456 | bytes 2621440 | tf_op jit(solution)/shard_map/pallas_call | solution.py:89
  (33 shorter events, 2.3 us)
Async XLA Ops:
  0.0 1.0 %copy-start = (f32[1,2,256,256]{3,2,1,0:T(8,128)S(1)}, f32[1,2,256,256]{3,2,1,0:T(8,128)}, u32[]{:S(2)}) copy-start(f32[1,2,256,256]{3,2,1,0:T(8,128)} %drawn_ref.1) | copy-start | bytes 1572868
  1.2 6.2 %collective-permute-start.1 = (f32[256,256]{1,0:T(8,128)S(1)}, f32[256,256]{1,0:T(8,128)S(1)}, u32[]{:S(2)}, u32[]{:S(2)}) collective-permute-start(f32[256,256]{1,0:T(8,128)S(1)} %shard_map.17.packed_ref), channel_id=1, source_target_pairs={{0,24},{1,0},{2,1},{3,2},{4,3},{5,4},{6,5},{7,6},{8,7},{9,8},{10,9... | collective-permute-start | bytes 786440 | tf_op jit(solution)/shard_map/ppermute | solution.py:36
  1.9 5.4 %collective-permute-start = (f32[256,256]{1,0:T(8,128)S(1)}, f32[256,256]{1,0:T(8,128)S(1)}, u32[]{:S(2)}, u32[]{:S(2)}) collective-permute-start(f32[256,256]{1,0:T(8,128)S(1)} %shard_map.17.packed_ref), channel_id=1, source_target_pairs={{0,1},{1,0},{2,3},{3,2},{4,5},{5,4},{6,7},{7,6},{8,9},{9,8},{10,11... | collective-permute-start | bytes 786440 | tf_op jit(solution)/shard_map/ppermute | solution.py:18
  9.3 2.0 %collective-permute-start.2 = (f32[2,256,256]{2,1,0:T(8,128)S(1)}, f32[2,256,256]{2,1,0:T(8,128)S(1)}, u32[]{:S(2)}, u32[]{:S(2)}) collective-permute-start(f32[2,256,256]{2,1,0:T(8,128)S(1)} %shard_map.19.own_ref), channel_id=1, source_target_pairs={{0,1},{1,0},{2,3},{3,2},{4,5},{5,4},{6,7},{7,6},{8,9},{9,8},{10,11... | collective-permute-start | bytes 1572872 | tf_op jit(solution)/shard_map/ppermute | solution.py:18
  11.6 5.0 %collective-permute-start.10 = (f32[128,256]{1,0:T(8,128)S(1)}, f32[128,256]{1,0:T(8,128)S(1)}, u32[]{:S(2)}, u32[]{:S(2)}) collective-permute-start(f32[128,256]{1,0:T(8,128)S(1)} %get-tuple-element.27), channel_id=1, source_target_pairs={{0,2},{1,3},{2,0},{3,1},{4,6},{5,7},{6,4},{7,5},{8,10},{9,11},{10,... | collective-permute-start | bytes 393224 | tf_op jit(solution)/shard_map/ppermute | solution.py:18
  11.7 6.0 %collective-permute-start.3 = (f32[128,256]{1,0:T(8,128)S(1)}, f32[128,256]{1,0:T(8,128)S(1)}, u32[]{:S(2)}, u32[]{:S(2)}) collective-permute-start(f32[128,256]{1,0:T(8,128)S(1)} %get-tuple-element.27), channel_id=1, source_target_pairs={{0,4},{1,5},{2,6},{3,7},{4,0},{5,1},{6,2},{7,3},{8,12},{9,13},{10,... | collective-permute-start | bytes 393224 | tf_op jit(solution)/shard_map/ppermute | solution.py:18
  14.5 6.0 %collective-permute-start.14 = (f32[128,256]{1,0:T(8,128)S(1)}, f32[128,256]{1,0:T(8,128)S(1)}, u32[]{:S(2)}, u32[]{:S(2)}) collective-permute-start(f32[128,256]{1,0:T(8,128)S(1)} %get-tuple-element.28), channel_id=1, source_target_pairs={{0,4},{1,5},{2,6},{3,7},{4,0},{5,1},{6,2},{7,3},{8,12},{9,13},{10,... | collective-permute-start | bytes 393224 | tf_op jit(solution)/shard_map/ppermute | solution.py:18
  14.5 6.1 %collective-permute-start.6 = (f32[128,256]{1,0:T(8,128)S(1)}, f32[128,256]{1,0:T(8,128)S(1)}, u32[]{:S(2)}, u32[]{:S(2)}) collective-permute-start(f32[128,256]{1,0:T(8,128)S(1)} %get-tuple-element.28), channel_id=1, source_target_pairs={{0,2},{1,3},{2,0},{3,1},{4,6},{5,7},{6,4},{7,5},{8,10},{9,11},{10,... | collective-permute-start | bytes 393224 | tf_op jit(solution)/shard_map/ppermute | solution.py:18
  16.6 5.5 %collective-permute-start.11 = (f32[128,256]{1,0:T(8,128)S(1)}, f32[128,256]{1,0:T(8,128)S(1)}, u32[]{:S(2)}, u32[]{:S(2)}) collective-permute-start(f32[128,256]{1,0:T(8,128)S(1)} %collective-permute-done.10.refs_2_), channel_id=1, source_target_pairs={{0,1},{1,0},{2,3},{3,2},{4,5},{5,4},{6,7},{7,6},{8,9},{9,8},{10,11... | collective-permute-start | bytes 393224 | tf_op jit(solution)/shard_map/ppermute | solution.py:18
  17.7 6.2 %collective-permute-start.13 = (f32[128,256]{1,0:T(8,128)S(1)}, f32[128,256]{1,0:T(8,128)S(1)}, u32[]{:S(2)}, u32[]{:S(2)}) collective-permute-start(f32[128,256]{1,0:T(8,128)S(1)} %collective-permute-done.3.refs_6_), channel_id=1, source_target_pairs={{0,1},{1,0},{2,3},{3,2},{4,5},{5,4},{6,7},{7,6},{8,9},{9,8},{10,11... | collective-permute-start | bytes 393224 | tf_op jit(solution)/shard_map/ppermute | solution.py:18
  19.8 7.3 %collective-permute-start.9 = (f32[2,128,256]{2,1,0:T(8,128)S(1)}, f32[2,128,256]{2,1,0:T(8,128)S(1)}, u32[]{:S(2)}, u32[]{:S(2)}) collective-permute-start(f32[2,128,256]{2,1,0:T(8,128)S(1)} %get-tuple-element.29.refs_0_), channel_id=1, source_target_pairs={{0,1},{1,0},{2,3},{3,2},{4,5},{5,4},{6,7},{7,6},{8,9},{9,8},{10,11... | collective-permute-start | bytes 786440 | tf_op jit(solution)/shard_map/ppermute | solution.py:18
  20.6 3.8 %collective-permute-start.4 = (f32[128,256]{1,0:T(8,128)S(1)}, f32[128,256]{1,0:T(8,128)S(1)}, u32[]{:S(2)}, u32[]{:S(2)}) collective-permute-start(f32[128,256]{1,0:T(8,128)S(1)} %collective-permute-done.3.refs_6_), channel_id=1, source_target_pairs={{0,2},{1,3},{2,0},{3,1},{4,6},{5,7},{6,4},{7,5},{8,10},{9,11},{10,... | collective-permute-start | bytes 393224 | tf_op jit(solution)/shard_map/ppermute | solution.py:18
  20.6 6.1 %collective-permute-start.7 = (f32[128,256]{1,0:T(8,128)S(1)}, f32[128,256]{1,0:T(8,128)S(1)}, u32[]{:S(2)}, u32[]{:S(2)}) collective-permute-start(f32[128,256]{1,0:T(8,128)S(1)} %collective-permute-done.6.refs_4_), channel_id=1, source_target_pairs={{0,4},{1,5},{2,6},{3,7},{4,0},{5,1},{6,2},{7,3},{8,12},{9,13},{10,... | collective-permute-start | bytes 393224 | tf_op jit(solution)/shard_map/ppermute | solution.py:18
  22.1 5.0 %collective-permute-start.15 = (f32[128,256]{1,0:T(8,128)S(1)}, f32[128,256]{1,0:T(8,128)S(1)}, u32[]{:S(2)}, u32[]{:S(2)}) collective-permute-start(f32[128,256]{1,0:T(8,128)S(1)} %collective-permute-done.14.refs_8_), channel_id=1, source_target_pairs={{0,1},{1,0},{2,3},{3,2},{4,5},{5,4},{6,7},{7,6},{8,9},{9,8},{10,11... | collective-permute-start | bytes 393224 | tf_op jit(solution)/shard_map/ppermute | solution.py:18
  23.9 3.2 %collective-permute-start.12 = (f32[128,256]{1,0:T(8,128)S(1)}, f32[128,256]{1,0:T(8,128)S(1)}, u32[]{:S(2)}, u32[]{:S(2)}) collective-permute-start(f32[128,256]{1,0:T(8,128)S(1)} %collective-permute-done.6.refs_4_), channel_id=1, source_target_pairs={{0,1},{1,0},{2,3},{3,2},{4,5},{5,4},{6,7},{7,6},{8,9},{9,8},{10,11... | collective-permute-start | bytes 393224 | tf_op jit(solution)/shard_map/ppermute | solution.py:18
  24.4 3.6 %collective-permute-start.5 = (f32[128,256]{1,0:T(8,128)S(1)}, f32[128,256]{1,0:T(8,128)S(1)}, u32[]{:S(2)}, u32[]{:S(2)}) collective-permute-start(f32[128,256]{1,0:T(8,128)S(1)} %collective-permute-done.4.refs_0_), channel_id=1, source_target_pairs={{0,1},{1,0},{2,3},{3,2},{4,5},{5,4},{6,7},{7,6},{8,9},{9,8},{10,11... | collective-permute-start | bytes 393224 | tf_op jit(solution)/shard_map/ppermute | solution.py:18
  26.8 1.4 %collective-permute-start.8 = (f32[128,256]{1,0:T(8,128)S(1)}, f32[128,256]{1,0:T(8,128)S(1)}, u32[]{:S(2)}, u32[]{:S(2)}) collective-permute-start(f32[128,256]{1,0:T(8,128)S(1)} %collective-permute-done.7.refs_2_), channel_id=1, source_target_pairs={{0,1},{1,0},{2,3},{3,2},{4,5},{5,4},{6,7},{7,6},{8,9},{9,8},{10,11... | collective-permute-start | bytes 393224 | tf_op jit(solution)/shard_map/ppermute | solution.py:18
  31.5 15.9 %collective-permute-start.21 = (f32[2,128,256]{2,1,0:T(8,128)S(1)}, f32[2,128,256]{2,1,0:T(8,128)S(1)}, u32[]{:S(2)}, u32[]{:S(2)}) collective-permute-start(f32[2,128,256]{2,1,0:T(8,128)S(1)} %get-tuple-element.38), channel_id=1, source_target_pairs={{0,8},{1,9},{2,10},{3,11},{4,12},{5,13},{6,14},{7,15},{8,0},{9,1},... | collective-permute-start | bytes 786440 | tf_op jit(solution)/shard_map/ppermute | solution.py:18
  32.4 2.1 %collective-permute-start.16 = (f32[2,32,256]{2,1,0:T(8,128)S(1)}, f32[2,32,256]{2,1,0:T(8,128)S(1)}, u32[]{:S(2)}, u32[]{:S(2)}) collective-permute-start(f32[2,32,256]{2,1,0:T(8,128)S(1)} %get-tuple-element.34), channel_id=1, source_target_pairs={{0,8},{1,9},{2,10},{3,11},{4,12},{5,13},{6,14},{7,15},{8,0},{9,1},... | collective-permute-start | bytes 196616 | tf_op jit(solution)/shard_map/ppermute | solution.py:23
  34.5 8.8 %collective-permute-start.17 = (f32[2,32,256]{2,1,0:T(8,128)S(1)}, f32[2,32,256]{2,1,0:T(8,128)S(1)}, u32[]{:S(2)}, u32[]{:S(2)}) collective-permute-start(f32[2,32,256]{2,1,0:T(8,128)S(1)} %shard_map.24), channel_id=1, source_target_pairs={{0,16},{1,17},{2,18},{3,19},{4,20},{5,21},{6,22},{7,23},{8,24},{9,... | collective-permute-start | bytes 196616 | tf_op jit(solution)/shard_map/ppermute | solution.py:18
  43.4 6.9 %collective-permute-start.20 = (f32[2,32,256]{2,1,0:T(8,128)S(1)}, f32[2,32,256]{2,1,0:T(8,128)S(1)}, u32[]{:S(2)}, u32[]{:S(2)}) collective-permute-start(f32[2,32,256]{2,1,0:T(8,128)S(1)} %collective-permute-done.17.refs_0_), channel_id=1, source_target_pairs={{0,1},{1,0},{2,3},{3,2},{4,5},{5,4},{6,7},{7,6},{8,9},{9,8},{10,11... | collective-permute-start | bytes 196616 | tf_op jit(solution)/shard_map/ppermute | solution.py:28
  44.2 6.0 %collective-permute-start.19 = (f32[2,32,256]{2,1,0:T(8,128)S(1)}, f32[2,32,256]{2,1,0:T(8,128)S(1)}, u32[]{:S(2)}, u32[]{:S(2)}) collective-permute-start(f32[2,32,256]{2,1,0:T(8,128)S(1)} %collective-permute-done.17.refs_0_), channel_id=1, source_target_pairs={{0,1},{1,0},{2,3},{3,2},{4,5},{5,4},{6,7},{7,6},{8,9},{9,8},{10,11... | collective-permute-start | bytes 196616 | tf_op jit(solution)/shard_map/ppermute | solution.py:28
  44.6 5.6 %collective-permute-start.18 = (f32[2,32,256]{2,1,0:T(8,128)S(1)}, f32[2,32,256]{2,1,0:T(8,128)S(1)}, u32[]{:S(2)}, u32[]{:S(2)}) collective-permute-start(f32[2,32,256]{2,1,0:T(8,128)S(1)} %collective-permute-done.17.refs_0_), channel_id=1, source_target_pairs={{0,1},{1,0},{2,3},{3,2},{4,5},{5,4},{6,7},{7,6},{8,9},{9,8},{10,11... | collective-permute-start | bytes 196616 | tf_op jit(solution)/shard_map/ppermute | solution.py:28
  46.0 8.7 %collective-permute-start.23 = (f32[256,256]{1,0:T(8,128)S(1)}, f32[256,256]{1,0:T(8,128)S(1)}, u32[]{:S(2)}, u32[]{:S(2)}) collective-permute-start(f32[256,256]{1,0:T(8,128)S(1)} %collective-permute-done.1.next_ref), channel_id=1, source_target_pairs={{24,31}} | collective-permute-start | bytes 786440 | tf_op jit(solution)/shard_map/ppermute | solution.py:41
  47.3 9.3 %collective-permute-start.22 = (f32[2,128,256]{2,1,0:T(8,128)S(1)}, f32[2,128,256]{2,1,0:T(8,128)S(1)}, u32[]{:S(2)}, u32[]{:S(2)}) collective-permute-start(f32[2,128,256]{2,1,0:T(8,128)S(1)} %collective-permute-done.21.mine_ref), channel_id=1, source_target_pairs={{0,1},{1,0},{2,3},{3,2},{4,5},{5,4},{6,7},{7,6},{8,9},{9,8},{10,11... | collective-permute-start | bytes 786440 | tf_op jit(solution)/shard_map/ppermute | solution.py:18
  50.3 8.1 %collective-permute-start.24 = (f32[4,2,32,256]{3,2,1,0:T(8,128)S(1)}, f32[4,2,32,256]{3,2,1,0:T(8,128)S(1)}, u32[]{:S(2)}, u32[]{:S(2)}) collective-permute-start(f32[4,2,32,256]{3,2,1,0:T(8,128)S(1)} %shard_map.25.mine_ref), channel_id=1, source_target_pairs={{0,1},{1,0},{2,3},{3,2},{4,5},{5,4},{6,7},{7,6},{8,9},{9,8},{10,11... | collective-permute-start | bytes 786440 | tf_op jit(solution)/shard_map/ppermute | solution.py:18

commit v7 on v6

--- a/solution.py
+++ b/solution.py
@@ -270,22 +270,22 @@
             hold(axis, 3, other, k, pieces[2 * k + other][...], high_ref, low_ref)
     me = lax.axis_index(axis)
     rows = own_rows(me, slice_ref.shape[1])
-    upper, second_row = (me // level) & 1, (me >> 2) & 1
+    block, second_row = (me // level) & 3, (me >> 2) & 1
     row = get_pair(row_high_ref, row_low_ref)
 
-    @pl.when((upper == 0) & (second_row == 0))
+    @pl.when((block == 0) & (second_row == 0))
     def _():
         value = product(get_pair(row_high_ref, row_low_ref, rows), get(high_ref, low_ref, 2))
         store(slice_ref, product(halves(value), get(high_ref, low_ref, 3)))
 
-    @pl.when((upper == 0) & (second_row == 1))
+    @pl.when((block == 0) & (second_row == 1))
     def _():
         value = product(get(high_ref, low_ref, 0, rows), get(high_ref, low_ref, 1))
         store(slice_ref, product(halves(value), row))
 
     begin = (me & (parts - 1)) * slice_ref.shape[1]
     width = room_ref.shape[0]
-    block = pl.ds(pl.multiple_of(begin // width * width, width), width)
+    columns_of = pl.ds(pl.multiple_of(begin // width * width, width), width)
 
     def columns(high, low):
         return (
@@ -301,19 +301,23 @@
             room_ref[...] = grown[k].T
             slice_ref[k] = room_ref[inside, :]
 
-    @pl.when((upper == 1) & (second_row == 1))
+    @pl.when((block == 1) & (second_row == 1))
     def _():
         right = columns(
-            [row_high_ref[k, :, block] for k in range(2)], [row_low_ref[k, :, block] for k in range(2)]
+            [row_high_ref[k, :, columns_of] for k in range(2)], [row_low_ref[k, :, columns_of] for k in range(2)]
         )
         put(get(high_ref, low_ref, 1), get(high_ref, low_ref, 0), right)
 
-    @pl.when((upper == 1) & (second_row == 0))
+    @pl.when((block == 1) & (second_row == 0))
     def _():
         right = columns(
-            [high_ref[3, k, :, block] for k in range(2)], [low_ref[3, k, :, block] for k in range(2)]
+            [high_ref[3, k, :, columns_of] for k in range(2)], [low_ref[3, k, :, columns_of] for k in range(2)]
         )
         put(get(high_ref, low_ref, 2), row, right)
+
+    @pl.when(block >= 2)
+    def _():
+        slice_ref[...] = jnp.zeros_like(slice_ref)
 
 
 def prefix_kernel(axis, high_ref, low_ref, own_ref, other_ref, total_ref, local_ref, half_ref):

time: 60 us -> 60 us (level)
  starting transfers between devices: 30.7 us -> 31.6 us
  Pallas kernels: 11.7 us -> 10.9 us
    ppermute x19, starting transfers between devices: 24.9 us -> 25.7 us  [exchanged(): return lax.ppermute(x, axis, [(i, i ^ mask) for i in range(size)])]
    pallas_call x13, Pallas kernels: 11.7 us -> 10.9 us  [call(): pl.pallas_call(kernel, out_shape=outs, in_specs=in_specs, out_specs=out_s...]
where the time goes in v7:
time: 60 us; the launch traced here: 59.9 us
  starting transfers between devices  31.6 us (53%)
  waiting for transfers between devices  16.1 us (27%)
  Pallas kernels  10.9 us (18%)
  local copies, waits for them, and re-layouts  1.04 us (2%)
    ppermute x19, starting transfers between devices, exchanged(): return lax.ppermute(x, axis, [(i, i ^ mask) for i in range(size)])  25.7 us
    pallas_call x13, Pallas kernels, call(): pl.pallas_call(kernel, out_shape=outs, in_specs=in_specs, out_specs=out_s...  10.9 us
    ppermute x19, waiting for transfers between devices, exchanged(): return lax.ppermute(x, axis, [(i, i ^ mask) for i in range(size)])  7.48 us
    ppermute x1, waiting for transfers between devices, from_next(): return lax.ppermute(x, axis, sorted(target.items()))  5.16 us
    ppermute x3, starting transfers between devices, upper_exchanged(): lax.ppermute(x, axis, [(i, i ^ (mask if i // level & 2 else 1)) for i in...  2.65 us
    ppermute x1, waiting for transfers between devices, to_last(): return lax.ppermute(x, axis, [(size - plane, size - 1)])  2.52 us
    ppermute x1, starting transfers between devices, to_last(): return lax.ppermute(x, axis, [(size - plane, size - 1)])  1.28 us
  transfers between devices with their start and end apart: 25, of which 10 were waited for; matrix products, arithmetic and copies ran while one was open for 0% of the time, Pallas kernels for 8%

profile of v7, /device:TPU:31, one launch (start us, length us, event | category | flops | bytes accessed | tf_op | source)
XLA Modules:
  0.0 59.9 jit_solution(17514872002389683595)
XLA Ops:
  0.0 1.0 %copy-done = f32[1,2,256,256]{3,2,1,0:T(8,128)S(1)} copy-done((f32[1,2,256,256]{3,2,1,0:T(8,128)S(1)}, f32[1,2,256,256]{3,2,1,0:T(8,128)}, u32[]{:S(2)}) %copy-start) | copy-done | bytes 524312
  1.2 0.7 %collective-permute-start.1 = (f32[256,256]{1,0:T(8,128)S(1)}, f32[256,256]{1,0:T(8,128)S(1)}, u32[]{:S(2)}, u32[]{:S(2)}) collective-permute-start(f32[256,256]{1,0:T(8,128)S(1)} %shard_map.17.packed_ref), channel_id=1, source_target_pairs={{0,24},{1,0},{2,1},{3,2},{4,3},{5,4},{6,5},{7,6},{8,7},{9,8},{10,9... | collective-permute-start | bytes 786440 | tf_op jit(solution)/shard_map/ppermute | solution.py:36
  2.2 5.2 %collective-permute-done.1.next_ref = f32[256,256]{1,0:T(8,128)S(1)} collective-permute-done((f32[256,256]{1,0:T(8,128)S(1)}, f32[256,256]{1,0:T(8,128)S(1)}, u32[]{:S(2)}, u32[]{:S(2)}) %collective-permute-start.1) | collective-permute-done | bytes 262176 | tf_op jit(solution)/shard_map/ppermute | solution.py:36
  7.4 1.9 %shard_map.19.own_ref = f32[2,256,256]{2,1,0:T(8,128)S(1)} custom-call(f32[2,256,256]{2,1,0:T(8,128)S(1)} %get-tuple-element.24.parts_ref, bf16[3,256,256]{2,1,0:T(8,128)(2,1)S(1)} %get-tuple-element.25.high_ref, bf16[3,256,256]{2,1,0:T(8,128)(2,1)S(1)} %get-tuple-element.26.low_ref, f32[256,256]{1,0:T(8,128)S(1)} %collective-permute-done.pair_ref, ...), custom_call_target="tpu_custom_call" | custom-call | flops 1207959552 | bytes 2359296 | tf_op jit(solution)/shard_map/pallas_call | solution.py:89
  9.4 1.9 %collective-permute-done.2.other_ref = f32[2,256,256]{2,1,0:T(8,128)S(1)} collective-permute-done((f32[2,256,256]{2,1,0:T(8,128)S(1)}, f32[2,256,256]{2,1,0:T(8,128)S(1)}, u32[]{:S(2)}, u32[]{:S(2)}) %collective-permute-start.2) | collective-permute-done | bytes 524320 | tf_op jit(solution)/shard_map/ppermute | solution.py:18
  11.7 2.8 %collective-permute-start.3 = (f32[128,256]{1,0:T(8,128)S(1)}, f32[128,256]{1,0:T(8,128)S(1)}, u32[]{:S(2)}, u32[]{:S(2)}) collective-permute-start(f32[128,256]{1,0:T(8,128)S(1)} %get-tuple-element.27), channel_id=1, source_target_pairs={{0,4},{1,5},{2,6},{3,7},{4,0},{5,1},{6,2},{7,3},{8,12},{9,13},{10,... | collective-permute-start | bytes 393224 | tf_op jit(solution)/shard_map/ppermute | solution.py:18
  14.7 1.9 %collective-permute-done.10.refs_2_ = f32[128,256]{1,0:T(8,128)S(1)} collective-permute-done((f32[128,256]{1,0:T(8,128)S(1)}, f32[128,256]{1,0:T(8,128)S(1)}, u32[]{:S(2)}, u32[]{:S(2)}) %collective-permute-start.10) | collective-permute-done | bytes 131104 | tf_op jit(solution)/shard_map/ppermute | solution.py:18
  16.6 1.0 %collective-permute-start.11 = (f32[128,256]{1,0:T(8,128)S(1)}, f32[128,256]{1,0:T(8,128)S(1)}, u32[]{:S(2)}, u32[]{:S(2)}) collective-permute-start(f32[128,256]{1,0:T(8,128)S(1)} %collective-permute-done.10.refs_2_), channel_id=1, source_target_pairs={{0,1},{1,0},{2,3},{3,2},{4,5},{5,4},{6,7},{7,6},{8,9},{9,8},{10,11... | collective-permute-start | bytes 393224 | tf_op jit(solution)/shard_map/ppermute | solution.py:18
  17.7 2.1 %collective-permute-start.13 = (f32[128,256]{1,0:T(8,128)S(1)}, f32[128,256]{1,0:T(8,128)S(1)}, u32[]{:S(2)}, u32[]{:S(2)}) collective-permute-start(f32[128,256]{1,0:T(8,128)S(1)} %collective-permute-done.3.refs_6_), channel_id=1, source_target_pairs={{0,1},{1,0},{2,3},{3,2},{4,5},{5,4},{6,7},{7,6},{8,9},{9,8},{10,11... | collective-permute-start | bytes 393224 | tf_op jit(solution)/shard_map/ppermute | solution.py:18
  19.8 0.7 %collective-permute-done.14.refs_8_ = f32[128,256]{1,0:T(8,128)S(1)} collective-permute-done((f32[128,256]{1,0:T(8,128)S(1)}, f32[128,256]{1,0:T(8,128)S(1)}, u32[]{:S(2)}, u32[]{:S(2)}) %collective-permute-start.14) | collective-permute-done | bytes 131104 | tf_op jit(solution)/shard_map/ppermute | solution.py:18
  20.6 1.5 %collective-permute-start.7 = (f32[128,256]{1,0:T(8,128)S(1)}, f32[128,256]{1,0:T(8,128)S(1)}, u32[]{:S(2)}, u32[]{:S(2)}) collective-permute-start(f32[128,256]{1,0:T(8,128)S(1)} %collective-permute-done.6.refs_4_), channel_id=1, source_target_pairs={{0,4},{1,5},{2,6},{3,7},{4,0},{5,1},{6,2},{7,3},{8,12},{9,13},{10,... | collective-permute-start | bytes 393224 | tf_op jit(solution)/shard_map/ppermute | solution.py:18
  22.1 1.8 %collective-permute-start.15 = (f32[128,256]{1,0:T(8,128)S(1)}, f32[128,256]{1,0:T(8,128)S(1)}, u32[]{:S(2)}, u32[]{:S(2)}) collective-permute-start(f32[128,256]{1,0:T(8,128)S(1)} %collective-permute-done.14.refs_8_), channel_id=1, source_target_pairs={{0,1},{1,0},{2,3},{3,2},{4,5},{5,4},{6,7},{7,6},{8,9},{9,8},{10,11... | collective-permute-start | bytes 393224 | tf_op jit(solution)/shard_map/ppermute | solution.py:18
  24.0 0.4 collective-permute-done.4.refs_0_
  24.4 2.4 %collective-permute-start.5 = (f32[128,256]{1,0:T(8,128)S(1)}, f32[128,256]{1,0:T(8,128)S(1)}, u32[]{:S(2)}, u32[]{:S(2)}) collective-permute-start(f32[128,256]{1,0:T(8,128)S(1)} %collective-permute-done.4.refs_0_), channel_id=1, source_target_pairs={{0,1},{1,0},{2,3},{3,2},{4,5},{5,4},{6,7},{7,6},{8,9},{9,8},{10,11... | collective-permute-start | bytes 393224 | tf_op jit(solution)/shard_map/ppermute | solution.py:18
  26.8 0.4 collective-permute-start.8
  27.2 0.8 %shard_map.21 = (bf16[4,2,256,256]{3,2,1,0:T(8,128)(2,1)S(1)}, bf16[4,2,256,256]{3,2,1,0:T(8,128)(2,1)S(1)}, bf16[2,256,256]{2,1,0:T(8,128)(2,1)S(1)}, bf16[2,256,256]{2,1,0:T(8,128)(2,1)S(1)}) custom-call(f32[2,128,256]{2,1,0:T(8,128)S(1)} %get-tuple-element.29.refs_0_, f32[2,128,256]{2,1,0:T(8,128)S(1)} %collective-permute-done.9.refs_1_, ...), custom_call_target="tpu_custom_call" | custom-call | flops 402653184 | bytes 4194304 | tf_op jit(solution)/shard_map/pallas_call | solution.py:89
  28.2 2.4 %shard_map.23 = (f32[2,256,256]{2,1,0:T(8,128)S(1)}, f32[2,256,256]{2,1,0:T(8,128)S(1)}, f32[2,128,256]{2,1,0:T(8,128)S(1)}) custom-call(bf16[4,2,256,256]{3,2,1,0:T(8,128)(2,1)S(1)} %get-tuple-element.35.high_ref, bf16[4,2,256,256]{3,2,1,0:T(8,128)(2,1)S(1)} %get-tuple-element.36.low_ref, f32[2,256,256]{2,1,0:T(8,128)S(1)} %shard_map.19.own_ref, ...), custom_call_target="tpu_custom_call" | custom-call | flops 1610612736 | bytes 4456448 | tf_op jit(solution)/shard_map/pallas_call | solution.py:89
  30.6 1.2 %collective-permute-start.21 = (f32[2,128,256]{2,1,0:T(8,128)S(1)}, f32[2,128,256]{2,1,0:T(8,128)S(1)}, u32[]{:S(2)}, u32[]{:S(2)}) collective-permute-start(f32[2,128,256]{2,1,0:T(8,128)S(1)} %get-tuple-element.38), channel_id=1, source_target_pairs={{0,8},{1,9},{2,10},{3,11},{4,12},{5,13},{6,14},{7,15},{8,0},{9,1},... | collective-permute-start | bytes 786440 | tf_op jit(solution)/shard_map/ppermute | solution.py:18
  31.8 1.2 %collective-permute-start.16 = (f32[2,32,256]{2,1,0:T(8,128)S(1)}, f32[2,32,256]{2,1,0:T(8,128)S(1)}, u32[]{:S(2)}, u32[]{:S(2)}) collective-permute-start(f32[2,32,256]{2,1,0:T(8,128)S(1)} %get-tuple-element.34), channel_id=1, source_target_pairs={{0,8},{1,9},{2,10},{3,11},{4,12},{5,13},{6,14},{7,15},{8,0},{9,1},... | collective-permute-start | bytes 196616 | tf_op jit(solution)/shard_map/ppermute | solution.py:23
  33.0 0.9 %collective-permute-done.16.came_ref = f32[2,32,256]{2,1,0:T(8,128)S(1)} collective-permute-done((f32[2,32,256]{2,1,0:T(8,128)S(1)}, f32[2,32,256]{2,1,0:T(8,128)S(1)}, u32[]{:S(2)}, u32[]{:S(2)}) %collective-permute-start.16) | collective-permute-done | bytes 65568 | tf_op jit(solution)/shard_map/ppermute | solution.py:23
  33.9 7.3 %collective-permute-start.17 = (f32[2,32,256]{2,1,0:T(8,128)S(1)}, f32[2,32,256]{2,1,0:T(8,128)S(1)}, u32[]{:S(2)}, u32[]{:S(2)}) collective-permute-start(f32[2,32,256]{2,1,0:T(8,128)S(1)} %shard_map.24), channel_id=1, source_target_pairs={{0,16},{1,17},{2,18},{3,19},{4,20},{5,21},{6,22},{7,23},{8,24},{9,... | collective-permute-start | bytes 196616 | tf_op jit(solution)/shard_map/ppermute | solution.py:18
  41.2 2.2 %collective-permute-done.17.refs_0_ = f32[2,32,256]{2,1,0:T(8,128)S(1)} collective-permute-done((f32[2,32,256]{2,1,0:T(8,128)S(1)}, f32[2,32,256]{2,1,0:T(8,128)S(1)}, u32[]{:S(2)}, u32[]{:S(2)}) %collective-permute-start.17) | collective-permute-done | bytes 65568 | tf_op jit(solution)/shard_map/ppermute | solution.py:18
  43.4 0.9 %collective-permute-start.20 = (f32[2,32,256]{2,1,0:T(8,128)S(1)}, f32[2,32,256]{2,1,0:T(8,128)S(1)}, u32[]{:S(2)}, u32[]{:S(2)}) collective-permute-start(f32[2,32,256]{2,1,0:T(8,128)S(1)} %collective-permute-done.17.refs_0_), channel_id=1, source_target_pairs={{0,1},{1,0},{2,3},{3,2},{4,5},{5,4},{6,7},{7,6},{8,9},{9,8},{10,11... | collective-permute-start | bytes 196616 | tf_op jit(solution)/shard_map/ppermute | solution.py:28
  44.2 0.4 collective-permute-start.19
  44.6 1.4 %collective-permute-start.18 = (f32[2,32,256]{2,1,0:T(8,128)S(1)}, f32[2,32,256]{2,1,0:T(8,128)S(1)}, u32[]{:S(2)}, u32[]{:S(2)}) collective-permute-start(f32[2,32,256]{2,1,0:T(8,128)S(1)} %collective-permute-done.17.refs_0_), channel_id=1, source_target_pairs={{0,1},{1,0},{2,3},{3,2},{4,5},{5,4},{6,7},{7,6},{8,9},{9,8},{10,11... | collective-permute-start | bytes 196616 | tf_op jit(solution)/shard_map/ppermute | solution.py:28
  46.0 1.3 %collective-permute-start.23 = (f32[256,256]{1,0:T(8,128)S(1)}, f32[256,256]{1,0:T(8,128)S(1)}, u32[]{:S(2)}, u32[]{:S(2)}) collective-permute-start(f32[256,256]{1,0:T(8,128)S(1)} %collective-permute-done.1.next_ref), channel_id=1, source_target_pairs={{24,31}} | collective-permute-start | bytes 786440 | tf_op jit(solution)/shard_map/ppermute | solution.py:41
  47.3 2.9 %collective-permute-start.22 = (f32[2,128,256]{2,1,0:T(8,128)S(1)}, f32[2,128,256]{2,1,0:T(8,128)S(1)}, u32[]{:S(2)}, u32[]{:S(2)}) collective-permute-start(f32[2,128,256]{2,1,0:T(8,128)S(1)} %collective-permute-done.21.mine_ref), channel_id=1, source_target_pairs={{0,1},{1,0},{2,3},{3,2},{4,5},{5,4},{6,7},{7,6},{8,9},{9,8},{10,11... | collective-permute-start | bytes 786440 | tf_op jit(solution)/shard_map/ppermute | solution.py:18
  50.3 1.9 %collective-permute-start.24 = (f32[4,2,32,256]{3,2,1,0:T(8,128)S(1)}, f32[4,2,32,256]{3,2,1,0:T(8,128)S(1)}, u32[]{:S(2)}, u32[]{:S(2)}) collective-permute-start(f32[4,2,32,256]{3,2,1,0:T(8,128)S(1)} %shard_map.25.mine_ref), channel_id=1, source_target_pairs={{0,1},{1,0},{2,3},{3,2},{4,5},{5,4},{6,7},{7,6},{8,9},{9,8},{10,11... | collective-permute-start | bytes 786440 | tf_op jit(solution)/shard_map/ppermute | solution.py:18
  52.2 2.5 %collective-permute-done.23.next_ref = f32[256,256]{1,0:T(8,128)S(1)} collective-permute-done((f32[256,256]{1,0:T(8,128)S(1)}, f32[256,256]{1,0:T(8,128)S(1)}, u32[]{:S(2)}, u32[]{:S(2)}) %collective-permute-start.23) | collective-permute-done | bytes 262176 | tf_op jit(solution)/shard_map/ppermute | solution.py:41
  54.7 1.9 %shard_map.26.late_ref = f32[2,256,256]{2,1,0:T(8,128)S(1)} custom-call(f32[2,256,256]{2,1,0:T(8,128)S(1)} %get-tuple-element.24.parts_ref, bf16[3,256,256]{2,1,0:T(8,128)(2,1)S(1)} %get-tuple-element.25.high_ref, bf16[3,256,256]{2,1,0:T(8,128)(2,1)S(1)} %get-tuple-element.26.low_ref, f32[256,256]{1,0:T(8,128)S(1)} %collective-permute-done.23.next_ref), custom_call_target="tpu_custom_call" | custom-call | flops 134217728 | bytes 2097152 | tf_op jit(solution)/shard_map/pallas_call | solution.py:89
  56.7 1.3 %shard_map.27 = (f32[1,2,256,256]{3,2,1,0:T(8,128)}, bf16[3,256,256]{2,1,0:T(8,128)(2,1)S(1)}, bf16[3,256,256]{2,1,0:T(8,128)(2,1)S(1)}) custom-call(f32[2,128,256]{2,1,0:T(8,128)S(1)} %collective-permute-done.21.mine_ref, f32[2,128,256]{2,1,0:T(8,128)S(1)} %collective-permute-done.22.twin_ref, f32[2,256,256]{2,1,0:T(8,128)S(1)} %get-tuple-element.39.local_ref, ...), custom_call_target="tpu_custom_call" | custom-call | flops 402653184 | bytes 2883584 | tf_op jit(solution)/shard_map/pallas_call | solution.py:89
  58.4 1.3 %shard_map.29 = f32[1,2,256,256]{3,2,1,0:T(8,128)} custom-call(f32[2,256,256]{2,1,0:T(8,128)S(1)} %shard_map.28.part_ref, f32[4,2,32,256]{3,2,1,0:T(8,128)S(1)} %collective-permute-done.24.twin_ref, bf16[3,256,256]{2,1,0:T(8,128)(2,1)S(1)} %get-tuple-element.40.high_ref, ...), custom_call_target="tpu_custom_call", output_to_operand_aliasing={{}: (4, {})} | custom-call | flops 268435456 | bytes 2621440 | tf_op jit(solution)/shard_map/pallas_call | solution.py:89
  (33 shorter events, 2.0 us)
Async XLA Ops:
  0.0 1.0 %copy-start = (f32[1,2,256,256]{3,2,1,0:T(8,128)S(1)}, f32[1,2,256,256]{3,2,1,0:T(8,128)}, u32[]{:S(2)}) copy-start(f32[1,2,256,256]{3,2,1,0:T(8,128)} %drawn_ref.1) | copy-start | bytes 1572868
  1.2 6.2 %collective-permute-start.1 = (f32[256,256]{1,0:T(8,128)S(1)}, f32[256,256]{1,0:T(8,128)S(1)}, u32[]{:S(2)}, u32[]{:S(2)}) collective-permute-start(f32[256,256]{1,0:T(8,128)S(1)} %shard_map.17.packed_ref), channel_id=1, source_target_pairs={{0,24},{1,0},{2,1},{3,2},{4,3},{5,4},{6,5},{7,6},{8,7},{9,8},{10,9... | collective-permute-start | bytes 786440 | tf_op jit(solution)/shard_map/ppermute | solution.py:36
  1.9 5.4 %collective-permute-start = (f32[256,256]{1,0:T(8,128)S(1)}, f32[256,256]{1,0:T(8,128)S(1)}, u32[]{:S(2)}, u32[]{:S(2)}) collective-permute-start(f32[256,256]{1,0:T(8,128)S(1)} %shard_map.17.packed_ref), channel_id=1, source_target_pairs={{0,1},{1,0},{2,3},{3,2},{4,5},{5,4},{6,7},{7,6},{8,9},{9,8},{10,11... | collective-permute-start | bytes 786440 | tf_op jit(solution)/shard_map/ppermute | solution.py:18
  9.3 2.0 %collective-permute-start.2 = (f32[2,256,256]{2,1,0:T(8,128)S(1)}, f32[2,256,256]{2,1,0:T(8,128)S(1)}, u32[]{:S(2)}, u32[]{:S(2)}) collective-permute-start(f32[2,256,256]{2,1,0:T(8,128)S(1)} %shard_map.19.own_ref), channel_id=1, source_target_pairs={{0,1},{1,0},{2,3},{3,2},{4,5},{5,4},{6,7},{7,6},{8,9},{9,8},{10,11... | collective-permute-start | bytes 1572872 | tf_op jit(solution)/shard_map/ppermute | solution.py:18
  11.6 5.0 %collective-permute-start.10 = (f32[128,256]{1,0:T(8,128)S(1)}, f32[128,256]{1,0:T(8,128)S(1)}, u32[]{:S(2)}, u32[]{:S(2)}) collective-permute-start(f32[128,256]{1,0:T(8,128)S(1)} %get-tuple-element.27), channel_id=1, source_target_pairs={{0,2},{1,3},{2,0},{3,1},{4,6},{5,7},{6,4},{7,5},{8,10},{9,11},{10,... | collective-permute-start | bytes 393224 | tf_op jit(solution)/shard_map/ppermute | solution.py:18
  11.7 6.0 %collective-permute-start.3 = (f32[128,256]{1,0:T(8,128)S(1)}, f32[128,256]{1,0:T(8,128)S(1)}, u32[]{:S(2)}, u32[]{:S(2)}) collective-permute-start(f32[128,256]{1,0:T(8,128)S(1)} %get-tuple-element.27), channel_id=1, source_target_pairs={{0,4},{1,5},{2,6},{3,7},{4,0},{5,1},{6,2},{7,3},{8,12},{9,13},{10,... | collective-permute-start | bytes 393224 | tf_op jit(solution)/shard_map/ppermute | solution.py:18
  14.5 6.0 %collective-permute-start.14 = (f32[128,256]{1,0:T(8,128)S(1)}, f32[128,256]{1,0:T(8,128)S(1)}, u32[]{:S(2)}, u32[]{:S(2)}) collective-permute-start(f32[128,256]{1,0:T(8,128)S(1)} %get-tuple-element.28), channel_id=1, source_target_pairs={{0,4},{1,5},{2,6},{3,7},{4,0},{5,1},{6,2},{7,3},{8,12},{9,13},{10,... | collective-permute-start | bytes 393224 | tf_op jit(solution)/shard_map/ppermute | solution.py:18
  14.5 6.1 %collective-permute-start.6 = (f32[128,256]{1,0:T(8,128)S(1)}, f32[128,256]{1,0:T(8,128)S(1)}, u32[]{:S(2)}, u32[]{:S(2)}) collective-permute-start(f32[128,256]{1,0:T(8,128)S(1)} %get-tuple-element.28), channel_id=1, source_target_pairs={{0,2},{1,3},{2,0},{3,1},{4,6},{5,7},{6,4},{7,5},{8,10},{9,11},{10,... | collective-permute-start | bytes 393224 | tf_op jit(solution)/shard_map/ppermute | solution.py:18
  16.6 5.5 %collective-permute-start.11 = (f32[128,256]{1,0:T(8,128)S(1)}, f32[128,256]{1,0:T(8,128)S(1)}, u32[]{:S(2)}, u32[]{:S(2)}) collective-permute-start(f32[128,256]{1,0:T(8,128)S(1)} %collective-permute-done.10.refs_2_), channel_id=1, source_target_pairs={{0,1},{1,0},{2,3},{3,2},{4,5},{5,4},{6,7},{7,6},{8,9},{9,8},{10,11... | collective-permute-start | bytes 393224 | tf_op jit(solution)/shard_map/ppermute | solution.py:18
  17.7 6.2 %collective-permute-start.13 = (f32[128,256]{1,0:T(8,128)S(1)}, f32[128,256]{1,0:T(8,128)S(1)}, u32[]{:S(2)}, u32[]{:S(2)}) collective-permute-start(f32[128,256]{1,0:T(8,128)S(1)} %collective-permute-done.3.refs_6_), channel_id=1, source_target_pairs={{0,1},{1,0},{2,3},{3,2},{4,5},{5,4},{6,7},{7,6},{8,9},{9,8},{10,11... | collective-permute-start | bytes 393224 | tf_op jit(solution)/shard_map/ppermute | solution.py:18
  19.8 7.3 %collective-permute-start.9 = (f32[2,128,256]{2,1,0:T(8,128)S(1)}, f32[2,128,256]{2,1,0:T(8,128)S(1)}, u32[]{:S(2)}, u32[]{:S(2)}) collective-permute-start(f32[2,128,256]{2,1,0:T(8,128)S(1)} %get-tuple-element.29.refs_0_), channel_id=1, source_target_pairs={{0,1},{1,0},{2,3},{3,2},{4,5},{5,4},{6,7},{7,6},{8,9},{9,8},{10,11... | collective-permute-start | bytes 786440 | tf_op jit(solution)/shard_map/ppermute | solution.py:18
  20.6 3.8 %collective-permute-start.4 = (f32[128,256]{1,0:T(8,128)S(1)}, f32[128,256]{1,0:T(8,128)S(1)}, u32[]{:S(2)}, u32[]{:S(2)}) collective-permute-start(f32[128,256]{1,0:T(8,128)S(1)} %collective-permute-done.3.refs_6_), channel_id=1, source_target_pairs={{0,2},{1,3},{2,0},{3,1},{4,6},{5,7},{6,4},{7,5},{8,10},{9,11},{10,... | collective-permute-start | bytes 393224 | tf_op jit(solution)/shard_map/ppermute | solution.py:18
  20.6 6.1 %collective-permute-start.7 = (f32[128,256]{1,0:T(8,128)S(1)}, f32[128,256]{1,0:T(8,128)S(1)}, u32[]{:S(2)}, u32[]{:S(2)}) collective-permute-start(f32[128,256]{1,0:T(8,128)S(1)} %collective-permute-done.6.refs_4_), channel_id=1, source_target_pairs={{0,4},{1,5},{2,6},{3,7},{4,0},{5,1},{6,2},{7,3},{8,12},{9,13},{10,... | collective-permute-start | bytes 393224 | tf_op jit(solution)/shard_map/ppermute | solution.py:18
  22.1 5.0 %collective-permute-start.15 = (f32[128,256]{1,0:T(8,128)S(1)}, f32[128,256]{1,0:T(8,128)S(1)}, u32[]{:S(2)}, u32[]{:S(2)}) collective-permute-start(f32[128,256]{1,0:T(8,128)S(1)} %collective-permute-done.14.refs_8_), channel_id=1, source_target_pairs={{0,1},{1,0},{2,3},{3,2},{4,5},{5,4},{6,7},{7,6},{8,9},{9,8},{10,11... | collective-permute-start | bytes 393224 | tf_op jit(solution)/shard_map/ppermute | solution.py:18
  23.9 3.2 %collective-permute-start.12 = (f32[128,256]{1,0:T(8,128)S(1)}, f32[128,256]{1,0:T(8,128)S(1)}, u32[]{:S(2)}, u32[]{:S(2)}) collective-permute-start(f32[128,256]{1,0:T(8,128)S(1)} %collective-permute-done.6.refs_4_), channel_id=1, source_target_pairs={{0,1},{1,0},{2,3},{3,2},{4,5},{5,4},{6,7},{7,6},{8,9},{9,8},{10,11... | collective-permute-start | bytes 393224 | tf_op jit(solution)/shard_map/ppermute | solution.py:18
  24.4 3.6 %collective-permute-start.5 = (f32[128,256]{1,0:T(8,128)S(1)}, f32[128,256]{1,0:T(8,128)S(1)}, u32[]{:S(2)}, u32[]{:S(2)}) collective-permute-start(f32[128,256]{1,0:T(8,128)S(1)} %collective-permute-done.4.refs_0_), channel_id=1, source_target_pairs={{0,1},{1,0},{2,3},{3,2},{4,5},{5,4},{6,7},{7,6},{8,9},{9,8},{10,11... | collective-permute-start | bytes 393224 | tf_op jit(solution)/shard_map/ppermute | solution.py:18
  26.8 1.4 %collective-permute-start.8 = (f32[128,256]{1,0:T(8,128)S(1)}, f32[128,256]{1,0:T(8,128)S(1)}, u32[]{:S(2)}, u32[]{:S(2)}) collective-permute-start(f32[128,256]{1,0:T(8,128)S(1)} %collective-permute-done.7.refs_2_), channel_id=1, source_target_pairs={{0,1},{1,0},{2,3},{3,2},{4,5},{5,4},{6,7},{7,6},{8,9},{9,8},{10,11... | collective-permute-start | bytes 393224 | tf_op jit(solution)/shard_map/ppermute | solution.py:18
  30.6 16.7 %collective-permute-start.21 = (f32[2,128,256]{2,1,0:T(8,128)S(1)}, f32[2,128,256]{2,1,0:T(8,128)S(1)}, u32[]{:S(2)}, u32[]{:S(2)}) collective-permute-start(f32[2,128,256]{2,1,0:T(8,128)S(1)} %get-tuple-element.38), channel_id=1, source_target_pairs={{0,8},{1,9},{2,10},{3,11},{4,12},{5,13},{6,14},{7,15},{8,0},{9,1},... | collective-permute-start | bytes 786440 | tf_op jit(solution)/shard_map/ppermute | solution.py:18
  31.8 2.1 %collective-permute-start.16 = (f32[2,32,256]{2,1,0:T(8,128)S(1)}, f32[2,32,256]{2,1,0:T(8,128)S(1)}, u32[]{:S(2)}, u32[]{:S(2)}) collective-permute-start(f32[2,32,256]{2,1,0:T(8,128)S(1)} %get-tuple-element.34), channel_id=1, source_target_pairs={{0,8},{1,9},{2,10},{3,11},{4,12},{5,13},{6,14},{7,15},{8,0},{9,1},... | collective-permute-start | bytes 196616 | tf_op jit(solution)/shard_map/ppermute | solution.py:23
  33.9 9.5 %collective-permute-start.17 = (f32[2,32,256]{2,1,0:T(8,128)S(1)}, f32[2,32,256]{2,1,0:T(8,128)S(1)}, u32[]{:S(2)}, u32[]{:S(2)}) collective-permute-start(f32[2,32,256]{2,1,0:T(8,128)S(1)} %shard_map.24), channel_id=1, source_target_pairs={{0,16},{1,17},{2,18},{3,19},{4,20},{5,21},{6,22},{7,23},{8,24},{9,... | collective-permute-start | bytes 196616 | tf_op jit(solution)/shard_map/ppermute | solution.py:18
  43.4 6.9 %collective-permute-start.20 = (f32[2,32,256]{2,1,0:T(8,128)S(1)}, f32[2,32,256]{2,1,0:T(8,128)S(1)}, u32[]{:S(2)}, u32[]{:S(2)}) collective-permute-start(f32[2,32,256]{2,1,0:T(8,128)S(1)} %collective-permute-done.17.refs_0_), channel_id=1, source_target_pairs={{0,1},{1,0},{2,3},{3,2},{4,5},{5,4},{6,7},{7,6},{8,9},{9,8},{10,11... | collective-permute-start | bytes 196616 | tf_op jit(solution)/shard_map/ppermute | solution.py:28
  44.2 6.0 %collective-permute-start.19 = (f32[2,32,256]{2,1,0:T(8,128)S(1)}, f32[2,32,256]{2,1,0:T(8,128)S(1)}, u32[]{:S(2)}, u32[]{:S(2)}) collective-permute-start(f32[2,32,256]{2,1,0:T(8,128)S(1)} %collective-permute-done.17.refs_0_), channel_id=1, source_target_pairs={{0,1},{1,0},{2,3},{3,2},{4,5},{5,4},{6,7},{7,6},{8,9},{9,8},{10,11... | collective-permute-start | bytes 196616 | tf_op jit(solution)/shard_map/ppermute | solution.py:28
  44.6 5.6 %collective-permute-start.18 = (f32[2,32,256]{2,1,0:T(8,128)S(1)}, f32[2,32,256]{2,1,0:T(8,128)S(1)}, u32[]{:S(2)}, u32[]{:S(2)}) collective-permute-start(f32[2,32,256]{2,1,0:T(8,128)S(1)} %collective-permute-done.17.refs_0_), channel_id=1, source_target_pairs={{0,1},{1,0},{2,3},{3,2},{4,5},{5,4},{6,7},{7,6},{8,9},{9,8},{10,11... | collective-permute-start | bytes 196616 | tf_op jit(solution)/shard_map/ppermute | solution.py:28
  46.0 8.7 %collective-permute-start.23 = (f32[256,256]{1,0:T(8,128)S(1)}, f32[256,256]{1,0:T(8,128)S(1)}, u32[]{:S(2)}, u32[]{:S(2)}) collective-permute-start(f32[256,256]{1,0:T(8,128)S(1)} %collective-permute-done.1.next_ref), channel_id=1, source_target_pairs={{24,31}} | collective-permute-start | bytes 786440 | tf_op jit(solution)/shard_map/ppermute | solution.py:41
  47.3 9.3 %collective-permute-start.22 = (f32[2,128,256]{2,1,0:T(8,128)S(1)}, f32[2,128,256]{2,1,0:T(8,128)S(1)}, u32[]{:S(2)}, u32[]{:S(2)}) collective-permute-start(f32[2,128,256]{2,1,0:T(8,128)S(1)} %collective-permute-done.21.mine_ref), channel_id=1, source_target_pairs={{0,1},{1,0},{2,3},{3,2},{4,5},{5,4},{6,7},{7,6},{8,9},{9,8},{10,11... | collective-permute-start | bytes 786440 | tf_op jit(solution)/shard_map/ppermute | solution.py:18
  50.3 8.1 %collective-permute-start.24 = (f32[4,2,32,256]{3,2,1,0:T(8,128)S(1)}, f32[4,2,32,256]{3,2,1,0:T(8,128)S(1)}, u32[]{:S(2)}, u32[]{:S(2)}) collective-permute-start(f32[4,2,32,256]{3,2,1,0:T(8,128)S(1)} %shard_map.25.mine_ref), channel_id=1, source_target_pairs={{0,1},{1,0},{2,3},{3,2},{4,5},{5,4},{6,7},{7,6},{8,9},{9,8},{10,11... | collective-permute-start | bytes 786440 | tf_op jit(solution)/shard_map/ppermute | solution.py:18
